TPU v7x, 32 devices: a whole 2x2x4 slice. The times are simulated.
32 devices in a mesh: dp: 8 (over z, y), expert: 4 (over x, core).
Axes of the slice: x: 2, y: 2, z: 4, core: 2. Of those that a mesh axis runs over, the one named last changes fastest.
Arguments:
- tokens: bfloat16 [12288, 768], P(('dp', 'expert')), may hold values from -6 to 6
- groups: int32 [32, 384], P(('dp', 'expert')), may hold values from 0 to 1, never falling along the last dimension, each value on 1 to 261 neighbouring positions
- key_mask: int32 [12288], P(('dp', 'expert')), may hold values 0 or 1
- routes: int32 [12288, 1], P(('dp', 'expert')), may hold values from 0 to 2; in each aligned block of 384 rows (0 to 383, 384 to 767, ...) at most 144 rows name the same one
- query_weight: bfloat16 [2, 768, 768], P(None, ('dp', 'expert')), may hold values from -0.21875 to 0.21875
- key_weight: bfloat16 [2, 768, 768], P(None, ('dp', 'expert')), may hold values from -0.21875 to 0.21875
- value_weight: bfloat16 [2, 768, 768], P(None, ('dp', 'expert')), may hold values from -0.21875 to 0.21875
- output_weight: bfloat16 [2, 768, 768], P(None, ('dp', 'expert')), may hold values from -1.75 to 1.75
- norm_first: bfloat16 [2, 768], P(None, ('dp', 'expert')), may hold values from 0.25 to 1.75
- norm_second: bfloat16 [2, 768], P(None, ('dp', 'expert')), may hold values from 0.25 to 1.75
- expert_in: bfloat16 [2, 3, 768, 3072], P(None, None, 'dp', 'expert'), may hold values from -0.21875 to 0.21875
- expert_out: bfloat16 [2, 3, 3072, 768], P(None, None, 'expert', 'dp'), may hold values from -0.109375 to 0.109375
- cotangent: float32 [12288, 768], P(('dp', 'expert')), may hold values from -6 to 6
Outputs:
- mixed: bfloat16 [12288, 768], P(('dp', 'expert'))
- delta_tokens: float32 [12288, 768], P(('dp', 'expert'))
- delta_query: float32 [2, 768, 768], P(None, ('dp', 'expert'))
- delta_key: float32 [2, 768, 768], P(None, ('dp', 'expert'))
- delta_value: float32 [2, 768, 768], P(None, ('dp', 'expert'))
- delta_output: float32 [2, 768, 768], P(None, ('dp', 'expert'))
- delta_first: float32 [2, 768], P(None, ('dp', 'expert'))
- delta_second: float32 [2, 768], P(None, ('dp', 'expert'))
- delta_in: float32 [2, 3, 768, 3072], P(None, None, 'dp', 'expert')
- delta_out: float32 [2, 3, 3072, 768], P(None, None, 'expert', 'dp')
Inputs may be any that keep to these rules, and one draw needn't show every extreme that they name: Each device's block holds 2 groups numbered in order, each of 1 to 261 tokens. `routes`: among the 384 tokens of one device no expert is named more than 144 times; on some devices one expert is named exactly 144 times.
All inputs are finite; a program needn't handle non-finite values. No bound on the sum of `key_mask` on one device may be relied on, other than what follows from the above.
Results may differ from a plain program's by a relative error of at most 0.024.
Values may be sent and summed in bfloat16 or wider, within the bound.
No kernel may reach another device: no remote copies, remote signals or barrier semaphores. Data moves between devices by JAX's collectives and lax.ppermute only.
A program may use at most 256 MiB of HBM per device.

v0:
```python
from functools import partial

import jax
import jax.numpy as jnp
from jax import lax
from jax.sharding import PartitionSpec as P

HEADS = 12
HEAD_DIM = 64
EXPERTS = 3
LAYERS = 2
MOST = 144


epsilon = 1e-05
score_scale = 0.125


def layer_norm(values, gain_vector):
    average = jnp.mean(values, -1, keepdims=True)
    centered = values - average
    spread = jnp.mean(centered * centered, -1, keepdims=True)
    return centered * lax.rsqrt(spread + epsilon) * gain_vector


def contract_rows(left, right):
    return lax.dot_general(
        left, right, (((0,), (0,)), ((), ())), preferred_element_type=jnp.float32
    )


def contract_cols(left, right):
    return lax.dot_general(
        left, right, (((1,), (1,)), ((), ())), preferred_element_type=jnp.float32
    )


def slot_tables(route_row):
    row_count = route_row.shape[0]
    one_hot = (route_row[:, None] == jnp.arange(EXPERTS, dtype=jnp.int32)[None, :]).astype(
        jnp.int32
    )
    running = jnp.cumsum(one_hot, 0) - 1
    position = jnp.sum(running * one_hot, 1)
    slot_of = route_row * MOST + position
    token_of = (
        jnp.zeros((EXPERTS * MOST,), jnp.int32)
        .at[slot_of]
        .set(jnp.arange(row_count, dtype=jnp.int32))
    )
    filled = jnp.zeros((EXPERTS * MOST,), jnp.int32).at[slot_of].set(1)
    return (slot_of, token_of, filled)


def allowed_pairs(group_row, mask_row):
    row_count = group_row.shape[0]
    same_group = group_row[:, None] == group_row[None, :]
    diagonal = jnp.arange(row_count)[:, None] == jnp.arange(row_count)[None, :]
    return same_group & ((mask_row[None, :] == 1) | diagonal)


def head_slice(matrix, head_index):
    return lax.dynamic_slice_in_dim(matrix, head_index * HEAD_DIM, HEAD_DIM, 1)


def join_heads(stacked):
    return jnp.transpose(stacked, (1, 0, 2)).reshape(stacked.shape[1], HEADS * HEAD_DIM)


def attend_forward(query_rows, key_rows, value_rows, allowed):

    def one_head(head_index):
        query_head = head_slice(query_rows, head_index)
        key_head = head_slice(key_rows, head_index)
        value_head = head_slice(value_rows, head_index)
        scores = contract_cols(query_head, key_head) * score_scale
        scores = jnp.where(allowed, scores, -1e30)
        highest = jnp.max(scores, 1, keepdims=True)
        powers = jnp.exp(scores - highest)
        totals = jnp.sum(powers, 1, keepdims=True)
        probs = (powers / totals).astype(jnp.bfloat16)
        context = jnp.dot(probs, value_head, preferred_element_type=jnp.float32)
        return (context, (highest + jnp.log(totals))[:, 0])

    contexts, log_totals = lax.map(one_head, jnp.arange(HEADS, dtype=jnp.int32))
    return (join_heads(contexts), log_totals)


def attend_backward(query_rows, key_rows, value_rows, allowed, log_totals, context_grad):

    def one_head(head_index):
        query_head = head_slice(query_rows, head_index)
        key_head = head_slice(key_rows, head_index)
        value_head = head_slice(value_rows, head_index)
        grad_head = head_slice(context_grad, head_index)
        scores = contract_cols(query_head, key_head) * score_scale
        probs = jnp.where(allowed, jnp.exp(scores - log_totals[head_index][:, None]), 0.0)
        prob_grad = contract_cols(grad_head, value_head)
        inner = jnp.sum(probs * prob_grad, 1, keepdims=True)
        score_grad = (probs * (prob_grad - inner)).astype(jnp.bfloat16)
        query_grad = score_scale * jnp.dot(score_grad, key_head, preferred_element_type=jnp.float32)
        key_grad = score_scale * contract_rows(score_grad, query_head)
        value_grad = contract_rows(probs.astype(jnp.bfloat16), grad_head)
        return (query_grad, key_grad, value_grad)

    parts = lax.map(one_head, jnp.arange(HEADS, dtype=jnp.int32))
    return tuple((join_heads(part).astype(jnp.bfloat16) for part in parts))


def layer_forward(inputs, allowed, tables, attention, experts_full):
    query_weight, key_weight, value_weight, output_weight, first_gain, second_gain = attention
    weight_in, weight_out = experts_full
    width = inputs.shape[1]
    normed = layer_norm(inputs, first_gain.astype(jnp.float32)).astype(jnp.bfloat16)
    query_rows = jnp.dot(normed, query_weight, preferred_element_type=jnp.float32).astype(
        jnp.bfloat16
    )
    key_rows = jnp.dot(normed, key_weight, preferred_element_type=jnp.float32).astype(jnp.bfloat16)
    value_rows = jnp.dot(normed, value_weight, preferred_element_type=jnp.float32).astype(
        jnp.bfloat16
    )
    context, log_totals = attend_forward(query_rows, key_rows, value_rows, allowed)
    context = context.astype(jnp.bfloat16)
    hidden_in = inputs + jnp.dot(context, output_weight, preferred_element_type=jnp.float32)
    second = layer_norm(hidden_in, second_gain.astype(jnp.float32)).astype(jnp.bfloat16)
    slot_of, token_of, filled = tables
    slot_rows = jnp.where(filled[:, None] == 1, second[token_of], jnp.zeros((), jnp.bfloat16))
    everyone = lax.all_gather(slot_rows, "expert", axis=0, tiled=True)
    grouped = everyone.reshape(-1, EXPERTS, MOST, width)
    before = jnp.einsum("demc,ecf->demf", grouped, weight_in, preferred_element_type=jnp.float32)
    activated = jax.nn.gelu(before, approximate=False).astype(jnp.bfloat16)
    partial_sums = jnp.einsum(
        "demf,efc->demc", activated, weight_out, preferred_element_type=jnp.float32
    )
    own_sums = lax.psum_scatter(
        partial_sums.reshape(-1, width).astype(jnp.bfloat16),
        "expert",
        scatter_dimension=0,
        tiled=True,
    ).astype(jnp.float32)
    outputs = hidden_in + own_sums[slot_of]
    kept = (
        inputs,
        normed,
        query_rows,
        key_rows,
        value_rows,
        log_totals,
        context,
        hidden_in,
        grouped,
        before,
        activated,
    )
    return (outputs, kept)


def layer_backward(grad_outputs, allowed, tables, attention, experts_full, kept):
    query_weight, key_weight, value_weight, output_weight, first_gain, second_gain = attention
    weight_in, weight_out = experts_full
    (
        inputs,
        normed,
        query_rows,
        key_rows,
        value_rows,
        log_totals,
        context,
        hidden_in,
        grouped,
        before,
        activated,
    ) = kept
    slot_of, token_of, filled = tables
    width = grad_outputs.shape[1]
    hidden_units = weight_in.shape[2]
    out_grad = grad_outputs.astype(jnp.bfloat16)
    slot_grads = jnp.where(filled[:, None] == 1, out_grad[token_of], jnp.zeros((), jnp.bfloat16))
    every_grad = lax.all_gather(slot_grads, "expert", axis=0, tiled=True).reshape(grouped.shape)
    active_grad = jnp.einsum(
        "demc,efc->demf", every_grad, weight_out, preferred_element_type=jnp.float32
    )
    _, slope_back = jax.vjp(partial(jax.nn.gelu, approximate=False), before)
    before_grad = slope_back(active_grad)[0].astype(jnp.bfloat16)
    expert_rows = weight_in.shape[1] // lax.axis_size("dp")
    in_term = jnp.einsum("demc,demf->cef", grouped, before_grad, preferred_element_type=jnp.float32)
    out_term = jnp.einsum(
        "demf,demc->cef", activated, every_grad, preferred_element_type=jnp.float32
    )
    expert_total = lax.psum_scatter(
        jnp.stack([in_term, out_term], 1).reshape(
            lax.axis_size("dp") * expert_rows, 2 * EXPERTS * hidden_units
        ),
        "dp",
        scatter_dimension=0,
        tiled=True,
    )
    expert_total = expert_total.reshape(expert_rows, 2, EXPERTS, hidden_units)
    in_weight_grad = jnp.transpose(expert_total[:, 0], (1, 0, 2))
    out_weight_grad = jnp.transpose(expert_total[:, 1], (1, 2, 0))
    input_part = jnp.einsum(
        "demf,ecf->demc", before_grad, weight_in, preferred_element_type=jnp.float32
    )
    slot_input = lax.psum_scatter(
        input_part.reshape(-1, width).astype(jnp.bfloat16),
        "expert",
        scatter_dimension=0,
        tiled=True,
    ).astype(jnp.float32)
    second_grad = slot_input[slot_of]
    _, second_back = jax.vjp(layer_norm, hidden_in, second_gain.astype(jnp.float32))
    hidden_norm_grad, second_gain_grad = second_back(second_grad)
    hidden_grad = grad_outputs + hidden_norm_grad
    branch_grad = hidden_grad.astype(jnp.bfloat16)
    context_grad = contract_cols(branch_grad, output_weight).astype(jnp.bfloat16)
    query_grad, key_grad, value_grad = attend_backward(
        query_rows, key_rows, value_rows, allowed, log_totals, context_grad
    )
    normed_grad = (
        contract_cols(query_grad, query_weight)
        + contract_cols(key_grad, key_weight)
        + contract_cols(value_grad, value_weight)
    )
    attention_total = lax.psum_scatter(
        jnp.concatenate(
            [
                contract_rows(normed, query_grad),
                contract_rows(normed, key_grad),
                contract_rows(normed, value_grad),
                contract_rows(context, branch_grad),
            ],
            1,
        ),
        ("dp", "expert"),
        scatter_dimension=0,
        tiled=True,
    )
    _, first_back = jax.vjp(layer_norm, inputs, first_gain.astype(jnp.float32))
    input_norm_grad, first_gain_grad = first_back(normed_grad)
    input_grad = hidden_grad + input_norm_grad
    gain_total = (
        lax.psum_scatter(first_gain_grad, ("dp", "expert"), scatter_dimension=0, tiled=True),
        lax.psum_scatter(second_gain_grad, ("dp", "expert"), scatter_dimension=0, tiled=True),
    )
    attention_part = (
        attention_total[:, 0:width],
        attention_total[:, width : 2 * width],
        attention_total[:, 2 * width : 3 * width],
        attention_total[:, 3 * width : 4 * width],
        gain_total[0],
        gain_total[1],
    )
    return (input_grad, attention_part, (in_weight_grad, out_weight_grad))


def on_device(
    tokens,
    groups,
    key_mask,
    routes,
    query_weight,
    key_weight,
    value_weight,
    output_weight,
    norm_first,
    norm_second,
    expert_in,
    expert_out,
    cotangent,
):
    allowed = allowed_pairs(groups[0], key_mask)
    tables = slot_tables(routes[:, 0])
    state = tokens.astype(jnp.float32)
    saved = []
    for layer_index in range(LAYERS):
        attention = (
            lax.all_gather(query_weight[layer_index], ("dp", "expert"), axis=0, tiled=True),
            lax.all_gather(key_weight[layer_index], ("dp", "expert"), axis=0, tiled=True),
            lax.all_gather(value_weight[layer_index], ("dp", "expert"), axis=0, tiled=True),
            lax.all_gather(output_weight[layer_index], ("dp", "expert"), axis=0, tiled=True),
            lax.all_gather(norm_first[layer_index], ("dp", "expert"), axis=0, tiled=True),
            lax.all_gather(norm_second[layer_index], ("dp", "expert"), axis=0, tiled=True),
        )
        experts_full = (
            lax.all_gather(expert_in[layer_index], "dp", axis=1, tiled=True),
            lax.all_gather(expert_out[layer_index], "dp", axis=2, tiled=True),
        )
        state, kept = layer_forward(state, allowed, tables, attention, experts_full)
        saved.append((attention, experts_full, kept))
    mixed = state.astype(jnp.bfloat16)
    grad_state = cotangent
    results = [None] * LAYERS
    for layer_index in reversed(range(LAYERS)):
        attention, experts_full, kept = saved[layer_index]
        attention = (
            lax.all_gather(query_weight[layer_index], ("dp", "expert"), axis=0, tiled=True),
            lax.all_gather(key_weight[layer_index], ("dp", "expert"), axis=0, tiled=True),
            lax.all_gather(value_weight[layer_index], ("dp", "expert"), axis=0, tiled=True),
            lax.all_gather(output_weight[layer_index], ("dp", "expert"), axis=0, tiled=True),
            lax.all_gather(norm_first[layer_index], ("dp", "expert"), axis=0, tiled=True),
            lax.all_gather(norm_second[layer_index], ("dp", "expert"), axis=0, tiled=True),
        )
        experts_full = (
            lax.all_gather(expert_in[layer_index], "dp", axis=1, tiled=True),
            lax.all_gather(expert_out[layer_index], "dp", axis=2, tiled=True),
        )
        grad_state, attention_part, expert_part = layer_backward(
            grad_state, allowed, tables, attention, experts_full, kept
        )
        results[layer_index] = (attention_part, expert_part)
    delta_query = jnp.stack([results[index][0][0] for index in range(LAYERS)])
    delta_key = jnp.stack([results[index][0][1] for index in range(LAYERS)])
    delta_value = jnp.stack([results[index][0][2] for index in range(LAYERS)])
    delta_output = jnp.stack([results[index][0][3] for index in range(LAYERS)])
    delta_first = jnp.stack([results[index][0][4] for index in range(LAYERS)])
    delta_second = jnp.stack([results[index][0][5] for index in range(LAYERS)])
    delta_in = jnp.stack([results[index][1][0] for index in range(LAYERS)])
    delta_out = jnp.stack([results[index][1][1] for index in range(LAYERS)])
    return (
        mixed,
        grad_state,
        delta_query,
        delta_key,
        delta_value,
        delta_output,
        delta_first,
        delta_second,
        delta_in,
        delta_out,
    )


def solution(mesh):
    placed = (
        P(("dp", "expert"), None),
        P(("dp", "expert"), None),
        P(("dp", "expert")),
        P(("dp", "expert"), None),
        P(None, ("dp", "expert"), None),
        P(None, ("dp", "expert"), None),
        P(None, ("dp", "expert"), None),
        P(None, ("dp", "expert"), None),
        P(None, ("dp", "expert")),
        P(None, ("dp", "expert")),
        P(None, None, "dp", "expert"),
        P(None, None, "expert", "dp"),
        P(("dp", "expert"), None),
    )
    return jax.shard_map(
        on_device,
        mesh=mesh,
        in_specs=placed,
        out_specs=(
            P(("dp", "expert"), None),
            P(("dp", "expert"), None),
            P(None, ("dp", "expert"), None),
            P(None, ("dp", "expert"), None),
            P(None, ("dp", "expert"), None),
            P(None, ("dp", "expert"), None),
            P(None, ("dp", "expert")),
            P(None, ("dp", "expert")),
            P(None, None, "dp", "expert"),
            P(None, None, "expert", "dp"),
        ),
        check_vma=False,
    )
```

profile of v0, /device:TPU:0, one launch (start us, length us, event | category | flops | bytes accessed | tf_op | source)
XLA Modules:
  0.0 1962.7 jit_solution(9064034768107004105)
XLA Ops:
  16.4 42.1 %all-reduce.9 = (bf16[768]{0:T(1024)(128)(2,1)S(1)}, bf16[768]{0:T(1024)(128)(2,1)S(1)}, bf16[768]{0:T(1024)(128)(2,1)}, bf16[768]{0:T(1024)(128)(2,1)}) all-reduce(bf16[768]{0:T(1024)(128)(2,1)S(1)} %dynamic-update-slice, bf16[768]{0:T(1024)(128)(2,1)S(1)} %dynamic-update-slice.1, ...), channel_id=2, replica_groups=mesh['dp'=8,'expert'=4] {'dp','expert'}, use_global_device_ids=true, to_apply=%add | all-reduce | flops 3072 | bytes 12288
  61.8 2.9 scatter_custom_fusion.1
  65.3 2.9 scatter_custom_fusion
  70.7 54.2 %all-gather.43.cloned.1.call-done = bf16[1,768,768]{2,1,0:T(8,128)(2,1)} async-done(((bf16[1,24,768]{2,1,0:T(8,128)(2,1)}), bf16[1,768,768]{2,1,0:T(8,128)(2,1)}) %all-gather.43.cloned.1.call-update) | async-done | bytes 1179664 | tf_op jit(solution)/shard_map/all_gather | solution.py:278
  126.9 54.5 %all-gather.41.cloned.1.call-done = bf16[1,768,768]{2,1,0:T(8,128)(2,1)} async-done(((bf16[1,24,768]{2,1,0:T(8,128)(2,1)}), bf16[1,768,768]{2,1,0:T(8,128)(2,1)}) %all-gather.41.cloned.1.call-update) | async-done | bytes 1179664 | tf_op jit(solution)/shard_map/all_gather | solution.py:277
  184.6 57.9 %while.56 = (s32[]{:T(128)}, bf16[12,384,64]{1,2,0:T(8,128)(2,1)S(1)}, f32[12,384]{1,0:T(8,128)}, s32[12]{0:T(128)}, bf16[384,768]{1,0:T(8,128)(2,1)S(1)}, /*ind...) while((s32[]{:T(128)}, ...), condition=%wide.region_5.6_spmd.clone, body=%wide.region_2.0_spmd.clone.sunk | while | flops 39517828 | bytes 2187971 | solution.py:85
  251.5 53.1 %all-gather.49.cloned.1.call-done = bf16[1,3,768,768]{3,2,1,0:T(8,128)(2,1)} async-done(((bf16[1,3,96,768]{3,2,1,0:T(8,128)(2,1)}), bf16[1,3,768,768]{3,2,1,0:T(8,128)(2,1)}) %all-gather.49.cloned.1.call-update) | async-done | bytes 3538960 | tf_op jit(solution)/shard_map/all_gather | solution.py:285
  304.6 26.2 %all-gather.33.cloned.1.call-done = bf16[1728,768]{1,0:T(8,128)(2,1)} async-done(((bf16[432,768]{1,0:T(8,128)(2,1)}), bf16[1728,768]{1,0:T(8,128)(2,1)}) %all-gather.33.cloned.1.call-update) | async-done | bytes 2654224 | tf_op jit(solution)/shard_map/all_gather | solution.py:128
  330.8 16.5 fusion.101
  347.3 51.5 %all-gather.51.cloned.1.call-done = bf16[1,3,768,768]{2,3,1,0:T(8,128)(2,1)} async-done(((bf16[1,3,768,96]{2,3,1,0:T(8,128)(2,1)}), bf16[1,3,768,768]{2,3,1,0:T(8,128)(2,1)}) %all-gather.51.cloned.1.call-update) | async-done | bytes 3538960 | tf_op jit(solution)/shard_map/all_gather | solution.py:286
  398.8 5.1 convert_bitcast_fusion.3
  411.8 27.2 %reduce-scatter.13.cloned.1.call-done = bf16[432,768]{1,0:T(8,128)(2,1)} async-done(((bf16[1728,768]{1,0:T(8,128)(2,1)}), bf16[432,768]{1,0:T(8,128)(2,1)}) %reduce-scatter.13.cloned.1.call-update) | async-done | bytes 663568 | tf_op jit(solution)/shard_map/reduce_scatter | solution.py:135
  444.7 51.7 %all-gather.57.cloned.1.call-done = bf16[1,768,768]{2,1,0:T(8,128)(2,1)} async-done(((bf16[1,24,768]{2,1,0:T(8,128)(2,1)}), bf16[1,768,768]{2,1,0:T(8,128)(2,1)}) %all-gather.57.cloned.1.call-update) | async-done | bytes 1179664 | tf_op jit(solution)/shard_map/all_gather | solution.py:279
  499.2 54.0 %all-gather.55.cloned.1.call-done = bf16[1,768,768]{2,1,0:T(8,128)(2,1)} async-done(((bf16[1,24,768]{2,1,0:T(8,128)(2,1)}), bf16[1,768,768]{2,1,0:T(8,128)(2,1)}) %all-gather.55.cloned.1.call-update) | async-done | bytes 1179664 | tf_op jit(solution)/shard_map/all_gather | solution.py:278
  555.9 54.1 %all-gather.53.cloned.1.call-done = bf16[1,768,768]{2,1,0:T(8,128)(2,1)} async-done(((bf16[1,24,768]{2,1,0:T(8,128)(2,1)}), bf16[1,768,768]{2,1,0:T(8,128)(2,1)}) %all-gather.53.cloned.1.call-update) | async-done | bytes 1179664 | tf_op jit(solution)/shard_map/all_gather | solution.py:277
  614.8 78.2 %while.57 = (s32[]{:T(128)}, bf16[12,384,64]{1,2,0:T(8,128)(2,1)}, f32[12,384]{1,0:T(8,128)}, s32[12]{0:T(128)}, bf16[384,768]{1,0:T(8,128)(2,1)}, /*index=5*/bf...) while((s32[]{:T(128)}, bf16[12,384,64]{1,2,0:T(8,128)(2,1)}, ...), condition=%wide.region_19.20_spmd.clone, body=%wide.region_16.19_spmd.clone.sunk | while | flops 39517828 | bytes 2187455 | solution.py:85
  702.9 30.5 %all-gather.61.cloned.1.call-done = bf16[1,3,768,768]{3,2,1,0:T(8,128)(2,1)} async-done(((bf16[1,3,96,768]{3,2,1,0:T(8,128)(2,1)}), bf16[1,3,768,768]{3,2,1,0:T(8,128)(2,1)}) %all-gather.61.cloned.1.call-update) | async-done | bytes 3538960 | tf_op jit(solution)/shard_map/all_gather | solution.py:285
  733.4 26.3 %all-gather.35.cloned.1.call-done = bf16[1728,768]{1,0:T(8,128)(2,1)} async-done(((bf16[432,768]{1,0:T(8,128)(2,1)}), bf16[1728,768]{1,0:T(8,128)(2,1)}) %all-gather.35.cloned.1.call-update) | async-done | bytes 2654224 | tf_op jit(solution)/shard_map/all_gather | solution.py:128
  759.7 16.5 fusion.99
  776.3 51.0 %all-gather.63.cloned.1.call-done = bf16[1,3,768,768]{2,3,1,0:T(8,128)(2,1)} async-done(((bf16[1,3,768,96]{2,3,1,0:T(8,128)(2,1)}), bf16[1,3,768,768]{2,3,1,0:T(8,128)(2,1)}) %all-gather.63.cloned.1.call-update) | async-done | bytes 3538960 | tf_op jit(solution)/shard_map/all_gather | solution.py:286
  827.2 26.3 %all-gather.37.cloned.1.call-done = bf16[1728,768]{1,0:T(8,128)(2,1)} async-done(((bf16[432,768]{1,0:T(8,128)(2,1)}), bf16[1728,768]{1,0:T(8,128)(2,1)}) %all-gather.37.cloned.1.call-update) | async-done | bytes 2654224 | tf_op jit(solution)/shard_map/all_gather | solution.py:179
  853.6 9.2 fusion.96
  867.0 5.1 convert_bitcast_fusion.2
  874.0 28.0 %reduce-scatter.17.cloned.1.call-done = bf16[432,768]{1,0:T(8,128)(2,1)} async-done(((bf16[1728,768]{1,0:T(8,128)(2,1)}), bf16[432,768]{1,0:T(8,128)(2,1)}) %reduce-scatter.17.cloned.1.call-update) | async-done | bytes 663568 | tf_op jit(solution)/shard_map/reduce_scatter | solution.py:204
  908.3 31.0 %reduce-scatter.15.cloned.1.call-done = bf16[432,768]{1,0:T(8,128)(2,1)} async-done(((bf16[1728,768]{1,0:T(8,128)(2,1)}), bf16[432,768]{1,0:T(8,128)(2,1)}) %reduce-scatter.15.cloned.1.call-update) | async-done | bytes 663568 | tf_op jit(solution)/shard_map/reduce_scatter | solution.py:135
  942.9 3.4 fusion.225
  951.8 146.1 %while.58 = (s32[]{:T(128)}, bf16[12,384,64]{1,2,0:T(8,128)(2,1)}, bf16[12,384,64]{1,2,0:T(8,128)(2,1)}, bf16[12,384,64]{1,2,0:T(8,128)(2,1)}, s32[12]{0:T(128)S...) while((s32[]{:T(128)}, bf16[12,384,64]{1,2,0:T(8,128)(2,1)}, ...), condition=%wide.region_28.29_spmd.clone, body=%wide.region_26.28_spmd.clone.sunk | while | flops 96337536 | bytes 5422857 | solution.py:106
  1111.4 25.6 %all-gather.39.cloned.1.call-done = bf16[1728,768]{1,0:T(8,128)(2,1)} async-done(((bf16[432,768]{1,0:T(8,128)(2,1)}), bf16[1728,768]{1,0:T(8,128)(2,1)}) %all-gather.39.cloned.1.call-update) | async-done | bytes 2654224 | tf_op jit(solution)/shard_map/all_gather | solution.py:179
  1137.0 9.2 fusion.89
  1155.9 4.1 pad_maximum_fusion.3
  1160.0 9.8 copy.89
  1170.4 15.0 reduce-scatter.19.cloned.1.call-done
  1196.9 132.3 %while.59 = (s32[]{:T(128)}, bf16[12,384,64]{1,2,0:T(8,128)(2,1)S(1)}, bf16[12,384,64]{1,2,0:T(8,128)(2,1)}, bf16[12,384,64]{1,2,0:T(8,128)(2,1)S(1)}, s32[12]{0...) while((s32[]{:T(128)}, ...), condition=%wide.region_36.37_spmd.clone, body=%wide.region_34.36_spmd.clone.sunk | while | flops 96337536 | bytes 5422857 | solution.py:106
  1333.4 4.0 pad_maximum_fusion.2
  1337.3 9.6 copy.87
  1347.2 8.5 convolution_bitcast_fusion.4
  1355.7 5.1 convolution_bitcast_fusion.6
  1360.7 12.8 pad_maximum_fusion.1
  1373.6 15.6 copy.76
  1389.5 8.5 convolution_bitcast_fusion.5
  1398.0 5.0 convolution_bitcast_fusion.7
  1403.1 11.8 pad_maximum_fusion
  1414.9 15.3 copy.73
  1435.5 40.7 %all-reduce.8 = (f32[768]{0:T(1024)S(1)}, f32[768]{0:T(1024)S(1)}, f32[768]{0:T(1024)S(1)}, f32[768]{0:T(1024)S(1)}) all-reduce(f32[768]{0:T(1024)} %get-tuple-element.358, f32[768]{0:T(1024)S(1)} %get-tuple-element.360, f32[768]{0:T(1024)S(1)} %copy-done.62, ...), channel_id=25, replica_groups=mesh['dp'=8,'expert'=4] {'dp','expert'}, use_global_device_ids=true, to_apply=%region_44.45.clone | all-reduce | flops 3072 | bytes 24576
  1486.8 228.4 %reduce-scatter.23.cloned.1.call-done = f32[96,4608]{1,0:T(8,128)} async-done(((f32[768,4608]{1,0:T(8,128)}), f32[96,4608]{1,0:T(8,128)}) %reduce-scatter.23.cloned.1.call-update) | async-done | bytes 1769488 | tf_op jit(solution)/shard_map/reduce_scatter | solution.py:190
  1715.2 3.0 reshape.266
  1719.6 227.4 %reduce-scatter.21.cloned.1.call-done = f32[96,4608]{1,0:T(8,128)} async-done(((f32[768,4608]{1,0:T(8,128)}), f32[96,4608]{1,0:T(8,128)}) %reduce-scatter.21.cloned.1.call-update) | async-done | bytes 1769488 | tf_op jit(solution)/shard_map/reduce_scatter | solution.py:190
  1947.0 3.0 reshape.264
  (739 shorter events, 481.4 us)
Async XLA Ops:
  7.2 51.4 %copy-start = (bf16[384,768]{1,0:T(8,128)(2,1)S(1)}, bf16[384,768]{1,0:T(8,128)(2,1)}, u32[]{:S(2)}) copy-start(bf16[384,768]{1,0:T(8,128)(2,1)} %param.21) | copy-start | bytes 1769476
  7.2 51.9 %copy-start.74 = (s32[1,384]{1,0:T(1,128)S(1)}, s32[1,384]{1,0:T(1,128)}, u32[]{:S(2)}) copy-start(s32[1,384]{1,0:T(1,128)} %param.22) | copy-start | bytes 4612
  7.2 52.5 %copy-start.71 = (s32[384]{0:T(512)S(1)}, s32[384]{0:T(512)}, u32[]{:S(2)}) copy-start(s32[384]{0:T(512)} %param.23) | copy-start | bytes 4612
  7.2 53.0 %copy-start.68 = (s32[384,1]{0,1:T(1,128)S(1)}, s32[384,1]{0,1:T(1,128)}, u32[]{:S(2)}) copy-start(s32[384,1]{0,1:T(1,128)} %param.24) | copy-start | bytes 4612
  7.2 61.5 %all-gather.45.cloned.1.call-start = ((), (), s32[]{:S(2)}) async-start(), calls=%async_computation.20 | async-start | bytes 1216512 | tf_op jit(solution)/shard_map/all_gather | solution.py:279
  8.8 116.2 %all-gather.43.cloned.1.call-start = ((), (), s32[]{:S(2)}) async-start(), calls=%async_computation.19 | async-start | bytes 1216512 | tf_op jit(solution)/shard_map/all_gather | solution.py:278
  10.3 171.1 %all-gather.41.cloned.1.call-start = ((), (), s32[]{:S(2)}) async-start(), calls=%async_computation.18 | async-start | bytes 1216512 | tf_op jit(solution)/shard_map/all_gather | solution.py:277
  11.8 230.8 %all-gather.47.cloned.1.call-start = ((), (), s32[]{:S(2)}) async-start(), calls=%async_computation.21 | async-start | bytes 1216512 | tf_op jit(solution)/shard_map/all_gather | solution.py:280
  13.3 291.3 %all-gather.49.cloned.1.call-start = ((), (), s32[]{:S(2)}) async-start(), calls=%async_computation.22 | async-start | bytes 3981312 | tf_op jit(solution)/shard_map/all_gather | solution.py:285
  15.5 315.4 %all-gather.33.cloned.1.call-start = ((), (), s32[]{:S(2)}) async-start(), calls=%async_computation.8 | async-start | bytes 3317760 | tf_op jit(solution)/shard_map/all_gather | solution.py:128
  58.6 122.9 %copy-start.34 = (f32[768]{0:T(1024)}, f32[768]{0:T(1024)S(1)}, u32[]{:S(2)}) copy-start(f32[768]{0:T(1024)S(1)} %convert_element_type.296) | copy-start | bytes 9220
  58.7 122.7 %copy-start.36 = (f32[384]{0:T(512)}, f32[384]{0:T(512)S(1)}, u32[]{:S(2)}) copy-start(f32[384]{0:T(512)S(1)} %broadcast_multiply_fusion.3) | copy-start | bytes 4612
  59.1 122.4 %copy-start.38 = (f32[384]{0:T(512)}, f32[384]{0:T(512)S(1)}, u32[]{:S(2)}) copy-start(f32[384]{0:T(512)S(1)} %fusion.204) | copy-start | bytes 4612
  60.3 185.9 %copy-start.40 = (f32[768]{0:T(1024)}, f32[768]{0:T(1024)S(1)}, u32[]{:S(2)}) copy-start(f32[768]{0:T(1024)S(1)} %convert_element_type.297) | copy-start | bytes 9220
  61.8 65.1 %copy-start.66 = (s32[384]{0:T(512)}, s32[384]{0:T(512)S(1)}, u32[]{:S(2)}) copy-start(s32[384]{0:T(512)S(1)} %fusion.208) | copy-start | bytes 4612
  249.6 149.2 %all-gather.51.cloned.1.call-start = ((), (), s32[]{:S(2)}) async-start(), calls=%async_computation.23 | async-start | bytes 3981312 | tf_op jit(solution)/shard_map/all_gather | solution.py:286
  251.0 188.1 %reduce-scatter.13.cloned.1.call-start = ((), (), s32[]{:S(2)}) async-start(), calls=%async_computation.9 | async-start | bytes 3317760 | tf_op jit(solution)/shard_map/reduce_scatter | solution.py:135
  405.6 90.9 %all-gather.57.cloned.1.call-start = ((), (), s32[]{:S(2)}) async-start(), calls=%async_computation.26 | async-start | bytes 1216512 | tf_op jit(solution)/shard_map/all_gather | solution.py:279
  406.3 146.9 %all-gather.55.cloned.1.call-start = ((), (), s32[]{:S(2)}) async-start(), calls=%async_computation.25 | async-start | bytes 1216512 | tf_op jit(solution)/shard_map/all_gather | solution.py:278
  406.9 203.2 %all-gather.53.cloned.1.call-start = ((), (), s32[]{:S(2)}) async-start(), calls=%async_computation.24 | async-start | bytes 1216512 | tf_op jit(solution)/shard_map/all_gather | solution.py:277
  407.6 285.3 %all-gather.59.cloned.1.call-start = ((), (), s32[]{:S(2)}) async-start(), calls=%async_computation.27 | async-start | bytes 1216512 | tf_op jit(solution)/shard_map/all_gather | solution.py:280
  408.2 325.2 %all-gather.61.cloned.1.call-start = ((), (), s32[]{:S(2)}) async-start(), calls=%async_computation.28 | async-start | bytes 3981312 | tf_op jit(solution)/shard_map/all_gather | solution.py:285
  409.0 350.8 %all-gather.35.cloned.1.call-start = ((), (), s32[]{:S(2)}) async-start(), calls=%async_computation.10 | async-start | bytes 3317760 | tf_op jit(solution)/shard_map/all_gather | solution.py:128
  409.0 31.2 %copy-start.50 = (s32[1024]{0:T(1024)}, s32[1024]{0:T(1024)S(1)}, u32[]{:S(2)}) copy-start(s32[1024]{0:T(1024)S(1)} %pad_clamp_fusion) | copy-start | bytes 12292
  409.1 35.4 %copy-start.42 = (f32[768]{0:T(1024)}, f32[768]{0:T(1024)S(1)}, u32[]{:S(2)}) copy-start(f32[768]{0:T(1024)S(1)} %convert_element_type.298) | copy-start | bytes 9220
  444.2 248.8 %copy-start.2 = (f32[384,768]{1,0:T(8,128)}, f32[384,768]{1,0:T(8,128)S(1)}, u32[]{:S(2)}) copy-start(f32[384,768]{1,0:T(8,128)S(1)} %get-tuple-element.463) | copy-start | bytes 3538948
  444.2 54.9 %copy-start.44 = (f32[384]{0:T(512)}, f32[384]{0:T(512)S(1)}, u32[]{:S(2)}) copy-start(f32[384]{0:T(512)S(1)} %broadcast_multiply_fusion.1) | copy-start | bytes 4612
  444.5 111.4 %copy-start.60 = (f32[384]{0:T(512)}, f32[384]{0:T(512)S(1)}, u32[]{:S(2)}) copy-start(f32[384]{0:T(512)S(1)} %multiply_reduce_fusion.9) | copy-start | bytes 4612
  444.5 111.4 %copy-start.52 = (f32[384]{0:T(512)}, f32[384]{0:T(512)S(1)}, u32[]{:S(2)}) copy-start(f32[384]{0:T(512)S(1)} %fusion.206) | copy-start | bytes 4612
  701.5 125.7 %all-gather.63.cloned.1.call-start = ((), (), s32[]{:S(2)}) async-start(), calls=%async_computation.29 | async-start | bytes 3981312 | tf_op jit(solution)/shard_map/all_gather | solution.py:286
  702.1 151.5 %all-gather.37.cloned.1.call-start = ((), (), s32[]{:S(2)}) async-start(), calls=%async_computation.12 | async-start | bytes 3317760 | tf_op jit(solution)/shard_map/all_gather | solution.py:179
  702.7 199.3 %reduce-scatter.17.cloned.1.call-start = ((), (), s32[]{:S(2)}) async-start(), calls=%async_computation.13 | async-start | bytes 3317760 | tf_op jit(solution)/shard_map/reduce_scatter | solution.py:204
  853.6 9.3 copy-start.76
  866.9 72.4 %reduce-scatter.15.cloned.1.call-start = ((), (), s32[]{:S(2)}) async-start(), calls=%async_computation.11 | async-start | bytes 3317760 | tf_op jit(solution)/shard_map/reduce_scatter | solution.py:135
  873.7 29.5 %copy-start.51 = (s32[1024]{0:T(1024)S(1)}, s32[1024]{0:T(1024)}, u32[]{:S(2)}) copy-start(s32[1024]{0:T(1024)} %copy-done.50) | copy-start | bytes 12292
  873.7 263.3 %all-gather.39.cloned.1.call-start = ((), (), s32[]{:S(2)}) async-start(), calls=%async_computation.14 | async-start | bytes 3317760 | tf_op jit(solution)/shard_map/all_gather | solution.py:179
  947.6 207.5 %copy-start.4 = (f32[384,768]{1,0:T(8,128)}, f32[384,768]{1,0:T(8,128)S(1)}, u32[]{:S(2)}) copy-start(f32[384,768]{1,0:T(8,128)S(1)} %add_add_fusion.7) | copy-start | bytes 3538948
  1111.1 74.3 %reduce-scatter.19.cloned.1.call-start = ((), (), s32[]{:S(2)}) async-start(), calls=%async_computation.15 | async-start | bytes 3317760 | tf_op jit(solution)/shard_map/reduce_scatter | solution.py:204
  1137.0 9.3 copy-start.75
  1150.3 328.6 %reduce-scatter.27.cloned.1.call-start = ((), (), s32[]{:S(2)}) async-start(), calls=%async_computation.31 | async-start | bytes 9732096
  1169.8 313.2 %reduce-scatter.25.cloned.1.call-start = ((), (), s32[]{:S(2)}) async-start(), calls=%async_computation.30 | async-start | bytes 9732096
  1196.9 132.4 %copy-start.1 = (bf16[384,768]{1,0:T(8,128)(2,1)S(1)}, bf16[384,768]{1,0:T(8,128)(2,1)}, u32[]{:S(2)}) copy-start(bf16[384,768]{1,0:T(8,128)(2,1)} %param.21) | copy-start | bytes 1769476
  1196.9 132.4 %copy-start.35 = (f32[768]{0:T(1024)S(1)}, f32[768]{0:T(1024)}, u32[]{:S(2)}) copy-start(f32[768]{0:T(1024)} %copy-done.34) | copy-start | bytes 9220
  1196.9 132.4 %copy-start.37 = (f32[384]{0:T(512)S(1)}, f32[384]{0:T(512)}, u32[]{:S(2)}) copy-start(f32[384]{0:T(512)} %copy-done.36) | copy-start | bytes 4612
  1196.9 132.4 %copy-start.39 = (f32[384]{0:T(512)S(1)}, f32[384]{0:T(512)}, u32[]{:S(2)}) copy-start(f32[384]{0:T(512)} %copy-done.38) | copy-start | bytes 4612
  1346.9 368.3 %reduce-scatter.23.cloned.1.call-start = ((), (), s32[]{:S(2)}) async-start(), calls=%async_computation.17 | async-start | bytes 15925248 | tf_op jit(solution)/shard_map/reduce_scatter | solution.py:190
  1389.2 557.8 %reduce-scatter.21.cloned.1.call-start = ((), (), s32[]{:S(2)}) async-start(), calls=%async_computation.16 | async-start | bytes 15925248 | tf_op jit(solution)/shard_map/reduce_scatter | solution.py:190
  1389.5 8.6 copy-start.77
  (59 other events, 149.9 us)
Sparse Core Ops, SparseCore 0:
  11.5 56.7 all-gather.44
  71.8 53.1 all-gather.42
  128.4 52.9 all-gather.40
  184.7 53.0 all-gather.46
  240.4 64.1 all-gather.48
  306.6 24.2 all-gather.32
  333.6 65.1 all-gather.50
  405.7 33.3 reduce-scatter.12
  442.4 54.0 all-gather.56
  500.2 52.9 all-gather.54
  557.1 52.9 all-gather.52
  613.2 53.0 all-gather.58
  669.3 64.0 all-gather.60
  735.5 24.2 all-gather.34
  762.0 65.1 all-gather.62
  829.3 24.2 all-gather.36
  867.0 34.8 reduce-scatter.16
  904.4 34.8 reduce-scatter.14
  1111.2 25.7 all-gather.38
  1150.4 34.8 reduce-scatter.18
  1191.3 135.6 reduce-scatter.26
  1347.1 135.9 reduce-scatter.24
  1486.7 228.4 reduce-scatter.22
  1718.7 228.2 reduce-scatter.20
where the time goes:
time: 1980 us; the launch traced here: 1960 us
  waiting for transfers between devices  1120 us (57%)
  matrix products  369 us (19%)
  local copies, waits for them, and re-layouts  220 us (11%)
  blocking collectives  82.8 us (4%)
  loops' own time  79.3 us (4%)
  other arithmetic  70.6 us (4%)
    reduce_scatter x2, waiting for transfers between devices, layer_backward(): lax.psum_scatter(jnp.stack([in_term, out_term], 1).reshape(lax.axis_size(...  456 us
    all_gather x2, waiting for transfers between devices, on_device(): lax.all_gather(query_weight[layer_index], ('dp', 'expert'), axis=0, tiled...  109 us
    all_gather x2, waiting for transfers between devices, on_device(): lax.all_gather(key_weight[layer_index], ('dp', 'expert'), axis=0, tiled=T...  108 us
    dot_general x80, matrix products, contract_cols(): lax.dot_general(left, right, (((1,), (1,)), ((), ())), preferred_element_...  106 us
    all_gather x2, waiting for transfers between devices, on_device(): lax.all_gather(expert_out[layer_index], 'dp', axis=2, tiled=True)  102 us
    dot_general x56, matrix products, contract_rows(): lax.dot_general(left, right, (((0,), (0,)), ((), ())), preferred_element_...  89.6 us
    all_gather x2, waiting for transfers between devices, on_device(): lax.all_gather(expert_in[layer_index], 'dp', axis=1, tiled=True)  83.6 us
    unnamed x2, blocking collectives  82.8 us
  transfers between devices with their start and end apart: 24, of which 20 were waited for; matrix products, arithmetic and copies ran while one was open for 24% of the time, Pallas kernels for 0%

commit v1 on v0

v1 whole, which is shorter than its diff:
```python
from functools import partial

import jax
import jax.numpy as jnp
from jax import lax
from jax.experimental import pallas as pl
from jax.experimental.pallas import tpu as pltpu
from jax.sharding import PartitionSpec as P

HEADS = 12
HEAD_DIM = 64
EXPERTS = 3
LAYERS = 2
MOST = 144

SLOTS = EXPERTS * MOST
PAIR = 2 * HEAD_DIM
epsilon = 1e-05
score_scale = 0.125
FAR = -1e30
VMEM_BYTES = 56 << 20
f32 = jnp.float32
bf16 = jnp.bfloat16


def mat(left, right):
    return jnp.dot(left, right, preferred_element_type=f32)


def contract_rows(left, right):
    return lax.dot_general(left, right, (((0,), (0,)), ((), ())), preferred_element_type=f32)


def contract_cols(left, right):
    return lax.dot_general(left, right, (((1,), (1,)), ((), ())), preferred_element_type=f32)


def norm_parts(values):
    average = jnp.mean(values, -1, keepdims=True)
    centered = values - average
    spread = jnp.mean(centered * centered, -1, keepdims=True)
    rate = lax.rsqrt(spread + epsilon)
    return centered * rate, rate


def norm_back(unit, rate, scaled_grad):
    first = jnp.mean(scaled_grad, -1, keepdims=True)
    second = jnp.mean(scaled_grad * unit, -1, keepdims=True)
    return rate * (scaled_grad - first - unit * second)


def whole_call(body, out_shape, scratch_shapes=(), name=None):
    return pl.pallas_call(
        body,
        out_shape=out_shape,
        scratch_shapes=scratch_shapes,
        compiler_params=pltpu.CompilerParams(vmem_limit_bytes=VMEM_BYTES),
        name=name,
    )


def attend_forward_body(first, *refs):
    if first:
        rows_ref, spot_ref, bias_ref, gain_ref, weight_ref = refs[:5]
        outs = refs[5:]
        rows = rows_ref[...].astype(f32)
    else:
        rows_ref, part_a_ref, part_b_ref, spot_ref, bias_ref, gain_ref, weight_ref = refs[:7]
        outs = refs[7:]
        spot = spot_ref[...]
        rows = rows_ref[...] + mat(spot, part_a_ref[...]) + mat(spot, part_b_ref[...])
    width = rows.shape[1]
    triple_ref, logs_ref, context_ref, hidden_ref, slots_ref = outs[:5]
    if not first:
        outs[5][...] = rows
    unit, _ = norm_parts(rows)
    normed = (unit * gain_ref[0:1, :]).astype(bf16)
    triple_ref[...] = mat(normed, weight_ref[:, : 3 * width]).astype(bf16)
    row_count = rows.shape[0]
    lane = lax.broadcasted_iota(jnp.int32, (row_count, PAIR), 1)
    logs_ref[...] = jnp.zeros_like(logs_ref)

    def one_pair(pair, carry):
        at = pl.multiple_of(pair * PAIR, PAIR)
        query = triple_ref[:, pl.ds(at, PAIR)]
        key = triple_ref[:, pl.ds(at + width, PAIR)]
        value = triple_ref[:, pl.ds(at + 2 * width, PAIR)]
        sides = []
        logs = logs_ref[...]
        for side in range(2):
            mine = (lane >= HEAD_DIM) if side else (lane < HEAD_DIM)
            scores = contract_cols(jnp.where(mine, query, jnp.zeros((), bf16)), key)
            scores = scores * score_scale + bias_ref[...]
            highest = jnp.max(scores, 1, keepdims=True)
            powers = jnp.exp(scores - highest)
            totals = jnp.sum(powers, 1, keepdims=True)
            probs = (powers * (1.0 / totals)).astype(bf16)
            sides.append(mat(probs, value))
            logs = jnp.where(lane == 2 * pair + side, highest + jnp.log(totals), logs)
        logs_ref[...] = logs
        context_ref[:, pl.ds(at, PAIR)] = jnp.where(lane < HEAD_DIM, sides[0], sides[1]).astype(bf16)
        return carry

    lax.fori_loop(0, HEADS // 2, one_pair, 0)
    hidden = rows + mat(context_ref[...], weight_ref[:, 3 * width :])
    hidden_ref[...] = hidden
    unit, _ = norm_parts(hidden)
    second = (unit * gain_ref[1:2, :]).astype(bf16)
    slots_ref[...] = contract_rows(spot_ref[...], second).astype(bf16)


def attend_backward_body(last, *refs):
    (
        part_a_ref,
        part_b_ref,
        grad_ref,
        hidden_ref,
        rows_ref,
        triple_ref,
        logs_ref,
        context_ref,
        spot_ref,
        bias_ref,
        gain_ref,
        weight_ref,
    ) = refs[:12]
    if last:
        grad_out_ref, weight_grad_ref, context_grad_ref, triple_grad_ref = refs[12:]
        slots_ref = None
    else:
        grad_out_ref, weight_grad_ref, slots_ref, context_grad_ref, triple_grad_ref = refs[12:]
    spot = spot_ref[...]
    second_grad = mat(spot, part_a_ref[...]) + mat(spot, part_b_ref[...])
    unit, rate = norm_parts(hidden_ref[...])
    second_gain_grad = jnp.sum(second_grad * unit, 0, keepdims=True)
    hidden_grad = grad_ref[...] + norm_back(unit, rate, second_grad * gain_ref[1:2, :])
    row_count, width = hidden_grad.shape
    grad_out_ref[...] = hidden_grad
    branch = hidden_grad.astype(bf16)
    context_grad_ref[...] = contract_cols(branch, weight_ref[:, 3 * width :]).astype(bf16)
    weight_grad_ref[:, 3 * width : 4 * width] = contract_rows(context_ref[...], branch).astype(bf16)
    lane = lax.broadcasted_iota(jnp.int32, (row_count, PAIR), 1)

    def one_pair(pair, carry):
        at = pl.multiple_of(pair * PAIR, PAIR)
        query = triple_ref[:, pl.ds(at, PAIR)]
        key = triple_ref[:, pl.ds(at + width, PAIR)]
        value = triple_ref[:, pl.ds(at + 2 * width, PAIR)]
        gone = context_grad_ref[:, pl.ds(at, PAIR)]
        zero = jnp.zeros((), bf16)
        query_sides, key_sides, value_sides = [], [], []
        for side in range(2):
            mine = (lane >= HEAD_DIM) if side else (lane < HEAD_DIM)
            log_total = jnp.sum(
                jnp.where(lane == 2 * pair + side, logs_ref[...], 0.0), 1, keepdims=True
            )
            scores = contract_cols(jnp.where(mine, query, zero), key)
            scores = scores * score_scale + bias_ref[...]
            probs = jnp.exp(scores - log_total)
            prob_grad = contract_cols(jnp.where(mine, gone, zero), value)
            inner = jnp.sum(probs * prob_grad, 1, keepdims=True)
            score_grad = (probs * (prob_grad - inner)).astype(bf16)
            query_sides.append(mat(score_grad, key))
            key_sides.append(contract_rows(score_grad, query))
            value_sides.append(contract_rows(probs.astype(bf16), gone))
        left = lane < HEAD_DIM
        triple_grad_ref[:, pl.ds(at, PAIR)] = (
            score_scale * jnp.where(left, query_sides[0], query_sides[1])
        ).astype(bf16)
        triple_grad_ref[:, pl.ds(at + width, PAIR)] = (
            score_scale * jnp.where(left, key_sides[0], key_sides[1])
        ).astype(bf16)
        triple_grad_ref[:, pl.ds(at + 2 * width, PAIR)] = jnp.where(
            left, value_sides[0], value_sides[1]
        ).astype(bf16)
        return carry

    lax.fori_loop(0, HEADS // 2, one_pair, 0)
    unit, rate = norm_parts(rows_ref[...].astype(f32))
    normed = (unit * gain_ref[0:1, :]).astype(bf16)
    triple_grad = triple_grad_ref[...]
    weight_grad_ref[:, : 3 * width] = contract_rows(normed, triple_grad).astype(bf16)
    normed_grad = contract_cols(triple_grad, weight_ref[:, : 3 * width])
    first_gain_grad = jnp.sum(normed_grad * unit, 0, keepdims=True)
    out_grad = grad_out_ref[...] + norm_back(unit, rate, normed_grad * gain_ref[0:1, :])
    grad_out_ref[...] = out_grad
    if slots_ref is not None:
        slots_ref[...] = contract_rows(spot, out_grad.astype(bf16)).astype(bf16)
    which = lax.broadcasted_iota(jnp.int32, (PAIR, width), 0)
    gain_rows = jnp.where(
        which == 0, first_gain_grad, jnp.where(which == 1, second_gain_grad, 0.0)
    )
    weight_grad_ref[:, 4 * width :] = gain_rows.T.astype(bf16)


def expert_forward_body(*refs):
    block_refs, weight_ref = refs[:4], refs[4]
    out_refs, active_ref, slope_ref = refs[5:9], refs[9], refs[10]
    width = block_refs[0].shape[1]
    units = weight_ref.shape[1] // 2
    for half in range(2):
        rows = jnp.concatenate([block_refs[2 * half][...], block_refs[2 * half + 1][...]], 0)
        before = mat(rows, weight_ref[:, :units])
        share = 0.5 + 0.5 * lax.erf(before * 0.7071067811865476)
        slope = share + before * (0.3989422804014327 * jnp.exp(-0.5 * before * before))
        active = (before * share).astype(bf16)
        span = slice(half * 2 * MOST, (half + 1) * 2 * MOST)
        active_ref[span, :] = active
        slope_ref[span, :] = slope.astype(bf16)
        sums = contract_cols(active, weight_ref[:, units:]).astype(bf16)
        out_refs[2 * half][...] = sums[:MOST]
        out_refs[2 * half + 1][...] = sums[MOST:]


def expert_backward_body(*refs):
    grad_refs, block_refs = refs[:4], refs[4:8]
    active_ref, slope_ref, weight_ref = refs[8:11]
    out_refs, weight_grad_ref = refs[11:15], refs[15]
    units = weight_ref.shape[1] // 2
    grads = jnp.concatenate([ref[...] for ref in grad_refs], 0)
    rows = jnp.concatenate([ref[...] for ref in block_refs], 0)
    active_grad = mat(grads, weight_ref[:, units:])
    before_grad = (active_grad * slope_ref[...].astype(f32)).astype(bf16)
    sums = contract_cols(before_grad, weight_ref[:, :units]).astype(bf16)
    for place in range(4):
        out_refs[place][...] = sums[place * MOST : (place + 1) * MOST]
    weight_grad_ref[:, :units] = contract_rows(rows, before_grad).astype(bf16)
    weight_grad_ref[:, units:] = contract_rows(grads, active_ref[...]).astype(bf16)


def expert_forward(blocks, weights):
    width = blocks[0].shape[1]
    units = weights.shape[1] // (2 * EXPERTS)
    block = pl.BlockSpec((MOST, width), lambda e: (e, 0))
    kept = pl.BlockSpec((4 * MOST, units), lambda e: (e, 0))
    outs = pl.pallas_call(
        expert_forward_body,
        grid=(EXPERTS,),
        in_specs=[block] * 4 + [pl.BlockSpec((width, 2 * units), lambda e: (0, e))],
        out_specs=[block] * 4 + [kept] * 2,
        out_shape=[jax.ShapeDtypeStruct((SLOTS, width), bf16)] * 4
        + [jax.ShapeDtypeStruct((4 * SLOTS, units), bf16)] * 2,
        compiler_params=pltpu.CompilerParams(vmem_limit_bytes=VMEM_BYTES),
        name="expert_forward",
    )(*blocks, weights)
    return outs[:4], outs[4], outs[5]


def expert_backward(grads, blocks, active, slope, weights):
    width = blocks[0].shape[1]
    units = weights.shape[1] // (2 * EXPERTS)
    block = pl.BlockSpec((MOST, width), lambda e: (e, 0))
    kept = pl.BlockSpec((4 * MOST, units), lambda e: (e, 0))
    square = pl.BlockSpec((width, 2 * units), lambda e: (0, e))
    outs = pl.pallas_call(
        expert_backward_body,
        grid=(EXPERTS,),
        in_specs=[block] * 8 + [kept] * 2 + [square],
        out_specs=[block] * 4 + [square],
        out_shape=[jax.ShapeDtypeStruct((SLOTS, width), bf16)] * 4
        + [jax.ShapeDtypeStruct(weights.shape, bf16)],
        compiler_params=pltpu.CompilerParams(vmem_limit_bytes=VMEM_BYTES),
        name="expert_backward",
    )(*grads, *blocks, active, slope, weights)
    return outs[:4], outs[4]


def swap(values, flip):
    count = lax.axis_size("expert")
    return lax.ppermute(values, "expert", [(i, i ^ flip) for i in range(count)])


def spread_slots(slots):
    across = swap(slots, 2)
    beside = swap(slots, 1)
    corner = swap(across, 1)
    return [slots, beside, across, corner]


def collect_slots(parts):
    own, beside, across, corner = parts
    corner_in = swap(corner, 1)
    beside_in = swap(beside, 1)
    far = (across.astype(f32) + corner_in.astype(f32)).astype(bf16)
    far_in = swap(far, 2)
    near = (own.astype(f32) + beside_in.astype(f32)).astype(bf16)
    return near, far_in


def on_device(
    tokens,
    groups,
    key_mask,
    routes,
    query_weight,
    key_weight,
    value_weight,
    output_weight,
    norm_first,
    norm_second,
    expert_in,
    expert_out,
    cotangent,
):
    both = ("dp", "expert")
    row_count, width = tokens.shape
    units = expert_in.shape[3]
    shard_rows = expert_in.shape[2]
    own_rows = query_weight.shape[1]

    gains = jnp.stack([norm_first[0], norm_second[0], norm_first[1], norm_second[1]], 1)
    gains = jnp.pad(gains, ((0, 0), (0, PAIR - gains.shape[1])))
    attention_shard = jnp.concatenate(
        [
            weight[layer]
            for layer in range(LAYERS)
            for weight in (query_weight, key_weight, value_weight, output_weight)
        ]
        + [gains],
        1,
    )
    attention_all = lax.all_gather(attention_shard, both, axis=0, tiled=True)
    gain_rows = attention_all[:, 4 * LAYERS * width :].T.astype(f32)

    def expert_shard(layer):
        pieces = jnp.concatenate(
            [expert_in[layer], jnp.transpose(expert_out[layer], (0, 2, 1))], 2
        )
        return jnp.transpose(pieces, (1, 0, 2)).reshape(shard_rows, EXPERTS * 2 * units)

    experts_all = [
        lax.all_gather(expert_shard(layer), "dp", axis=0, tiled=True) for layer in range(LAYERS)
    ]

    route = routes[:, 0]
    place = jnp.arange(row_count, dtype=jnp.int32)
    earlier = (route[:, None] == route[None, :]) & (place[None, :] < place[:, None])
    slot_of = route * MOST + jnp.sum(earlier.astype(jnp.int32), 1)
    spot = (slot_of[:, None] == jnp.arange(SLOTS, dtype=jnp.int32)[None, :]).astype(bf16)
    group = groups[0]
    allowed = (group[:, None] == group[None, :]) & (
        (key_mask[None, :] == 1) | (place[:, None] == place[None, :])
    )
    bias = jnp.where(allowed, 0.0, FAR).astype(f32)

    last_grads = spread_slots(contract_rows(spot, cotangent.astype(bf16)).astype(bf16))

    def shape_of(rows, cols, kind):
        return jax.ShapeDtypeStruct((rows, cols), kind)

    saved = []
    rows = tokens
    parts = None
    for layer in range(LAYERS):
        first = layer == 0
        weight = attention_all[:, 4 * layer * width : 4 * (layer + 1) * width]
        gain = gain_rows[2 * layer : 2 * layer + 2]
        outs = whole_call(
            partial(attend_forward_body, first),
            [
                shape_of(row_count, 3 * width, bf16),
                shape_of(row_count, PAIR, f32),
                shape_of(row_count, width, bf16),
                shape_of(row_count, width, f32),
                shape_of(SLOTS, width, bf16),
            ]
            + ([] if first else [shape_of(row_count, width, f32)]),
            name="attend_forward",
        )(*([rows] if first else [rows, *parts]), spot, bias, gain, weight)
        triple, logs, context, hidden, slots = outs[:5]
        inputs = tokens if first else outs[5]
        blocks = spread_slots(slots)
        sums, active, slope = expert_forward(blocks, experts_all[layer])
        parts = collect_slots(sums)
        rows = hidden
        saved.append((inputs, triple, logs, context, hidden, blocks, active, slope, weight, gain))
    mixed = (rows + mat(spot, parts[0]) + mat(spot, parts[1])).astype(bf16)

    grad = cotangent
    grad_blocks = last_grads
    results = [None] * LAYERS
    for layer in reversed(range(LAYERS)):
        inputs, triple, logs, context, hidden, blocks, active, slope, weight, gain = saved[layer]
        last = layer == 0
        sums, expert_grad = expert_backward(
            grad_blocks, blocks, active, slope, experts_all[layer]
        )
        expert_total = lax.psum_scatter(expert_grad, "dp", scatter_dimension=0, tiled=True)
        parts = collect_slots(sums)
        outs = whole_call(
            partial(attend_backward_body, last),
            [
                shape_of(row_count, width, f32),
                shape_of(width, 4 * width + PAIR, bf16),
            ]
            + ([] if last else [shape_of(SLOTS, width, bf16)]),
            scratch_shapes=[
                pltpu.VMEM((row_count, width), bf16),
                pltpu.VMEM((row_count, 3 * width), bf16),
            ],
            name="attend_backward",
        )(*parts, grad, hidden, inputs, triple, logs, context, spot, bias, gain, weight)
        grad, attention_grad = outs[:2]
        attention_total = lax.psum_scatter(attention_grad, both, scatter_dimension=0, tiled=True)
        if not last:
            grad_blocks = spread_slots(outs[2])
        results[layer] = (attention_total, expert_total)

    def columns(layer, start, stop):
        return results[layer][0][:, start:stop].astype(f32)

    deltas = [
        jnp.stack([columns(layer, i * width, (i + 1) * width) for layer in range(LAYERS)])
        for i in range(4)
    ]
    gain_deltas = [
        jnp.stack([columns(layer, 4 * width + i, 4 * width + i + 1)[:, 0] for layer in range(LAYERS)])
        for i in range(2)
    ]
    pieces = [
        results[layer][1].reshape(shard_rows, EXPERTS, 2, units).astype(f32)
        for layer in range(LAYERS)
    ]
    delta_in = jnp.stack([jnp.transpose(piece[:, :, 0], (1, 0, 2)) for piece in pieces])
    delta_out = jnp.stack([jnp.transpose(piece[:, :, 1], (1, 2, 0)) for piece in pieces])
    return (mixed, grad, *deltas, *gain_deltas, delta_in, delta_out)


def solution(mesh):
    placed = (
        P(("dp", "expert"), None),
        P(("dp", "expert"), None),
        P(("dp", "expert")),
        P(("dp", "expert"), None),
        P(None, ("dp", "expert"), None),
        P(None, ("dp", "expert"), None),
        P(None, ("dp", "expert"), None),
        P(None, ("dp", "expert"), None),
        P(None, ("dp", "expert")),
        P(None, ("dp", "expert")),
        P(None, None, "dp", "expert"),
        P(None, None, "expert", "dp"),
        P(("dp", "expert"), None),
    )
    return jax.shard_map(
        on_device,
        mesh=mesh,
        in_specs=placed,
        out_specs=(
            P(("dp", "expert"), None),
            P(("dp", "expert"), None),
            P(None, ("dp", "expert"), None),
            P(None, ("dp", "expert"), None),
            P(None, ("dp", "expert"), None),
            P(None, ("dp", "expert"), None),
            P(None, ("dp", "expert")),
            P(None, ("dp", "expert")),
            P(None, None, "dp", "expert"),
            P(None, None, "expert", "dp"),
        ),
        check_vma=False,
    )
```

time: 1980 us -> 952 us (0.48)
  waiting for transfers between devices: 1120 us -> 732 us
  matrix products: 369 us -> 3.73 us
  local copies, waits for them, and re-layouts: 220 us -> 39.6 us
  Pallas kernels: 0 us -> 127 us
  blocking collectives: 82.8 us -> 0 us
  loops' own time: 79.3 us -> 0 us
  other arithmetic: 70.6 us -> 16.7 us
    all_gather x16 -> x3, waiting for transfers between devices: 559 us -> 178 us  [the longest x2 98.1 us: on_device(): lax.all_gather(expert_shard(layer), 'dp', axis=0, tiled=True)]
    reduce_scatter x6 -> x2, waiting for transfers between devices: 557 us -> 253 us  [on_device(): lax.psum_scatter(expert_grad, 'dp', scatter_dimension=0, tiled=True)]
    dot_general x148 -> x2, matrix products: 279 us -> 3.08 us  [mat(): return jnp.dot(left, right, preferred_element_type=f32)]
    unnamed x26 -> x7, waiting for transfers between devices: 6.38 us -> 160 us
    ppermute x0 -> x24, waiting for transfers between devices: none -> 141 us  [swap(): return lax.ppermute(values, 'expert', [(i, i ^ flip) for i in range(count)])]
    pallas_call x0 -> x8, Pallas kernels: none -> 127 us  [the longest x2 46.2 us: on_device(): whole_call(partial(attend_backward_body, last), [shape_of(row_count, widt...]
    dot_general x56 -> x1, matrix products: 89.6 us -> 0.64 us  [contract_rows(): lax.dot_general(left, right, (((0,), (0,)), ((), ())), preferred_element_...]
    unnamed x2 -> x0, blocking collectives: 82.8 us -> none
  transfers between devices with their start and end apart: 24 -> 30, of which waited for: 20 -> 19; matrix products, arithmetic and copies ran while one was open for 24% -> 4% of each run, Pallas kernels for 0% -> 5%
where the time goes in v1:
time: 952 us; the launch traced here: 948 us
  waiting for transfers between devices  732 us (77%)
  Pallas kernels  127 us (13%)
  local copies, waits for them, and re-layouts  39.6 us (4%)
  other arithmetic  16.7 us (2%)
  between operations  14.7 us (2%)
  starting transfers between devices  13.5 us (1%)
    reduce_scatter x2, waiting for transfers between devices, on_device(): lax.psum_scatter(expert_grad, 'dp', scatter_dimension=0, tiled=True)  253 us
    unnamed x7, waiting for transfers between devices  160 us
    ppermute x24, waiting for transfers between devices, swap(): return lax.ppermute(values, 'expert', [(i, i ^ flip) for i in range(count)])  141 us
    all_gather x2, waiting for transfers between devices, on_device(): lax.all_gather(expert_shard(layer), 'dp', axis=0, tiled=True)  98.1 us
    all_gather x1, waiting for transfers between devices, on_device(): attention_all = lax.all_gather(attention_shard, both, axis=0, tiled=True)  80 us
    pallas_call x2, Pallas kernels, on_device(): whole_call(partial(attend_backward_body, last), [shape_of(row_count, widt...  46.2 us
    pallas_call x2, Pallas kernels, expert_backward(): pl.pallas_call(expert_backward_body, grid=(EXPERTS,), in_specs=[block] *...  31.3 us
    pallas_call x2, Pallas kernels, on_device(): whole_call(partial(attend_forward_body, first), [shape_of(row_count, 3 *...  29 us
  transfers between devices with their start and end apart: 30, of which 19 were waited for; matrix products, arithmetic and copies ran while one was open for 4% of the time, Pallas kernels for 5%

profile of v1, /device:TPU:0, one launch (start us, length us, event | category | flops | bytes accessed | tf_op | source)
XLA Modules:
  0.0 947.6 jit_solution(7765618620349359048)
XLA Ops:
  15.1 1.2 slice_bitcast_fusion
  20.9 80.0 %all-gather.4.cloned.1.call-done = bf16[768,6272]{1,0:T(8,128)(2,1)} async-done(((bf16[24,6272]{1,0:T(8,128)(2,1)}), bf16[768,6272]{1,0:T(8,128)(2,1)}) %all-gather.4.cloned.1.call-update) | async-done | bytes 9633808 | tf_op jit(solution)/shard_map/all_gather | solution.py:322
  102.7 8.4 fusion.12
  111.2 13.9 %attend_forward.2 = (bf16[384,2304]{1,0:T(8,128)(2,1)}, f32[384,128]{1,0:T(8,128)}, bf16[384,768]{1,0:T(8,128)(2,1)}, f32[384,768]{1,0:T(8,128)}, bf16[432,768]{1,0:T(8,128)(2,1)}) custom-call(bf16[384,768]{1,0:T(8,128)(2,1)} %refs_4_.1, bf16[384,432]{1,0:T(8,128)(2,1)} %fusion.3.refs_1_.refs_3_.refs_8_, f32[384,384]{1,0:T(8,128)} %fusion.8.refs_2_.refs_4_.refs_9_, ...), custom_call_target="tpu_custom_call" | custom-call | tf_op jit(solution)/shard_map/attend_forward/pallas_call | solution.py:358
  125.1 1.5 collective-permute-start.1
  126.5 15.8 %collective-permute-done.1.refs_2_.refs_6_ = bf16[432,768]{1,0:T(8,128)(2,1)S(1)} collective-permute-done((bf16[432,768]{1,0:T(8,128)(2,1)}, bf16[432,768]{1,0:T(8,128)(2,1)S(1)}, u32[]{:S(2)}, u32[]{:S(2)}) %collective-permute-start.1) | collective-permute-done | bytes 663584 | tf_op jit(solution)/shard_map/ppermute | solution.py:270
  142.4 68.7 %all-gather.6.cloned.1.call-done.refs_4_.refs_10_ = bf16[768,4608]{1,0:T(8,128)(2,1)} async-done(((bf16[96,4608]{1,0:T(8,128)(2,1)}), bf16[768,4608]{1,0:T(8,128)(2,1)}) %all-gather.6.cloned.1.call-update) | async-done | bytes 7077904 | tf_op jit(solution)/shard_map/all_gather | solution.py:332
  212.8 10.8 %expert_forward.2 = (bf16[432,768]{1,0:T(8,128)(2,1)}, bf16[432,768]{1,0:T(8,128)(2,1)}, bf16[432,768]{1,0:T(8,128)(2,1)}, bf16[432,768]{1,0:T(8,128)(2,1)}, bf1...) custom-call(bf16[432,768]{1,0:T(8,128)(2,1)} %get-tuple-element.49.refs_0_.refs_4_, bf16[432,768]{1,0:T(8,128)(2,1)} %copy-done.4, ...), custom_call_target="tpu_custom_call" | custom-call | tf_op jit(solution)/shard_map/expert_forward/pallas_call | solution.py:236
  224.1 1.8 collective-permute-done.4
  225.9 1.2 add_convert_fusion.6
  227.2 1.3 collective-permute-start.5
  230.3 13.9 %collective-permute-done.5.refs_2_ = bf16[432,768]{1,0:T(8,128)(2,1)S(1)} collective-permute-done((bf16[432,768]{1,0:T(8,128)(2,1)S(1)}, bf16[432,768]{1,0:T(8,128)(2,1)S(1)}, u32[]{:S(2)}, u32[]{:S(2)}) %collective-permute-start.5) | collective-permute-done | bytes 663584 | tf_op jit(solution)/shard_map/ppermute | solution.py:270
  245.1 15.1 %attend_forward.3 = (bf16[384,2304]{1,0:T(8,128)(2,1)}, f32[384,128]{1,0:T(8,128)}, bf16[384,768]{1,0:T(8,128)(2,1)}, f32[384,768]{1,0:T(8,128)}, bf16[432,768]{1,0:T(8,128)(2,1)}, /*index=5*/f32[384,768]{1,0:T(8,128)}) custom-call(f32[384,768]{1,0:T(8,128)} %get-tuple-element.48.refs_0_.refs_3_, bf16[432,768]{1,0:T(8,128)(2,1)} %add_convert_fusion.7.refs_1_, ...), custom_call_target="tpu_custom_call" | custom-call | tf_op jit(solution)/shard_map/attend_forward/pallas_call | solution.py:358
  260.2 1.3 collective-permute-start.7
  262.9 15.3 %collective-permute-done.7.refs_2_.refs_6_ = bf16[432,768]{1,0:T(8,128)(2,1)S(1)} collective-permute-done((bf16[432,768]{1,0:T(8,128)(2,1)}, bf16[432,768]{1,0:T(8,128)(2,1)S(1)}, u32[]{:S(2)}, u32[]{:S(2)}) %collective-permute-start.7) | collective-permute-done | bytes 663584 | tf_op jit(solution)/shard_map/ppermute | solution.py:270
  278.7 12.1 %collective-permute-done.13.refs_2_ = bf16[432,768]{1,0:T(8,128)(2,1)S(1)} collective-permute-done((bf16[432,768]{1,0:T(8,128)(2,1)S(1)}, bf16[432,768]{1,0:T(8,128)(2,1)S(1)}, u32[]{:S(2)}, u32[]{:S(2)}) %collective-permute-start.13) | collective-permute-done | bytes 663584 | tf_op jit(solution)/shard_map/ppermute | solution.py:270
  290.8 29.4 %all-gather.8.cloned.1.call-done.refs_4_.refs_10_ = bf16[768,4608]{1,0:T(8,128)(2,1)} async-done(((bf16[96,4608]{1,0:T(8,128)(2,1)}), bf16[768,4608]{1,0:T(8,128)(2,1)}) %all-gather.8.cloned.1.call-update) | async-done | bytes 7077904 | tf_op jit(solution)/shard_map/all_gather | solution.py:332
  321.2 10.1 %expert_forward.3 = (bf16[432,768]{1,0:T(8,128)(2,1)}, bf16[432,768]{1,0:T(8,128)(2,1)}, bf16[432,768]{1,0:T(8,128)(2,1)}, bf16[432,768]{1,0:T(8,128)(2,1)}, bf1...) custom-call(bf16[432,768]{1,0:T(8,128)(2,1)} %get-tuple-element.55.refs_0_.refs_4_, bf16[432,768]{1,0:T(8,128)(2,1)} %copy-done.8, ...), custom_call_target="tpu_custom_call" | custom-call | tf_op jit(solution)/shard_map/expert_forward/pallas_call | solution.py:236
  331.3 15.6 %expert_backward.2 = (bf16[432,768]{1,0:T(8,128)(2,1)}, bf16[432,768]{1,0:T(8,128)(2,1)}, bf16[432,768]{1,0:T(8,128)(2,1)}, bf16[432,768]{1,0:T(8,128)(2,1)}, bf16[768,4608]{1,0:T(8,128)(2,1)}) custom-call(bf16[432,768]{1,0:T(8,128)(2,1)} %copy-done.2, bf16[432,768]{1,0:T(8,128)(2,1)} %collective-permute-done.12.refs_1_, bf16[432,768]{1,0:T(8,128)(2,1)} %copy-done.10, ...), custom_call_target="tpu_custom_call" | custom-call | tf_op jit(solution)/shard_map/expert_backward/pallas_call | solution.py:255
  347.5 1.8 collective-permute-done.16
  349.3 1.2 add_convert_fusion.2
  350.5 1.5 collective-permute-start.17
  352.0 1.1 add_convert_fusion.3.refs_0_
  353.1 14.5 %collective-permute-done.17.refs_1_ = bf16[432,768]{1,0:T(8,128)(2,1)S(1)} collective-permute-done((bf16[432,768]{1,0:T(8,128)(2,1)S(1)}, bf16[432,768]{1,0:T(8,128)(2,1)S(1)}, u32[]{:S(2)}, u32[]{:S(2)}) %collective-permute-start.17) | collective-permute-done | bytes 663584 | tf_op jit(solution)/shard_map/ppermute | solution.py:270
  368.4 23.5 %attend_backward.2 = (f32[384,768]{1,0:T(8,128)}, bf16[768,3200]{1,0:T(8,128)(2,1)}, bf16[432,768]{1,0:T(8,128)(2,1)}) custom-call(bf16[432,768]{1,0:T(8,128)(2,1)} %add_convert_fusion.3.refs_0_, bf16[432,768]{1,0:T(8,128)(2,1)} %copy-done.15, f32[384,768]{1,0:T(8,128)} %refs_2_.1, f32[384,768]{1,0:T(8,128)} %get-tuple-element.54.refs_3_, ...), custom_call_target="tpu_custom_call" | custom-call | tf_op jit(solution)/shard_map/attend_backward/pallas_call | solution.py:390
  391.9 1.4 collective-permute-start.19
  393.3 14.9 %collective-permute-done.19.refs_2_ = bf16[432,768]{1,0:T(8,128)(2,1)S(1)} collective-permute-done((bf16[432,768]{1,0:T(8,128)(2,1)}, bf16[432,768]{1,0:T(8,128)(2,1)S(1)}, u32[]{:S(2)}, u32[]{:S(2)}) %collective-permute-start.19) | collective-permute-done | bytes 663584 | tf_op jit(solution)/shard_map/ppermute | solution.py:270
  408.2 2.1 collective-permute-done.20.refs_3_
  411.1 15.7 %expert_backward.3 = (bf16[432,768]{1,0:T(8,128)(2,1)}, bf16[432,768]{1,0:T(8,128)(2,1)}, bf16[432,768]{1,0:T(8,128)(2,1)}, bf16[432,768]{1,0:T(8,128)(2,1)}, bf16[768,4608]{1,0:T(8,128)(2,1)}) custom-call(bf16[432,768]{1,0:T(8,128)(2,1)} %get-tuple-element.70.refs_0_, bf16[432,768]{1,0:T(8,128)(2,1)} %copy-done.12, bf16[432,768]{1,0:T(8,128)(2,1)} %copy-done.11, ...), custom_call_target="tpu_custom_call" | custom-call | tf_op jit(solution)/shard_map/expert_backward/pallas_call | solution.py:255
  427.4 1.8 collective-permute-done.22
  429.2 1.2 add_convert_fusion
  430.5 1.5 collective-permute-start.23
  432.0 1.0 add_convert_fusion.1.refs_0_
  433.0 14.5 %collective-permute-done.23.refs_1_ = bf16[432,768]{1,0:T(8,128)(2,1)S(1)} collective-permute-done((bf16[432,768]{1,0:T(8,128)(2,1)S(1)}, bf16[432,768]{1,0:T(8,128)(2,1)S(1)}, u32[]{:S(2)}, u32[]{:S(2)}) %collective-permute-start.23) | collective-permute-done | bytes 663584 | tf_op jit(solution)/shard_map/ppermute | solution.py:270
  448.3 22.7 %attend_backward.3 = (f32[384,768]{1,0:T(8,128)}, bf16[768,3200]{1,0:T(8,128)(2,1)}) custom-call(bf16[432,768]{1,0:T(8,128)(2,1)} %add_convert_fusion.1.refs_0_, bf16[432,768]{1,0:T(8,128)(2,1)} %copy-done.13, f32[384,768]{1,0:T(8,128)} %get-tuple-element.77.refs_2_, f32[384,768]{1,0:T(8,128)} %get-tuple-element.48.refs_0_.refs_3_, ...), custom_call_target="tpu_custom_call" | custom-call | tf_op jit(solution)/shard_map/attend_backward/pallas_call | solution.py:390
  472.9 2.1 collective-permute-done.10
  475.2 1.5 collective-permute-start.11
  476.7 30.1 %collective-permute-done.11 = bf16[432,768]{1,0:T(8,128)(2,1)S(1)} collective-permute-done((bf16[432,768]{1,0:T(8,128)(2,1)S(1)}, bf16[432,768]{1,0:T(8,128)(2,1)S(1)}, u32[]{:S(2)}, u32[]{:S(2)}) %collective-permute-start.11) | collective-permute-done | bytes 663584 | tf_op jit(solution)/shard_map/ppermute | solution.py:270
  507.4 2.6 fusion.1
  510.0 159.4 %all-reduce.6.cloned.1.call-done = (bf16[768,3200]{1,0:T(8,128)(2,1)}, bf16[768,3200]{1,0:T(8,128)(2,1)}) async-done(((bf16[768,3200]{1,0:T(8,128)(2,1)}, bf16[768,3200]{1,0:T(8,128)(2,1)}), (bf16[768,3200]{1,0:T(8,128)(2,1)}, bf16[768,3200]{1,0:T(8,128)(2,1)})) %all-reduce.6.cloned.1.call-update) | async-done | bytes 9830416
  677.1 125.4 %reduce-scatter.5.cloned.1.call-done = bf16[96,4608]{1,0:T(8,128)(2,1)} async-done(((bf16[768,4608]{1,0:T(8,128)(2,1)}), bf16[96,4608]{1,0:T(8,128)(2,1)}) %reduce-scatter.5.cloned.1.call-update) | async-done | bytes 884752 | tf_op jit(solution)/shard_map/reduce_scatter | solution.py:388
  802.4 2.4 reshape.40
  804.8 1.4 fusion.14
  806.4 127.6 %reduce-scatter.3.cloned.1.call-done = bf16[96,4608]{1,0:T(8,128)(2,1)} async-done(((bf16[768,4608]{1,0:T(8,128)(2,1)}), bf16[96,4608]{1,0:T(8,128)(2,1)}) %reduce-scatter.3.cloned.1.call-update) | async-done | bytes 884752 | tf_op jit(solution)/shard_map/reduce_scatter | solution.py:388
  934.0 2.4 reshape.39
  936.4 1.4 fusion.13
  938.0 1.3 pad_maximum_fusion
  939.3 1.3 pad_maximum_fusion.1
  (139 shorter events, 36.3 us)
Async XLA Ops:
  7.2 9.2 copy-start.9
  7.2 93.7 %all-gather.4.cloned.1.call-start = ((), (), s32[]{:S(2)}) async-start(), calls=%async_computation.2 | async-start | bytes 9934848 | tf_op jit(solution)/shard_map/all_gather | solution.py:322
  15.1 196.0 %all-gather.6.cloned.1.call-start = ((), (), s32[]{:S(2)}) async-start(), calls=%async_computation.3 | async-start | bytes 7962624 | tf_op jit(solution)/shard_map/all_gather | solution.py:332
  17.5 1.2 copy-start.23
  17.5 1.2 copy-start.25
  17.5 1.5 copy-start.24
  17.5 302.7 %all-gather.8.cloned.1.call-start = ((), (), s32[]{:S(2)}) async-start(), calls=%async_computation.4 | async-start | bytes 7962624 | tf_op jit(solution)/shard_map/all_gather | solution.py:332
  18.6 650.7 %all-reduce.6.cloned.1.call-start = ((), (), s32[]{:S(2)}) async-start(), calls=%async_computation.7 | async-start | bytes 19660800
  125.1 17.3 %collective-permute-start.1 = (bf16[432,768]{1,0:T(8,128)(2,1)}, bf16[432,768]{1,0:T(8,128)(2,1)S(1)}, u32[]{:S(2)}, u32[]{:S(2)}) collective-permute-start(bf16[432,768]{1,0:T(8,128)(2,1)} %get-tuple-element.49.refs_0_.refs_4_), channel_id=1, source_target_pairs={{0,2},{1,3},{2,0},{3,1},{4,6},{5,7},{6,4},{7,5},{8,10},{9,11},{10,... | collective-permute-start | bytes 1990664 | tf_op jit(solution)/shard_map/ppermute | solution.py:270
  126.5 84.5 %collective-permute-start = (bf16[432,768]{1,0:T(8,128)(2,1)}, bf16[432,768]{1,0:T(8,128)(2,1)S(1)}, u32[]{:S(2)}, u32[]{:S(2)}) collective-permute-start(bf16[432,768]{1,0:T(8,128)(2,1)} %get-tuple-element.49.refs_0_.refs_4_), channel_id=1, source_target_pairs={{0,1},{1,0},{2,3},{3,2},{4,5},{5,4},{6,7},{7,6},{8,9},{9,8},{10,11... | collective-permute-start | bytes 1990664 | tf_op jit(solution)/shard_map/ppermute | solution.py:270
  142.4 68.7 %copy-start.3 = (bf16[432,768]{1,0:T(8,128)(2,1)}, bf16[432,768]{1,0:T(8,128)(2,1)S(1)}, u32[]{:S(2)}) copy-start(bf16[432,768]{1,0:T(8,128)(2,1)S(1)} %collective-permute-done.1.refs_2_.refs_6_) | copy-start | bytes 1990660
  142.4 68.7 %collective-permute-start.2 = (bf16[432,768]{1,0:T(8,128)(2,1)S(1)}, bf16[432,768]{1,0:T(8,128)(2,1)S(1)}, u32[]{:S(2)}, u32[]{:S(2)}) collective-permute-start(bf16[432,768]{1,0:T(8,128)(2,1)S(1)} %collective-permute-done.1.refs_2_.refs_6_), channel_id=1, source_target_pairs={{0,1},{1,0},{2,3},{3,2},{4,5},{5,4},{6,7},{7,6},{8,9},{9,8},{10,11... | collective-permute-start | bytes 1990664 | tf_op jit(solution)/shard_map/ppermute | solution.py:270
  223.5 5.7 copy-start.19
  223.5 2.4 collective-permute-start.4
  223.6 5.6 collective-permute-start.3
  227.2 17.0 %collective-permute-start.5 = (bf16[432,768]{1,0:T(8,128)(2,1)S(1)}, bf16[432,768]{1,0:T(8,128)(2,1)S(1)}, u32[]{:S(2)}, u32[]{:S(2)}) collective-permute-start(bf16[432,768]{1,0:T(8,128)(2,1)S(1)} %add_convert_fusion.6), channel_id=1, source_target_pairs={{0,2},{1,3},{2,0},{3,1},{4,6},{5,7},{6,4},{7,5},{8,10},{9,11},{10,... | collective-permute-start | bytes 1990664 | tf_op jit(solution)/shard_map/ppermute | solution.py:270
  245.0 16.4 %copy-start = (f32[384,768]{1,0:T(8,128)S(1)}, f32[384,768]{1,0:T(8,128)}, u32[]{:S(2)}) copy-start(f32[384,768]{1,0:T(8,128)} %refs_2_.1) | copy-start | bytes 3538948
  260.2 2.8 copy-start.6
  260.2 18.1 %collective-permute-start.7 = (bf16[432,768]{1,0:T(8,128)(2,1)}, bf16[432,768]{1,0:T(8,128)(2,1)S(1)}, u32[]{:S(2)}, u32[]{:S(2)}) collective-permute-start(bf16[432,768]{1,0:T(8,128)(2,1)} %get-tuple-element.55.refs_0_.refs_4_), channel_id=1, source_target_pairs={{0,2},{1,3},{2,0},{3,1},{4,6},{5,7},{6,4},{7,5},{8,10},{9,11},{10,... | collective-permute-start | bytes 1990664 | tf_op jit(solution)/shard_map/ppermute | solution.py:270
  262.1 69.1 %copy-start.2 = (bf16[432,768]{1,0:T(8,128)(2,1)}, bf16[432,768]{1,0:T(8,128)(2,1)S(1)}, u32[]{:S(2)}) copy-start(bf16[432,768]{1,0:T(8,128)(2,1)S(1)} %convolution_convert_fusion.refs_0_) | copy-start | bytes 1990660
  262.1 28.7 %collective-permute-start.13 = (bf16[432,768]{1,0:T(8,128)(2,1)S(1)}, bf16[432,768]{1,0:T(8,128)(2,1)S(1)}, u32[]{:S(2)}, u32[]{:S(2)}) collective-permute-start(bf16[432,768]{1,0:T(8,128)(2,1)S(1)} %convolution_convert_fusion.refs_0_), channel_id=1, source_target_pairs={{0,2},{1,3},{2,0},{3,1},{4,6},{5,7},{6,4},{7,5},{8,10},{9,11},{10,... | collective-permute-start | bytes 1990664 | tf_op jit(solution)/shard_map/ppermute | solution.py:270
  262.9 57.3 %collective-permute-start.6 = (bf16[432,768]{1,0:T(8,128)(2,1)S(1)}, bf16[432,768]{1,0:T(8,128)(2,1)S(1)}, u32[]{:S(2)}, u32[]{:S(2)}) collective-permute-start(bf16[432,768]{1,0:T(8,128)(2,1)S(1)} %copy-done.6), channel_id=1, source_target_pairs={{0,1},{1,0},{2,3},{3,2},{4,5},{5,4},{6,7},{7,6},{8,9},{9,8},{10,11... | collective-permute-start | bytes 1990664 | tf_op jit(solution)/shard_map/ppermute | solution.py:270
  278.2 42.1 %copy-start.7 = (bf16[432,768]{1,0:T(8,128)(2,1)}, bf16[432,768]{1,0:T(8,128)(2,1)S(1)}, u32[]{:S(2)}) copy-start(bf16[432,768]{1,0:T(8,128)(2,1)S(1)} %collective-permute-done.7.refs_2_.refs_6_) | copy-start | bytes 1990660
  278.2 42.1 %collective-permute-start.8 = (bf16[432,768]{1,0:T(8,128)(2,1)S(1)}, bf16[432,768]{1,0:T(8,128)(2,1)}, u32[]{:S(2)}, u32[]{:S(2)}) collective-permute-start(bf16[432,768]{1,0:T(8,128)(2,1)S(1)} %collective-permute-done.7.refs_2_.refs_6_), channel_id=1, source_target_pairs={{0,1},{1,0},{2,3},{3,2},{4,5},{5,4},{6,7},{7,6},{8,9},{9,8},{10,11... | collective-permute-start | bytes 1990664 | tf_op jit(solution)/shard_map/ppermute | solution.py:270
  278.2 53.0 %collective-permute-start.12 = (bf16[432,768]{1,0:T(8,128)(2,1)S(1)}, bf16[432,768]{1,0:T(8,128)(2,1)}, u32[]{:S(2)}, u32[]{:S(2)}) collective-permute-start(bf16[432,768]{1,0:T(8,128)(2,1)S(1)} %convolution_convert_fusion.refs_0_), channel_id=1, source_target_pairs={{0,1},{1,0},{2,3},{3,2},{4,5},{5,4},{6,7},{7,6},{8,9},{9,8},{10,11... | collective-permute-start | bytes 1990664 | tf_op jit(solution)/shard_map/ppermute | solution.py:270
  290.8 40.5 %copy-start.10 = (bf16[432,768]{1,0:T(8,128)(2,1)}, bf16[432,768]{1,0:T(8,128)(2,1)S(1)}, u32[]{:S(2)}) copy-start(bf16[432,768]{1,0:T(8,128)(2,1)S(1)} %collective-permute-done.13.refs_2_) | copy-start | bytes 1990660
  290.8 40.4 %collective-permute-start.14 = (bf16[432,768]{1,0:T(8,128)(2,1)S(1)}, bf16[432,768]{1,0:T(8,128)(2,1)}, u32[]{:S(2)}, u32[]{:S(2)}) collective-permute-start(bf16[432,768]{1,0:T(8,128)(2,1)S(1)} %collective-permute-done.13.refs_2_), channel_id=1, source_target_pairs={{0,1},{1,0},{2,3},{3,2},{4,5},{5,4},{6,7},{7,6},{8,9},{9,8},{10,11... | collective-permute-start | bytes 1990664 | tf_op jit(solution)/shard_map/ppermute | solution.py:270
  346.9 5.2 copy-start.17
  346.9 2.4 collective-permute-start.16
  347.0 5.1 collective-permute-start.15
  350.5 17.0 %collective-permute-start.17 = (bf16[432,768]{1,0:T(8,128)(2,1)S(1)}, bf16[432,768]{1,0:T(8,128)(2,1)S(1)}, u32[]{:S(2)}, u32[]{:S(2)}) collective-permute-start(bf16[432,768]{1,0:T(8,128)(2,1)S(1)} %add_convert_fusion.2), channel_id=1, source_target_pairs={{0,2},{1,3},{2,0},{3,1},{4,6},{5,7},{6,4},{7,5},{8,10},{9,11},{10,... | collective-permute-start | bytes 1990664 | tf_op jit(solution)/shard_map/ppermute | solution.py:270
  391.9 16.3 %collective-permute-start.19 = (bf16[432,768]{1,0:T(8,128)(2,1)}, bf16[432,768]{1,0:T(8,128)(2,1)S(1)}, u32[]{:S(2)}, u32[]{:S(2)}) collective-permute-start(bf16[432,768]{1,0:T(8,128)(2,1)} %get-tuple-element.70.refs_0_), channel_id=1, source_target_pairs={{0,2},{1,3},{2,0},{3,1},{4,6},{5,7},{6,4},{7,5},{8,10},{9,11},{10,... | collective-permute-start | bytes 1990664 | tf_op jit(solution)/shard_map/ppermute | solution.py:270
  393.3 14.9 %collective-permute-start.18 = (bf16[432,768]{1,0:T(8,128)(2,1)}, bf16[432,768]{1,0:T(8,128)(2,1)S(1)}, u32[]{:S(2)}, u32[]{:S(2)}) collective-permute-start(bf16[432,768]{1,0:T(8,128)(2,1)} %get-tuple-element.70.refs_0_), channel_id=1, source_target_pairs={{0,1},{1,0},{2,3},{3,2},{4,5},{5,4},{6,7},{7,6},{8,9},{9,8},{10,11... | collective-permute-start | bytes 1990664 | tf_op jit(solution)/shard_map/ppermute | solution.py:270
  408.2 2.1 copy-start.11
  408.2 2.1 collective-permute-start.20
  408.2 2.1 copy-start.12
  426.8 5.2 copy-start.18
  426.9 2.4 collective-permute-start.22
  427.1 4.9 collective-permute-start.21
  430.5 17.0 %collective-permute-start.23 = (bf16[432,768]{1,0:T(8,128)(2,1)S(1)}, bf16[432,768]{1,0:T(8,128)(2,1)S(1)}, u32[]{:S(2)}, u32[]{:S(2)}) collective-permute-start(bf16[432,768]{1,0:T(8,128)(2,1)S(1)} %add_convert_fusion), channel_id=1, source_target_pairs={{0,2},{1,3},{2,0},{3,1},{4,6},{5,7},{6,4},{7,5},{8,10},{9,11},{10,... | collective-permute-start | bytes 1990664 | tf_op jit(solution)/shard_map/ppermute | solution.py:270
  471.0 331.4 %reduce-scatter.5.cloned.1.call-start = ((), (), s32[]{:S(2)}) async-start(), calls=%async_computation.6 | async-start | bytes 7962624 | tf_op jit(solution)/shard_map/reduce_scatter | solution.py:388
  471.6 462.4 %reduce-scatter.3.cloned.1.call-start = ((), (), s32[]{:S(2)}) async-start(), calls=%async_computation.5 | async-start | bytes 7962624 | tf_op jit(solution)/shard_map/reduce_scatter | solution.py:388
  471.9 3.2 copy-start.16
  472.9 2.1 collective-permute-start.10
  475.1 32.3 %copy-start.1 = (f32[384,768]{1,0:T(8,128)S(1)}, f32[384,768]{1,0:T(8,128)}, u32[]{:S(2)}) copy-start(f32[384,768]{1,0:T(8,128)} %get-tuple-element.54.refs_3_) | copy-start | bytes 3538948
  475.1 32.4 %copy-start.20 = (bf16[432,768]{1,0:T(8,128)(2,1)S(1)}, bf16[432,768]{1,0:T(8,128)(2,1)}, u32[]{:S(2)}) copy-start(bf16[432,768]{1,0:T(8,128)(2,1)} %get-tuple-element.56) | copy-start | bytes 1990660
  475.2 31.6 %collective-permute-start.11 = (bf16[432,768]{1,0:T(8,128)(2,1)S(1)}, bf16[432,768]{1,0:T(8,128)(2,1)S(1)}, u32[]{:S(2)}, u32[]{:S(2)}) collective-permute-start(bf16[432,768]{1,0:T(8,128)(2,1)S(1)} %add_convert_fusion.4), channel_id=1, source_target_pairs={{0,2},{1,3},{2,0},{3,1},{4,6},{5,7},{6,4},{7,5},{8,10},{9,11},{10,... | collective-permute-start | bytes 1990664 | tf_op jit(solution)/shard_map/ppermute | solution.py:270
  476.7 30.7 %collective-permute-start.9 = (bf16[432,768]{1,0:T(8,128)(2,1)}, bf16[432,768]{1,0:T(8,128)(2,1)}, u32[]{:S(2)}, u32[]{:S(2)}) collective-permute-start(bf16[432,768]{1,0:T(8,128)(2,1)} %get-tuple-element.57), channel_id=1, source_target_pairs={{0,1},{1,0},{2,3},{3,2},{4,5},{5,4},{6,7},{7,6},{8,9},{9,8},{10,11... | collective-permute-start | bytes 1990664 | tf_op jit(solution)/shard_map/ppermute | solution.py:270
  (9 other events, 7.8 us)
Sparse Core Ops, SparseCore 0:
  15.2 85.6 all-gather.3
  103.6 107.3 all-gather.5
  213.2 106.9 all-gather.7
  471.2 198.1 all-reduce.5
  673.3 129.0 reduce-scatter.4
  805.9 128.0 reduce-scatter.2

commit v2 on v1

--- a/solution.py
+++ b/solution.py
@@ -18,6 +18,7 @@
 epsilon = 1e-05
 score_scale = 0.125
 FAR = -1e30
+RING_MOST = 8
 VMEM_BYTES = 56 << 20
 f32 = jnp.float32
 bf16 = jnp.bfloat16
@@ -49,32 +50,59 @@
     return rate * (scaled_grad - first - unit * second)
 
 
-def whole_call(body, out_shape, scratch_shapes=(), name=None):
+def cost(micros):
+    return pl.CostEstimate(
+        flops=micros * 10**5, transcendentals=0, bytes_accessed=micros * 10**2
+    )
+
+
+def whole_call(body, out_shape, scratch_shapes=(), name=None, micros=15):
     return pl.pallas_call(
         body,
         out_shape=out_shape,
         scratch_shapes=scratch_shapes,
         compiler_params=pltpu.CompilerParams(vmem_limit_bytes=VMEM_BYTES),
+        cost_estimate=cost(micros),
         name=name,
     )
+
+
+def pack_body(*refs):
+    weight_refs, gain_refs, out_refs = refs[:4], refs[4:6], refs[6:]
+    rows, width = weight_refs[0].shape[1:]
+    lane = lax.broadcasted_iota(jnp.int32, (rows, PAIR), 1)
+    diagonal = lax.broadcasted_iota(jnp.int32, (rows, rows), 0) == lax.broadcasted_iota(
+        jnp.int32, (rows, rows), 1
+    )
+    for layer, out_ref in enumerate(out_refs):
+        for place, weight_ref in enumerate(weight_refs):
+            out_ref[:, place * width : (place + 1) * width] = weight_ref[layer]
+        columns = [
+            jnp.sum(jnp.where(diagonal, ref[layer : layer + 1, :].astype(f32), 0.0), 1, keepdims=True)
+            for ref in gain_refs
+        ]
+        out_ref[:, 4 * width :] = jnp.where(
+            lane == 0, columns[0], jnp.where(lane == 1, columns[1], 0.0)
+        ).astype(bf16)
 
 
 def attend_forward_body(first, *refs):
     if first:
-        rows_ref, spot_ref, bias_ref, gain_ref, weight_ref = refs[:5]
-        outs = refs[5:]
+        rows_ref, spot_ref, bias_ref, weight_ref = refs[:4]
+        outs = refs[4:]
         rows = rows_ref[...].astype(f32)
     else:
-        rows_ref, part_a_ref, part_b_ref, spot_ref, bias_ref, gain_ref, weight_ref = refs[:7]
-        outs = refs[7:]
+        rows_ref, part_a_ref, part_b_ref, spot_ref, bias_ref, weight_ref = refs[:6]
+        outs = refs[6:]
         spot = spot_ref[...]
         rows = rows_ref[...] + mat(spot, part_a_ref[...]) + mat(spot, part_b_ref[...])
     width = rows.shape[1]
+    gains = weight_ref[:, 4 * width :].astype(f32).T
     triple_ref, logs_ref, context_ref, hidden_ref, slots_ref = outs[:5]
     if not first:
         outs[5][...] = rows
     unit, _ = norm_parts(rows)
-    normed = (unit * gain_ref[0:1, :]).astype(bf16)
+    normed = (unit * gains[0:1, :]).astype(bf16)
     triple_ref[...] = mat(normed, weight_ref[:, : 3 * width]).astype(bf16)
     row_count = rows.shape[0]
     lane = lax.broadcasted_iota(jnp.int32, (row_count, PAIR), 1)
@@ -102,10 +130,10 @@
         return carry
 
     lax.fori_loop(0, HEADS // 2, one_pair, 0)
-    hidden = rows + mat(context_ref[...], weight_ref[:, 3 * width :])
+    hidden = rows + mat(context_ref[...], weight_ref[:, 3 * width : 4 * width])
     hidden_ref[...] = hidden
     unit, _ = norm_parts(hidden)
-    second = (unit * gain_ref[1:2, :]).astype(bf16)
+    second = (unit * gains[1:2, :]).astype(bf16)
     slots_ref[...] = contract_rows(spot_ref[...], second).astype(bf16)
 
 
@@ -121,24 +149,29 @@
         context_ref,
         spot_ref,
         bias_ref,
-        gain_ref,
         weight_ref,
-    ) = refs[:12]
+    ) = refs[:11]
+    slots_ref = None
     if last:
-        grad_out_ref, weight_grad_ref, context_grad_ref, triple_grad_ref = refs[12:]
-        slots_ref = None
+        grad_out_ref, first_grad_ref, second_grad_ref, context_grad_ref, triple_grad_ref = refs[11:]
     else:
-        grad_out_ref, weight_grad_ref, slots_ref, context_grad_ref, triple_grad_ref = refs[12:]
+        grad_out_ref, first_grad_ref, slots_ref, context_grad_ref, triple_grad_ref = refs[11:]
+    width = rows_ref.shape[1]
+    gains = weight_ref[:, 4 * width :].astype(f32).T
     spot = spot_ref[...]
     second_grad = mat(spot, part_a_ref[...]) + mat(spot, part_b_ref[...])
     unit, rate = norm_parts(hidden_ref[...])
     second_gain_grad = jnp.sum(second_grad * unit, 0, keepdims=True)
-    hidden_grad = grad_ref[...] + norm_back(unit, rate, second_grad * gain_ref[1:2, :])
+    hidden_grad = grad_ref[...] + norm_back(unit, rate, second_grad * gains[1:2, :])
     row_count, width = hidden_grad.shape
     grad_out_ref[...] = hidden_grad
     branch = hidden_grad.astype(bf16)
-    context_grad_ref[...] = contract_cols(branch, weight_ref[:, 3 * width :]).astype(bf16)
-    weight_grad_ref[:, 3 * width : 4 * width] = contract_rows(context_ref[...], branch).astype(bf16)
+    context_grad_ref[...] = contract_cols(branch, weight_ref[:, 3 * width : 4 * width]).astype(bf16)
+    output_grad = contract_rows(context_ref[...], branch).astype(bf16)
+    if last:
+        second_grad_ref[:, width : 2 * width] = output_grad
+    else:
+        first_grad_ref[:, 3 * width : 4 * width] = output_grad
     lane = lax.broadcasted_iota(jnp.int32, (row_count, PAIR), 1)
 
     def one_pair(pair, carry):
@@ -177,12 +210,16 @@
 
     lax.fori_loop(0, HEADS // 2, one_pair, 0)
     unit, rate = norm_parts(rows_ref[...].astype(f32))
-    normed = (unit * gain_ref[0:1, :]).astype(bf16)
+    normed = (unit * gains[0:1, :]).astype(bf16)
     triple_grad = triple_grad_ref[...]
-    weight_grad_ref[:, : 3 * width] = contract_rows(normed, triple_grad).astype(bf16)
+    if last:
+        first_grad_ref[...] = contract_rows(normed, triple_grad[:, : 2 * width]).astype(bf16)
+        second_grad_ref[:, :width] = contract_rows(normed, triple_grad[:, 2 * width :]).astype(bf16)
+    else:
+        first_grad_ref[:, : 3 * width] = contract_rows(normed, triple_grad).astype(bf16)
     normed_grad = contract_cols(triple_grad, weight_ref[:, : 3 * width])
     first_gain_grad = jnp.sum(normed_grad * unit, 0, keepdims=True)
-    out_grad = grad_out_ref[...] + norm_back(unit, rate, normed_grad * gain_ref[0:1, :])
+    out_grad = grad_out_ref[...] + norm_back(unit, rate, normed_grad * gains[0:1, :])
     grad_out_ref[...] = out_grad
     if slots_ref is not None:
         slots_ref[...] = contract_rows(spot, out_grad.astype(bf16)).astype(bf16)
@@ -190,7 +227,10 @@
     gain_rows = jnp.where(
         which == 0, first_gain_grad, jnp.where(which == 1, second_gain_grad, 0.0)
     )
-    weight_grad_ref[:, 4 * width :] = gain_rows.T.astype(bf16)
+    if last:
+        second_grad_ref[:, 2 * width :] = gain_rows.T.astype(bf16)
+    else:
+        first_grad_ref[:, 4 * width :] = gain_rows.T.astype(bf16)
 
 
 def expert_forward_body(*refs):
@@ -212,10 +252,12 @@
         out_refs[2 * half + 1][...] = sums[MOST:]
 
 
-def expert_backward_body(*refs):
+def expert_backward_body(split, *refs):
+    if split:
+        place_ref, *refs = refs
     grad_refs, block_refs = refs[:4], refs[4:8]
     active_ref, slope_ref, weight_ref = refs[8:11]
-    out_refs, weight_grad_ref = refs[11:15], refs[15]
+    out_refs = refs[11:15]
     units = weight_ref.shape[1] // 2
     grads = jnp.concatenate([ref[...] for ref in grad_refs], 0)
     rows = jnp.concatenate([ref[...] for ref in block_refs], 0)
@@ -224,8 +266,27 @@
     sums = contract_cols(before_grad, weight_ref[:, :units]).astype(bf16)
     for place in range(4):
         out_refs[place][...] = sums[place * MOST : (place + 1) * MOST]
-    weight_grad_ref[:, :units] = contract_rows(rows, before_grad).astype(bf16)
-    weight_grad_ref[:, units:] = contract_rows(grads, active_ref[...]).astype(bf16)
+    pieces = ((rows, before_grad, 0), (grads, active_ref[...], units))
+    if not split:
+        for left, right, start in pieces:
+            refs[15][:, start : start + units] = contract_rows(left, right).astype(bf16)
+        return
+    ring, mine = place_ref[0], place_ref[1]
+    outer, count = refs[15].shape[:2]
+    for left, right, start in pieces:
+        grad = contract_rows(left, right).astype(bf16)
+        for expert in range(EXPERTS):
+            kept_ref, sent_ref = refs[15 + 2 * expert], refs[16 + 2 * expert]
+            for half in range(2):
+
+                @pl.when((pl.program_id(0) == expert) & (mine == half))
+                def _():
+                    for block in range(outer):
+                        at = lax.rem(block - ring + outer, outer)
+                        low = (2 * block + half) * count
+                        high = (2 * block + 1 - half) * count
+                        kept_ref[at, :, start : start + units] = grad[low : low + count]
+                        sent_ref[at, :, start : start + units] = grad[high : high + count]
 
 
 def expert_forward(blocks, weights):
@@ -241,28 +302,45 @@
         out_shape=[jax.ShapeDtypeStruct((SLOTS, width), bf16)] * 4
         + [jax.ShapeDtypeStruct((4 * SLOTS, units), bf16)] * 2,
         compiler_params=pltpu.CompilerParams(vmem_limit_bytes=VMEM_BYTES),
+        cost_estimate=cost(10),
         name="expert_forward",
     )(*blocks, weights)
     return outs[:4], outs[4], outs[5]
 
 
-def expert_backward(grads, blocks, active, slope, weights):
+def expert_backward(grads, blocks, active, slope, weights, split):
     width = blocks[0].shape[1]
     units = weights.shape[1] // (2 * EXPERTS)
-    block = pl.BlockSpec((MOST, width), lambda e: (e, 0))
-    kept = pl.BlockSpec((4 * MOST, units), lambda e: (e, 0))
-    square = pl.BlockSpec((width, 2 * units), lambda e: (0, e))
+    block = pl.BlockSpec((MOST, width), lambda e, *_: (e, 0))
+    kept = pl.BlockSpec((4 * MOST, units), lambda e, *_: (e, 0))
+    square = pl.BlockSpec((width, 2 * units), lambda e, *_: (0, e))
+    out_specs = [block] * 4
+    out_shape = [jax.ShapeDtypeStruct((SLOTS, width), bf16)] * 4
+    places = []
+    if split:
+        count = lax.axis_size("dp")
+        me = lax.axis_index("dp")
+        places = [jnp.stack([me // 2, lax.rem(me, 2)]).astype(jnp.int32)]
+        shape = (count // 2, width // count, 2 * units)
+        out_specs += [pl.BlockSpec(shape, lambda e, *_: (0, 0, 0))] * (2 * EXPERTS)
+        out_shape += [jax.ShapeDtypeStruct(shape, bf16)] * (2 * EXPERTS)
+    else:
+        out_specs += [square]
+        out_shape += [jax.ShapeDtypeStruct(weights.shape, bf16)]
     outs = pl.pallas_call(
-        expert_backward_body,
-        grid=(EXPERTS,),
-        in_specs=[block] * 8 + [kept] * 2 + [square],
-        out_specs=[block] * 4 + [square],
-        out_shape=[jax.ShapeDtypeStruct((SLOTS, width), bf16)] * 4
-        + [jax.ShapeDtypeStruct(weights.shape, bf16)],
+        partial(expert_backward_body, split),
+        grid_spec=pltpu.PrefetchScalarGridSpec(
+            num_scalar_prefetch=len(places),
+            grid=(EXPERTS,),
+            in_specs=[block] * 8 + [kept] * 2 + [square],
+            out_specs=out_specs,
+        ),
+        out_shape=out_shape,
         compiler_params=pltpu.CompilerParams(vmem_limit_bytes=VMEM_BYTES),
+        cost_estimate=cost(16),
         name="expert_backward",
-    )(*grads, *blocks, active, slope, weights)
-    return outs[:4], outs[4]
+    )(*places, *grads, *blocks, active, slope, weights)
+    return outs[:4], outs[4:]
 
 
 def swap(values, flip):
@@ -285,6 +363,131 @@
     far_in = swap(far, 2)
     near = (own.astype(f32) + beside_in.astype(f32)).astype(bf16)
     return near, far_in
+
+
+def pair_perm(count):
+    return [(i, i ^ 1) for i in range(count)]
+
+
+def ring_perm(count):
+    return [(i, (i + 2) % count) for i in range(count)]
+
+
+def gather_rows(shard, line_done, pair_done):
+    count = lax.axis_size("dp")
+    if count > RING_MOST:
+        return lax.all_gather(shard, "dp", axis=0, tiled=True)
+    me = lax.axis_index("dp")
+    rows, cols = shard.shape
+    full = jnp.zeros((count * rows, cols), shard.dtype)
+    moving, _ = tie(shard, line_done)
+    for step in range(count // 2):
+        source = lax.rem(me - 2 * step + count, count)
+        mate, _ = tie(moving, pair_done) if step == 0 else (moving, None)
+        mate = lax.ppermute(mate, "dp", pair_perm(count))
+        full = lax.dynamic_update_slice(full, moving, (source * rows, 0))
+        full = lax.dynamic_update_slice(full, mate, ((source ^ 1) * rows, 0))
+        if step + 1 < count // 2:
+            moving = lax.ppermute(moving, "dp", ring_perm(count))
+    return full
+
+
+def tie(*values):
+    return lax.optimization_barrier(values)
+
+
+def add(left, right):
+    return left.astype(f32) + right.astype(f32)
+
+
+def pick(values, at, axis):
+    return lax.dynamic_index_in_dim(values, at, axis, keepdims=False)
+
+
+def put(values, piece, at, axis):
+    return lax.dynamic_update_index_in_dim(values, piece, at, axis)
+
+
+def shift_perm(count, step):
+    return [(i, (i + 2 * step) % count) for i in range(count)]
+
+
+def gather_attention(shard):
+    count, sides = lax.axis_size("dp"), lax.axis_size("expert")
+    if count > RING_MOST:
+        return lax.all_gather(shard, ("dp", "expert"), axis=0, tiled=True), None, None
+    rows, cols = shard.shape
+    outer = count // 2
+    me, side = lax.axis_index("dp"), lax.axis_index("expert")
+    line = me // 2
+    quad = put(jnp.zeros((outer, rows, cols), shard.dtype), shard, line, 0)
+    for step in range(1, outer):
+        got = lax.ppermute(shard, "dp", shift_perm(count, step))
+        quad = put(quad, got, lax.rem(line - step + outer, outer), 0)
+    mate = lax.ppermute(quad, "dp", pair_perm(count))
+    both = jnp.zeros((outer, 2, rows, cols), shard.dtype)
+    both = put(put(both, quad, lax.rem(me, 2), 1), mate, 1 - lax.rem(me, 2), 1)
+    across = swap(both, 2)
+    full = jnp.zeros((outer, 2, sides, rows, cols), shard.dtype)
+    full = put(full, both, side, 2)
+    full = put(full, swap(both, 1), side ^ 1, 2)
+    full = put(full, across, side ^ 2, 2)
+    full = put(full, swap(across, 1), side ^ 3, 2)
+    return full.reshape(-1, cols), got, mate
+
+
+def reduce_pairs(kept, got):
+    count = lax.axis_size("dp")
+    outer = count // 2
+    total = add(kept[0], got[0])
+    for step in range(1, outer):
+        sent = add(kept[step], got[step]).astype(bf16)
+        total = total + lax.ppermute(sent, "dp", shift_perm(count, step)).astype(f32)
+    return total
+
+
+def halve_core(blocks, axis):
+    core = lax.rem(lax.axis_index("expert"), 2)
+    got = swap(pick(blocks, 1 - core, axis), 1)
+    return add(pick(blocks, core, axis), got).astype(bf16)
+
+
+def halve_line(blocks, axis):
+    line = lax.axis_index("expert") // 2
+    got = swap(pick(blocks, 1 - line, axis), 2)
+    return add(pick(blocks, line, axis), got).astype(bf16)
+
+
+def halve_pair(blocks, axis):
+    mine = lax.rem(lax.axis_index("dp"), 2)
+    got = lax.ppermute(pick(blocks, 1 - mine, axis), "dp", pair_perm(lax.axis_size("dp")))
+    return add(pick(blocks, mine, axis), got).astype(bf16)
+
+
+def reduce_line(blocks):
+    count = lax.axis_size("dp")
+    outer = count // 2
+    line = lax.axis_index("dp") // 2
+    total = pick(blocks, line, 0).astype(f32)
+    for step in range(1, outer):
+        sent = pick(blocks, lax.rem(line + step, outer), 0)
+        total = total + lax.ppermute(sent, "dp", shift_perm(count, step)).astype(f32)
+    return total
+
+
+def reduce_attention(values, pair_first, after=None):
+    dp, sides = lax.axis_size("dp"), lax.axis_size("expert")
+    cols = values.shape[1]
+    if dp > RING_MOST:
+        return lax.psum_scatter(values, ("dp", "expert"), scatter_dimension=0, tiled=True).astype(f32)
+    blocks = halve_core(values.reshape(dp // 2, 2, sides // 2, 2, -1, cols), 3)
+    if after is not None:
+        blocks, _ = tie(blocks, after)
+    if pair_first:
+        blocks = halve_line(halve_pair(blocks, 1), 1)
+    else:
+        blocks = halve_pair(halve_line(blocks, 2), 1)
+    return reduce_line(blocks)
 
 
 def on_device(
@@ -308,19 +511,11 @@
     shard_rows = expert_in.shape[2]
     own_rows = query_weight.shape[1]
 
-    gains = jnp.stack([norm_first[0], norm_second[0], norm_first[1], norm_second[1]], 1)
-    gains = jnp.pad(gains, ((0, 0), (0, PAIR - gains.shape[1])))
-    attention_shard = jnp.concatenate(
-        [
-            weight[layer]
-            for layer in range(LAYERS)
-            for weight in (query_weight, key_weight, value_weight, output_weight)
-        ]
-        + [gains],
-        1,
-    )
-    attention_all = lax.all_gather(attention_shard, both, axis=0, tiled=True)
-    gain_rows = attention_all[:, 4 * LAYERS * width :].T.astype(f32)
+    attention_shards = whole_call(
+        pack_body,
+        [jax.ShapeDtypeStruct((own_rows, 4 * width + PAIR), bf16)] * LAYERS,
+        name="pack_attention",
+    )(query_weight, key_weight, value_weight, output_weight, norm_first, norm_second)
 
     def expert_shard(layer):
         pieces = jnp.concatenate(
@@ -328,8 +523,14 @@
         )
         return jnp.transpose(pieces, (1, 0, 2)).reshape(shard_rows, EXPERTS * 2 * units)
 
+    attention_first, line_done, pair_done = gather_attention(attention_shards[0])
+    attention_all = [
+        attention_first,
+        lax.all_gather(attention_shards[1], both, axis=0, tiled=True),
+    ]
     experts_all = [
-        lax.all_gather(expert_shard(layer), "dp", axis=0, tiled=True) for layer in range(LAYERS)
+        gather_rows(expert_shard(0), line_done, pair_done),
+        lax.all_gather(expert_shard(1), "dp", axis=0, tiled=True),
     ]
 
     route = routes[:, 0]
@@ -353,8 +554,7 @@
     parts = None
     for layer in range(LAYERS):
         first = layer == 0
-        weight = attention_all[:, 4 * layer * width : 4 * (layer + 1) * width]
-        gain = gain_rows[2 * layer : 2 * layer + 2]
+        weight = attention_all[layer]
         outs = whole_call(
             partial(attend_forward_body, first),
             [
@@ -366,48 +566,53 @@
             ]
             + ([] if first else [shape_of(row_count, width, f32)]),
             name="attend_forward",
-        )(*([rows] if first else [rows, *parts]), spot, bias, gain, weight)
+        )(*([rows] if first else [rows, *parts]), spot, bias, weight)
         triple, logs, context, hidden, slots = outs[:5]
         inputs = tokens if first else outs[5]
         blocks = spread_slots(slots)
         sums, active, slope = expert_forward(blocks, experts_all[layer])
         parts = collect_slots(sums)
         rows = hidden
-        saved.append((inputs, triple, logs, context, hidden, blocks, active, slope, weight, gain))
+        saved.append((inputs, triple, logs, context, hidden, blocks, active, slope, weight))
     mixed = (rows + mat(spot, parts[0]) + mat(spot, parts[1])).astype(bf16)
 
     grad = cotangent
     grad_blocks = last_grads
     results = [None] * LAYERS
     for layer in reversed(range(LAYERS)):
-        inputs, triple, logs, context, hidden, blocks, active, slope, weight, gain = saved[layer]
+        inputs, triple, logs, context, hidden, blocks, active, slope, weight = saved[layer]
         last = layer == 0
-        sums, expert_grad = expert_backward(
-            grad_blocks, blocks, active, slope, experts_all[layer]
+        sums, expert_grads = expert_backward(
+            grad_blocks, blocks, active, slope, experts_all[layer], False
         )
-        expert_total = lax.psum_scatter(expert_grad, "dp", scatter_dimension=0, tiled=True)
+        total = lax.psum_scatter(expert_grads[0], "dp", scatter_dimension=0, tiled=True)
+        total = total.astype(f32).reshape(shard_rows, EXPERTS, 2 * units)
+        expert_totals = [total[:, expert] for expert in range(EXPERTS)]
         parts = collect_slots(sums)
+        grad_widths = [2 * width, 2 * width + PAIR] if last else [4 * width + PAIR]
         outs = whole_call(
             partial(attend_backward_body, last),
-            [
-                shape_of(row_count, width, f32),
-                shape_of(width, 4 * width + PAIR, bf16),
-            ]
+            [shape_of(row_count, width, f32)]
+            + [shape_of(width, cols, bf16) for cols in grad_widths]
             + ([] if last else [shape_of(SLOTS, width, bf16)]),
             scratch_shapes=[
                 pltpu.VMEM((row_count, width), bf16),
                 pltpu.VMEM((row_count, 3 * width), bf16),
             ],
             name="attend_backward",
-        )(*parts, grad, hidden, inputs, triple, logs, context, spot, bias, gain, weight)
-        grad, attention_grad = outs[:2]
-        attention_total = lax.psum_scatter(attention_grad, both, scatter_dimension=0, tiled=True)
-        if not last:
+        )(*parts, grad, hidden, inputs, triple, logs, context, spot, bias, weight)
+        grad = outs[0]
+        if last:
+            attention_total = jnp.concatenate(
+                [reduce_attention(outs[1], False), reduce_attention(outs[2], True)], 1
+            )
+        else:
             grad_blocks = spread_slots(outs[2])
-        results[layer] = (attention_total, expert_total)
+            attention_total = reduce_attention(outs[1], False, grad_blocks[2])
+        results[layer] = (attention_total, expert_totals)
 
     def columns(layer, start, stop):
-        return results[layer][0][:, start:stop].astype(f32)
+        return results[layer][0][:, start:stop]
 
     deltas = [
         jnp.stack([columns(layer, i * width, (i + 1) * width) for layer in range(LAYERS)])
@@ -417,12 +622,12 @@
         jnp.stack([columns(layer, 4 * width + i, 4 * width + i + 1)[:, 0] for layer in range(LAYERS)])
         for i in range(2)
     ]
-    pieces = [
-        results[layer][1].reshape(shard_rows, EXPERTS, 2, units).astype(f32)
-        for layer in range(LAYERS)
-    ]
-    delta_in = jnp.stack([jnp.transpose(piece[:, :, 0], (1, 0, 2)) for piece in pieces])
-    delta_out = jnp.stack([jnp.transpose(piece[:, :, 1], (1, 2, 0)) for piece in pieces])
+    delta_in = jnp.stack(
+        [jnp.stack([piece[:, :units] for piece in results[layer][1]]) for layer in range(LAYERS)]
+    )
+    delta_out = jnp.stack(
+        [jnp.stack([piece[:, units:].T for piece in results[layer][1]]) for layer in range(LAYERS)]
+    )
     return (mixed, grad, *deltas, *gain_deltas, delta_in, delta_out)
 
 

time: 952 us -> 560 us (0.59)
  waiting for transfers between devices: 732 us -> 279 us
  starting transfers between devices: 13.5 us -> 56.2 us
    reduce_scatter x2, waiting for transfers between devices: 253 us -> 47.9 us  [on_device(): lax.psum_scatter(expert_grads[0], 'dp', scatter_dimension=0, tiled=True)]
    all_gather x3 -> x2, waiting for transfers between devices: 178 us -> 0.02 us  [the longest x1 0.02 us: on_device(): lax.all_gather(expert_shard(1), 'dp', axis=0, tiled=True)]
    unnamed x7 -> x4, waiting for transfers between devices: 160 us -> 0.07 us
    ppermute x0 -> x23, waiting for transfers between devices: none -> 134 us  [the longest x9 44.8 us: reduce_line(): lax.ppermute(sent, 'dp', shift_perm(count, step)).astype(f32)]
    ppermute x24 -> x33, waiting for transfers between devices: 141 us -> 97.6 us  [swap(): return lax.ppermute(values, 'expert', [(i, i ^ flip) for i in range(count)])]
    ppermute x0 -> x23, starting transfers between devices: none -> 35.9 us  [the longest x9 13.8 us: reduce_line(): lax.ppermute(sent, 'dp', shift_perm(count, step)).astype(f32)]
    dynamic_update_slice x0 -> x18, local copies, waits for them, and re-layouts: none -> 12.6 us  [the longest x10 8.51 us: put(): return lax.dynamic_update_index_in_dim(values, piece, at, axis)]
    slice x8 -> x4, local copies, waits for them, and re-layouts: 14.7 us -> 2.77 us  [the longest x2 2.43 us: on_device(): expert_totals = [total[:, expert] for expert in range(EXPERTS)]]
  transfers between devices with their start and end apart: 30 -> 60, of which waited for: 19 -> 27; matrix products, arithmetic and copies ran while one was open for 4% -> 10% of each run, Pallas kernels for 5% -> 20%
where the time goes in v2:
time: 560 us; the launch traced here: 555 us
  waiting for transfers between devices  279 us (50%)
  Pallas kernels  130 us (23%)
  starting transfers between devices  56.2 us (10%)
  local copies, waits for them, and re-layouts  46.4 us (8%)
  other arithmetic  22.8 us (4%)
  between operations  15.3 us (3%)
    ppermute x33, waiting for transfers between devices, swap(): return lax.ppermute(values, 'expert', [(i, i ^ flip) for i in range(count)])  97.6 us
    reduce_scatter x2, waiting for transfers between devices, on_device(): lax.psum_scatter(expert_grads[0], 'dp', scatter_dimension=0, tiled=True)  47.9 us
    pallas_call x2, Pallas kernels, on_device(): whole_call(partial(attend_backward_body, last), [shape_of(row_count, widt...  46.1 us
    ppermute x9, waiting for transfers between devices, reduce_line(): lax.ppermute(sent, 'dp', shift_perm(count, step)).astype(f32)  44.8 us
    ppermute x3, waiting for transfers between devices, gather_rows(): moving = lax.ppermute(moving, 'dp', ring_perm(count))  40.8 us
    pallas_call x2, Pallas kernels, expert_backward(): pl.pallas_call(partial(expert_backward_body, split), grid_spec=pltpu.Pref...  31.4 us
    pallas_call x2, Pallas kernels, on_device(): whole_call(partial(attend_forward_body, first), [shape_of(row_count, 3 *...  29.4 us
    ppermute x4, waiting for transfers between devices, gather_rows(): mate = lax.ppermute(mate, 'dp', pair_perm(count))  23.1 us
  transfers between devices with their start and end apart: 60, of which 27 were waited for; matrix products, arithmetic and copies ran while one was open for 10% of the time, Pallas kernels for 20%

profile of v2, /device:TPU:0, one launch (start us, length us, event | category | flops | bytes accessed | tf_op | source)
XLA Modules:
  0.0 554.6 jit_solution(17492854917734313800)
XLA Ops:
  9.2 3.1 collective-permute-start
  12.3 2.6 collective-permute-start.1
  28.0 4.4 collective-permute-start.11
  34.2 9.8 %collective-permute-done.3 = bf16[4,24,3200]{2,1,0:T(8,128)(2,1)S(1)} collective-permute-done((bf16[4,24,3200]{2,1,0:T(8,128)(2,1)}, bf16[4,24,3200]{2,1,0:T(8,128)(2,1)S(1)}, u32[]{:S(2)}, u32[]{:S(2)}) %collective-permute-start.3) | collective-permute-done | bytes 614432 | tf_op jit(solution)/shard_map/ppermute | solution.py:427
  45.7 2.1 collective-permute-start.10
  47.8 2.6 broadcast_in_dim.62
  51.6 7.9 %collective-permute-done.11 = bf16[96,4608]{1,0:T(8,128)(2,1)S(1)} collective-permute-done((bf16[96,4608]{1,0:T(8,128)(2,1)S(1)}, bf16[96,4608]{1,0:T(8,128)(2,1)S(1)}, u32[]{:S(2)}, u32[]{:S(2)}) %collective-permute-start.11) | collective-permute-done | bytes 884768 | tf_op jit(solution)/shard_map/ppermute | solution.py:391
  61.2 13.4 %collective-permute-done.10 = bf16[96,4608]{1,0:T(8,128)(2,1)S(1)} collective-permute-done((bf16[96,4608]{1,0:T(8,128)(2,1)S(1)}, bf16[96,4608]{1,0:T(8,128)(2,1)S(1)}, u32[]{:S(2)}, u32[]{:S(2)}) %collective-permute-start.10) | collective-permute-done | bytes 884768 | tf_op jit(solution)/shard_map/ppermute | solution.py:387
  74.8 20.9 %collective-permute-done.13 = bf16[96,4608]{1,0:T(8,128)(2,1)} collective-permute-done((bf16[96,4608]{1,0:T(8,128)(2,1)S(1)}, bf16[96,4608]{1,0:T(8,128)(2,1)}, u32[]{:S(2)}, u32[]{:S(2)}) %collective-permute-start.13) | collective-permute-done | bytes 884768 | tf_op jit(solution)/shard_map/ppermute | solution.py:391
  100.4 14.3 %attend_forward.2 = (bf16[384,2304]{1,0:T(8,128)(2,1)}, f32[384,128]{1,0:T(8,128)}, bf16[384,768]{1,0:T(8,128)(2,1)}, f32[384,768]{1,0:T(8,128)}, bf16[432,768]{1,0:T(8,128)(2,1)}) custom-call(bf16[384,768]{1,0:T(8,128)(2,1)} %refs_4_.3, bf16[384,432]{1,0:T(8,128)(2,1)} %fusion.10.refs_1_.refs_3_.refs_8_, f32[384,384]{1,0:T(8,128)} %fusion.17.refs_2_.refs_4_.refs_9_, ...), custom_call_target="tpu_custom_call" | custom-call | flops 1500000 | bytes 1500 | tf_op jit(solution)/shard_map/attend_forward/pallas_call | solution.py:558
  117.4 12.0 %collective-permute-done.15 = bf16[96,4608]{1,0:T(8,128)(2,1)} collective-permute-done((bf16[96,4608]{1,0:T(8,128)(2,1)}, bf16[96,4608]{1,0:T(8,128)(2,1)}, u32[]{:S(2)}, u32[]{:S(2)}) %collective-permute-start.15) | collective-permute-done | bytes 884768 | tf_op jit(solution)/shard_map/ppermute | solution.py:391
  134.4 9.7 %collective-permute-done.16 = bf16[96,4608]{1,0:T(8,128)(2,1)S(1)} collective-permute-done((bf16[96,4608]{1,0:T(8,128)(2,1)}, bf16[96,4608]{1,0:T(8,128)(2,1)S(1)}, u32[]{:S(2)}, u32[]{:S(2)}) %collective-permute-start.16) | collective-permute-done | bytes 884768 | tf_op jit(solution)/shard_map/ppermute | solution.py:387
  145.1 2.2 copy-done
  147.3 10.8 %expert_forward.2 = (bf16[432,768]{1,0:T(8,128)(2,1)}, bf16[432,768]{1,0:T(8,128)(2,1)}, bf16[432,768]{1,0:T(8,128)(2,1)}, bf16[432,768]{1,0:T(8,128)(2,1)}, bf1...) custom-call(bf16[432,768]{1,0:T(8,128)(2,1)} %get-tuple-element.56.refs_0_.refs_4_, bf16[432,768]{1,0:T(8,128)(2,1)} %copy-done.7, ...), custom_call_target="tpu_custom_call" | custom-call | flops 1000000 | bytes 1000 | tf_op jit(solution)/shard_map/expert_forward/pallas_call | solution.py:297
  161.8 2.3 collective-permute-start.19
  165.1 14.2 %collective-permute-done.19.refs_2_ = bf16[432,768]{1,0:T(8,128)(2,1)S(1)} collective-permute-done((bf16[432,768]{1,0:T(8,128)(2,1)S(1)}, bf16[432,768]{1,0:T(8,128)(2,1)S(1)}, u32[]{:S(2)}, u32[]{:S(2)}) %collective-permute-start.19) | collective-permute-done | bytes 663584 | tf_op jit(solution)/shard_map/ppermute | solution.py:348
  180.1 15.2 %attend_forward.3 = (bf16[384,2304]{1,0:T(8,128)(2,1)}, f32[384,128]{1,0:T(8,128)}, bf16[384,768]{1,0:T(8,128)(2,1)}, f32[384,768]{1,0:T(8,128)}, bf16[432,768]{1,0:T(8,128)(2,1)}, /*index=5*/f32[384,768]{1,0:T(8,128)}) custom-call(f32[384,768]{1,0:T(8,128)} %get-tuple-element.55.refs_0_.refs_3_, bf16[432,768]{1,0:T(8,128)(2,1)} %add_convert_fusion.7.refs_1_, ...), custom_call_target="tpu_custom_call" | custom-call | flops 1500000 | bytes 1500 | tf_op jit(solution)/shard_map/attend_forward/pallas_call | solution.py:558
  198.0 15.3 %collective-permute-done.21.refs_2_.refs_6_ = bf16[432,768]{1,0:T(8,128)(2,1)S(1)} collective-permute-done((bf16[432,768]{1,0:T(8,128)(2,1)}, bf16[432,768]{1,0:T(8,128)(2,1)S(1)}, u32[]{:S(2)}, u32[]{:S(2)}) %collective-permute-start.21) | collective-permute-done | bytes 663584 | tf_op jit(solution)/shard_map/ppermute | solution.py:348
  213.8 12.5 %collective-permute-done.27.refs_2_ = bf16[432,768]{1,0:T(8,128)(2,1)} collective-permute-done((bf16[432,768]{1,0:T(8,128)(2,1)S(1)}, bf16[432,768]{1,0:T(8,128)(2,1)}, u32[]{:S(2)}, u32[]{:S(2)}) %collective-permute-start.27) | collective-permute-done | bytes 663584 | tf_op jit(solution)/shard_map/ppermute | solution.py:348
  227.2 10.2 %expert_forward.3 = (bf16[432,768]{1,0:T(8,128)(2,1)}, bf16[432,768]{1,0:T(8,128)(2,1)}, bf16[432,768]{1,0:T(8,128)(2,1)}, bf16[432,768]{1,0:T(8,128)(2,1)}, bf1...) custom-call(bf16[432,768]{1,0:T(8,128)(2,1)} %get-tuple-element.65.refs_0_.refs_4_, bf16[432,768]{1,0:T(8,128)(2,1)} %copy-done.10, ...), custom_call_target="tpu_custom_call" | custom-call | flops 1000000 | bytes 1000 | tf_op jit(solution)/shard_map/expert_forward/pallas_call | solution.py:297
  237.4 15.6 %expert_backward.2 = (bf16[432,768]{1,0:T(8,128)(2,1)}, bf16[432,768]{1,0:T(8,128)(2,1)}, bf16[432,768]{1,0:T(8,128)(2,1)}, bf16[432,768]{1,0:T(8,128)(2,1)}, bf16[768,4608]{1,0:T(8,128)(2,1)}) custom-call(bf16[432,768]{1,0:T(8,128)(2,1)} %copy-done.4, bf16[432,768]{1,0:T(8,128)(2,1)} %collective-permute-done.26.refs_1_, ...), custom_call_target="tpu_custom_call" | custom-call | flops 1600000 | bytes 1600 | tf_op jit(solution)/shard_map/expert_backward/pallas_call | solution.py:330
  254.5 2.6 collective-permute-done.30
  259.8 14.7 %collective-permute-done.31.refs_1_ = bf16[432,768]{1,0:T(8,128)(2,1)S(1)} collective-permute-done((bf16[432,768]{1,0:T(8,128)(2,1)S(1)}, bf16[432,768]{1,0:T(8,128)(2,1)S(1)}, u32[]{:S(2)}, u32[]{:S(2)}) %collective-permute-start.31) | collective-permute-done | bytes 663584 | tf_op jit(solution)/shard_map/ppermute | solution.py:348
  275.5 23.8 %attend_backward.2 = (f32[384,768]{1,0:T(8,128)}, bf16[768,3200]{1,0:T(8,128)(2,1)}, bf16[432,768]{1,0:T(8,128)(2,1)}) custom-call(bf16[432,768]{1,0:T(8,128)(2,1)} %add_convert_fusion.3.refs_0_, bf16[432,768]{1,0:T(8,128)(2,1)} %copy-done.14, f32[384,768]{1,0:T(8,128)} %refs_2_.3, f32[384,768]{1,0:T(8,128)} %get-tuple-element.64.refs_3_, ...), custom_call_target="tpu_custom_call" | custom-call | flops 1500000 | bytes 1500 | tf_op jit(solution)/shard_map/attend_backward/pallas_call | solution.py:593
  299.3 2.8 constant_dynamic-slice_fusion.3
  305.3 15.7 %collective-permute-done.33.refs_2_ = bf16[432,768]{1,0:T(8,128)(2,1)S(1)} collective-permute-done((bf16[432,768]{1,0:T(8,128)(2,1)S(1)}, bf16[432,768]{1,0:T(8,128)(2,1)S(1)}, u32[]{:S(2)}, u32[]{:S(2)}) %collective-permute-start.33) | collective-permute-done | bytes 663584 | tf_op jit(solution)/shard_map/ppermute | solution.py:348
  321.5 2.5 collective-permute-done.34.refs_3_
  324.9 15.8 %expert_backward.3 = (bf16[432,768]{1,0:T(8,128)(2,1)}, bf16[432,768]{1,0:T(8,128)(2,1)}, bf16[432,768]{1,0:T(8,128)(2,1)}, bf16[432,768]{1,0:T(8,128)(2,1)}, bf16[768,4608]{1,0:T(8,128)(2,1)}) custom-call(bf16[432,768]{1,0:T(8,128)(2,1)} %get-tuple-element.80.refs_0_, bf16[432,768]{1,0:T(8,128)(2,1)} %copy-done.16, bf16[432,768]{1,0:T(8,128)(2,1)} %copy-done.15, ...), custom_call_target="tpu_custom_call" | custom-call | flops 1600000 | bytes 1600 | tf_op jit(solution)/shard_map/expert_backward/pallas_call | solution.py:330
  341.3 2.1 add_convert_fusion.4
  347.8 2.3 fusion
  351.7 9.7 %collective-permute-done.25 = bf16[432,768]{1,0:T(8,128)(2,1)} collective-permute-done((bf16[432,768]{1,0:T(8,128)(2,1)}, bf16[432,768]{1,0:T(8,128)(2,1)}, u32[]{:S(2)}, u32[]{:S(2)}) %collective-permute-start.25) | collective-permute-done | bytes 663584 | tf_op jit(solution)/shard_map/ppermute | solution.py:348
  363.1 2.6 fusion.5
  365.7 2.1 add_convert_fusion.1.refs_0_
  367.8 7.8 %collective-permute-done.37.refs_1_ = bf16[432,768]{1,0:T(8,128)(2,1)S(1)} collective-permute-done((bf16[432,768]{1,0:T(8,128)(2,1)S(1)}, bf16[432,768]{1,0:T(8,128)(2,1)S(1)}, u32[]{:S(2)}, u32[]{:S(2)}) %collective-permute-start.37) | collective-permute-done | bytes 663584 | tf_op jit(solution)/shard_map/ppermute | solution.py:348
  376.4 22.3 %attend_backward.3 = (f32[384,768]{1,0:T(8,128)}, bf16[768,1536]{1,0:T(8,128)(2,1)}, bf16[768,1664]{1,0:T(8,128)(2,1)}) custom-call(bf16[432,768]{1,0:T(8,128)(2,1)} %add_convert_fusion.1.refs_0_, bf16[432,768]{1,0:T(8,128)(2,1)} %copy-done.25, f32[384,768]{1,0:T(8,128)} %get-tuple-element.87.refs_2_, f32[384,768]{1,0:T(8,128)} %get-tuple-element.55.refs_0_.refs_3_, ...), custom_call_target="tpu_custom_call" | custom-call | flops 1500000 | bytes 1500 | tf_op jit(solution)/shard_map/attend_backward/pallas_call | solution.py:593
  407.4 13.4 %collective-permute-done.46 = bf16[4,24,3200]{2,1,0:T(8,128)(2,1)S(1)} collective-permute-done((bf16[4,24,3200]{2,1,0:T(8,128)(2,1)S(1)}, bf16[4,24,3200]{2,1,0:T(8,128)(2,1)S(1)}, u32[]{:S(2)}, u32[]{:S(2)}) %collective-permute-start.46) | collective-permute-done | bytes 614432 | tf_op jit(solution)/shard_map/ppermute | solution.py:463
  421.0 3.4 collective-permute-start.49
  424.3 2.1 collective-permute-start.48
  426.4 1.9 collective-permute-start.47
  428.7 6.2 %collective-permute-done.49 = bf16[24,3200]{1,0:T(8,128)(2,1)S(1)} collective-permute-done((bf16[24,3200]{1,0:T(8,128)(2,1)S(1)}, bf16[24,3200]{1,0:T(8,128)(2,1)S(1)}, u32[]{:S(2)}, u32[]{:S(2)}) %collective-permute-start.49) | collective-permute-done | bytes 153632 | tf_op jit(solution)/shard_map/ppermute | solution.py:474
  434.8 22.0 %collective-permute-done.48 = bf16[24,3200]{1,0:T(8,128)(2,1)S(1)} collective-permute-done((bf16[24,3200]{1,0:T(8,128)(2,1)S(1)}, bf16[24,3200]{1,0:T(8,128)(2,1)S(1)}, u32[]{:S(2)}, u32[]{:S(2)}) %collective-permute-start.48) | collective-permute-done | bytes 153632 | tf_op jit(solution)/shard_map/ppermute | solution.py:474
  461.6 3.6 collective-permute-done.43
  465.3 8.0 %collective-permute-done.42 = bf16[24,1536]{1,0:T(8,128)(2,1)S(1)} collective-permute-done((bf16[24,1536]{1,0:T(8,128)(2,1)S(1)}, bf16[24,1536]{1,0:T(8,128)(2,1)S(1)}, u32[]{:S(2)}, u32[]{:S(2)}) %collective-permute-start.42) | collective-permute-done | bytes 73760 | tf_op jit(solution)/shard_map/ppermute | solution.py:474
  477.7 1.9 collective-permute-done.55
  479.7 3.1 collective-permute-done.54
  485.5 3.2 reshape.104
  491.3 47.9 %reduce-scatter.3.cloned.1.call-done = bf16[96,4608]{1,0:T(8,128)(2,1)} async-done(((bf16[768,4608]{1,0:T(8,128)(2,1)}), bf16[96,4608]{1,0:T(8,128)(2,1)}) %reduce-scatter.3.cloned.1.call-update) | async-done | bytes 884752 | tf_op jit(solution)/shard_map/reduce_scatter | solution.py:588
  539.2 3.0 reshape.102
  (253 shorter events, 91.9 us)
Async XLA Ops:
  7.2 172.1 %all-gather.3.cloned.1.call-start = ((), (), s32[]{:S(2)}) async-start(), calls=%async_computation.2 | async-start | bytes 5068800 | tf_op jit(solution)/shard_map/all_gather | solution.py:529
  9.1 217.3 %all-gather.5.cloned.1.call-start = ((), (), s32[]{:S(2)}) async-start(), calls=%async_computation.3 | async-start | bytes 7962624 | tf_op jit(solution)/shard_map/all_gather | solution.py:533
  9.2 13.5 %collective-permute-start = (bf16[24,3200]{1,0:T(8,128)(2,1)}, bf16[24,3200]{1,0:T(8,128)(2,1)S(1)}, u32[]{:S(2)}, u32[]{:S(2)}) collective-permute-start(bf16[24,3200]{1,0:T(8,128)(2,1)} %get-tuple-element.54), channel_id=1, source_target_pairs={{0,8},{4,12},{8,16},{12,20},{16,24},{20,28},{24,0},{28,4},{1,9},{5... | collective-permute-start | bytes 460808 | tf_op jit(solution)/shard_map/ppermute | solution.py:425
  12.3 12.9 %collective-permute-start.1 = (bf16[24,3200]{1,0:T(8,128)(2,1)}, bf16[24,3200]{1,0:T(8,128)(2,1)S(1)}, u32[]{:S(2)}, u32[]{:S(2)}) collective-permute-start(bf16[24,3200]{1,0:T(8,128)(2,1)} %get-tuple-element.54), channel_id=1, source_target_pairs={{0,16},{4,20},{8,24},{12,28},{16,0},{20,4},{24,8},{28,12},{1,17},{... | collective-permute-start | bytes 460808 | tf_op jit(solution)/shard_map/ppermute | solution.py:425
  14.8 11.0 %collective-permute-start.2 = (bf16[24,3200]{1,0:T(8,128)(2,1)}, bf16[24,3200]{1,0:T(8,128)(2,1)S(1)}, u32[]{:S(2)}, u32[]{:S(2)}) collective-permute-start(bf16[24,3200]{1,0:T(8,128)(2,1)} %get-tuple-element.54), channel_id=1, source_target_pairs={{0,24},{4,28},{8,0},{12,4},{16,8},{20,12},{24,16},{28,20},{1,25},{... | collective-permute-start | bytes 460808 | tf_op jit(solution)/shard_map/ppermute | solution.py:425
  18.7 466.9 %reduce-scatter.5.cloned.1.call-start = ((), (), s32[]{:S(2)}) async-start(), calls=%async_computation.5 | async-start | bytes 7962624 | tf_op jit(solution)/shard_map/reduce_scatter | solution.py:588
  26.5 17.5 %collective-permute-start.3 = (bf16[4,24,3200]{2,1,0:T(8,128)(2,1)}, bf16[4,24,3200]{2,1,0:T(8,128)(2,1)S(1)}, u32[]{:S(2)}, u32[]{:S(2)}) collective-permute-start(bf16[4,24,3200]{2,1,0:T(8,128)(2,1)} %bitcast_dynamic-update-slice_fusion.6), channel_id=1, source_target_pairs={{0,4},{4,0},{8,12},{12,8},{16,20},{20,16},{24,28},{28,24},{1,5},{5... | collective-permute-start | bytes 1843208 | tf_op jit(solution)/shard_map/ppermute | solution.py:427
  28.0 31.5 %collective-permute-start.11 = (bf16[96,4608]{1,0:T(8,128)(2,1)S(1)}, bf16[96,4608]{1,0:T(8,128)(2,1)S(1)}, u32[]{:S(2)}, u32[]{:S(2)}) collective-permute-start(bf16[96,4608]{1,0:T(8,128)(2,1)S(1)} %bitcast.218), channel_id=1, source_target_pairs={{0,8},{4,12},{8,16},{12,20},{16,24},{20,28},{24,0},{28,4},{1,9},{5... | collective-permute-start | bytes 2654216 | tf_op jit(solution)/shard_map/ppermute | solution.py:391
  44.0 52.3 %collective-permute-start.4 = (bf16[4,2,24,3200]{3,2,1,0:T(8,128)(2,1)S(1)}, bf16[4,2,24,3200]{3,2,1,0:T(8,128)(2,1)S(1)}, u32[]{:S(2)}, u32[]{:S(2)}) collective-permute-start(bf16[4,2,24,3200]{3,2,1,0:T(8,128)(2,1)S(1)} %bitcast_dynamic-update-slice_fusion.5), channel_id=1, source_target_pairs={{0,1},{1,0},{2,3},{3,2},{4,5},{5,4},{6,7},{7,6},{8,9},{9,8},{10,11... | collective-permute-start | bytes 3686408 | tf_op jit(solution)/shard_map/ppermute | solution.py:348
  44.1 52.1 %collective-permute-start.5 = (bf16[4,2,24,3200]{3,2,1,0:T(8,128)(2,1)S(1)}, bf16[4,2,24,3200]{3,2,1,0:T(8,128)(2,1)S(1)}, u32[]{:S(2)}, u32[]{:S(2)}) collective-permute-start(bf16[4,2,24,3200]{3,2,1,0:T(8,128)(2,1)S(1)} %bitcast_dynamic-update-slice_fusion.5), channel_id=1, source_target_pairs={{0,2},{1,3},{2,0},{3,1},{4,6},{5,7},{6,4},{7,5},{8,10},{9,11},{10,... | collective-permute-start | bytes 3686408 | tf_op jit(solution)/shard_map/ppermute | solution.py:348
  45.7 28.9 %collective-permute-start.10 = (bf16[96,4608]{1,0:T(8,128)(2,1)S(1)}, bf16[96,4608]{1,0:T(8,128)(2,1)S(1)}, u32[]{:S(2)}, u32[]{:S(2)}) collective-permute-start(bf16[96,4608]{1,0:T(8,128)(2,1)S(1)} %bitcast.220), channel_id=1, source_target_pairs={{0,4},{4,0},{8,12},{12,8},{16,20},{20,16},{24,28},{28,24},{1,5},{5... | collective-permute-start | bytes 2654216 | tf_op jit(solution)/shard_map/ppermute | solution.py:387
  59.5 36.6 %collective-permute-start.12 = (bf16[96,4608]{1,0:T(8,128)(2,1)S(1)}, bf16[96,4608]{1,0:T(8,128)(2,1)S(1)}, u32[]{:S(2)}, u32[]{:S(2)}) collective-permute-start(bf16[96,4608]{1,0:T(8,128)(2,1)S(1)} %collective-permute-done.11), channel_id=1, source_target_pairs={{0,4},{4,0},{8,12},{12,8},{16,20},{20,16},{24,28},{28,24},{1,5},{5... | collective-permute-start | bytes 2654216 | tf_op jit(solution)/shard_map/ppermute | solution.py:387
  60.5 35.2 %collective-permute-start.13 = (bf16[96,4608]{1,0:T(8,128)(2,1)S(1)}, bf16[96,4608]{1,0:T(8,128)(2,1)}, u32[]{:S(2)}, u32[]{:S(2)}) collective-permute-start(bf16[96,4608]{1,0:T(8,128)(2,1)S(1)} %collective-permute-done.11), channel_id=1, source_target_pairs={{0,8},{4,12},{8,16},{12,20},{16,24},{20,28},{24,0},{28,4},{1,9},{5... | collective-permute-start | bytes 2654216 | tf_op jit(solution)/shard_map/ppermute | solution.py:391
  95.7 35.6 %collective-permute-start.14 = (bf16[96,4608]{1,0:T(8,128)(2,1)}, bf16[96,4608]{1,0:T(8,128)(2,1)}, u32[]{:S(2)}, u32[]{:S(2)}) collective-permute-start(bf16[96,4608]{1,0:T(8,128)(2,1)} %collective-permute-done.13), channel_id=1, source_target_pairs={{0,4},{4,0},{8,12},{12,8},{16,20},{20,16},{24,28},{28,24},{1,5},{5... | collective-permute-start | bytes 2654216 | tf_op jit(solution)/shard_map/ppermute | solution.py:387
  96.1 33.3 %collective-permute-start.15 = (bf16[96,4608]{1,0:T(8,128)(2,1)}, bf16[96,4608]{1,0:T(8,128)(2,1)}, u32[]{:S(2)}, u32[]{:S(2)}) collective-permute-start(bf16[96,4608]{1,0:T(8,128)(2,1)} %collective-permute-done.13), channel_id=1, source_target_pairs={{0,8},{4,12},{8,16},{12,20},{16,24},{20,28},{24,0},{28,4},{1,9},{5... | collective-permute-start | bytes 2654216 | tf_op jit(solution)/shard_map/ppermute | solution.py:391
  114.6 18.0 %collective-permute-start.8 = (bf16[432,768]{1,0:T(8,128)(2,1)}, bf16[432,768]{1,0:T(8,128)(2,1)S(1)}, u32[]{:S(2)}, u32[]{:S(2)}) collective-permute-start(bf16[432,768]{1,0:T(8,128)(2,1)} %get-tuple-element.56.refs_0_.refs_4_), channel_id=1, source_target_pairs={{0,2},{1,3},{2,0},{3,1},{4,6},{5,7},{6,4},{7,5},{8,10},{9,11},{10,... | collective-permute-start | bytes 1990664 | tf_op jit(solution)/shard_map/ppermute | solution.py:348
  129.4 14.7 %collective-permute-start.16 = (bf16[96,4608]{1,0:T(8,128)(2,1)}, bf16[96,4608]{1,0:T(8,128)(2,1)S(1)}, u32[]{:S(2)}, u32[]{:S(2)}) collective-permute-start(bf16[96,4608]{1,0:T(8,128)(2,1)} %collective-permute-done.15), channel_id=1, source_target_pairs={{0,4},{4,0},{8,12},{12,8},{16,20},{20,16},{24,28},{28,24},{1,5},{5... | collective-permute-start | bytes 2654216 | tf_op jit(solution)/shard_map/ppermute | solution.py:387
  132.5 11.6 %collective-permute-start.7 = (bf16[432,768]{1,0:T(8,128)(2,1)S(1)}, bf16[432,768]{1,0:T(8,128)(2,1)S(1)}, u32[]{:S(2)}, u32[]{:S(2)}) collective-permute-start(bf16[432,768]{1,0:T(8,128)(2,1)S(1)} %copy-done.5), channel_id=1, source_target_pairs={{0,1},{1,0},{2,3},{3,2},{4,5},{5,4},{6,7},{7,6},{8,9},{9,8},{10,11... | collective-permute-start | bytes 1990664 | tf_op jit(solution)/shard_map/ppermute | solution.py:348
  132.6 12.5 %collective-permute-start.9 = (bf16[432,768]{1,0:T(8,128)(2,1)S(1)}, bf16[432,768]{1,0:T(8,128)(2,1)}, u32[]{:S(2)}, u32[]{:S(2)}) collective-permute-start(bf16[432,768]{1,0:T(8,128)(2,1)S(1)} %collective-permute-done.8.refs_2_.refs_6_), channel_id=1, source_target_pairs={{0,1},{1,0},{2,3},{3,2},{4,5},{5,4},{6,7},{7,6},{8,9},{9,8},{10,11... | collective-permute-start | bytes 1990664 | tf_op jit(solution)/shard_map/ppermute | solution.py:348
  161.8 17.5 %collective-permute-start.19 = (bf16[432,768]{1,0:T(8,128)(2,1)S(1)}, bf16[432,768]{1,0:T(8,128)(2,1)S(1)}, u32[]{:S(2)}, u32[]{:S(2)}) collective-permute-start(bf16[432,768]{1,0:T(8,128)(2,1)S(1)} %add_convert_fusion.6), channel_id=1, source_target_pairs={{0,2},{1,3},{2,0},{3,1},{4,6},{5,7},{6,4},{7,5},{8,10},{9,11},{10,... | collective-permute-start | bytes 1990664 | tf_op jit(solution)/shard_map/ppermute | solution.py:348
  195.3 18.0 %collective-permute-start.21 = (bf16[432,768]{1,0:T(8,128)(2,1)}, bf16[432,768]{1,0:T(8,128)(2,1)S(1)}, u32[]{:S(2)}, u32[]{:S(2)}) collective-permute-start(bf16[432,768]{1,0:T(8,128)(2,1)} %get-tuple-element.65.refs_0_.refs_4_), channel_id=1, source_target_pairs={{0,2},{1,3},{2,0},{3,1},{4,6},{5,7},{6,4},{7,5},{8,10},{9,11},{10,... | collective-permute-start | bytes 1990664 | tf_op jit(solution)/shard_map/ppermute | solution.py:348
  197.7 28.7 %collective-permute-start.27 = (bf16[432,768]{1,0:T(8,128)(2,1)S(1)}, bf16[432,768]{1,0:T(8,128)(2,1)}, u32[]{:S(2)}, u32[]{:S(2)}) collective-permute-start(bf16[432,768]{1,0:T(8,128)(2,1)S(1)} %convolution_convert_fusion.refs_0_), channel_id=1, source_target_pairs={{0,2},{1,3},{2,0},{3,1},{4,6},{5,7},{6,4},{7,5},{8,10},{9,11},{10,... | collective-permute-start | bytes 1990664 | tf_op jit(solution)/shard_map/ppermute | solution.py:348
  198.0 28.3 %collective-permute-start.20 = (bf16[432,768]{1,0:T(8,128)(2,1)S(1)}, bf16[432,768]{1,0:T(8,128)(2,1)S(1)}, u32[]{:S(2)}, u32[]{:S(2)}) collective-permute-start(bf16[432,768]{1,0:T(8,128)(2,1)S(1)} %copy-done.8), channel_id=1, source_target_pairs={{0,1},{1,0},{2,3},{3,2},{4,5},{5,4},{6,7},{7,6},{8,9},{9,8},{10,11... | collective-permute-start | bytes 1990664 | tf_op jit(solution)/shard_map/ppermute | solution.py:348
  213.3 13.1 %collective-permute-start.22 = (bf16[432,768]{1,0:T(8,128)(2,1)S(1)}, bf16[432,768]{1,0:T(8,128)(2,1)}, u32[]{:S(2)}, u32[]{:S(2)}) collective-permute-start(bf16[432,768]{1,0:T(8,128)(2,1)S(1)} %collective-permute-done.21.refs_2_.refs_6_), channel_id=1, source_target_pairs={{0,1},{1,0},{2,3},{3,2},{4,5},{5,4},{6,7},{7,6},{8,9},{9,8},{10,11... | collective-permute-start | bytes 1990664 | tf_op jit(solution)/shard_map/ppermute | solution.py:348
  213.3 24.1 %collective-permute-start.26 = (bf16[432,768]{1,0:T(8,128)(2,1)S(1)}, bf16[432,768]{1,0:T(8,128)(2,1)}, u32[]{:S(2)}, u32[]{:S(2)}) collective-permute-start(bf16[432,768]{1,0:T(8,128)(2,1)S(1)} %convolution_convert_fusion.refs_0_), channel_id=1, source_target_pairs={{0,1},{1,0},{2,3},{3,2},{4,5},{5,4},{6,7},{7,6},{8,9},{9,8},{10,11... | collective-permute-start | bytes 1990664 | tf_op jit(solution)/shard_map/ppermute | solution.py:348
  226.3 11.0 %collective-permute-start.28 = (bf16[432,768]{1,0:T(8,128)(2,1)}, bf16[432,768]{1,0:T(8,128)(2,1)}, u32[]{:S(2)}, u32[]{:S(2)}) collective-permute-start(bf16[432,768]{1,0:T(8,128)(2,1)} %collective-permute-done.27.refs_2_), channel_id=1, source_target_pairs={{0,1},{1,0},{2,3},{3,2},{4,5},{5,4},{6,7},{7,6},{8,9},{9,8},{10,11... | collective-permute-start | bytes 1990664 | tf_op jit(solution)/shard_map/ppermute | solution.py:348
  253.0 286.3 %reduce-scatter.3.cloned.1.call-start = ((), (), s32[]{:S(2)}) async-start(), calls=%async_computation.4 | async-start | bytes 7962624 | tf_op jit(solution)/shard_map/reduce_scatter | solution.py:588
  257.3 17.3 %collective-permute-start.31 = (bf16[432,768]{1,0:T(8,128)(2,1)S(1)}, bf16[432,768]{1,0:T(8,128)(2,1)S(1)}, u32[]{:S(2)}, u32[]{:S(2)}) collective-permute-start(bf16[432,768]{1,0:T(8,128)(2,1)S(1)} %add_convert_fusion.2), channel_id=1, source_target_pairs={{0,2},{1,3},{2,0},{3,1},{4,6},{5,7},{6,4},{7,5},{8,10},{9,11},{10,... | collective-permute-start | bytes 1990664 | tf_op jit(solution)/shard_map/ppermute | solution.py:348
  303.7 44.2 %collective-permute-start.44 = (bf16[4,2,2,24,3200]{4,3,0,1,2:T(8,128)(2,1)}, bf16[4,2,2,24,3200]{4,3,0,1,2:T(8,128)(2,1)}, u32[]{:S(2)}, u32[]{:S(2)}) collective-permute-start(bf16[4,2,2,24,3200]{4,3,0,1,2:T(8,128)(2,1)} %bitcast.207), channel_id=1, source_target_pairs={{0,1},{1,0},{2,3},{3,2},{4,5},{5,4},{6,7},{7,6},{8,9},{9,8},{10,11... | collective-permute-start | bytes 7372808 | tf_op jit(solution)/shard_map/ppermute | solution.py:348
  303.7 17.3 %collective-permute-start.33 = (bf16[432,768]{1,0:T(8,128)(2,1)S(1)}, bf16[432,768]{1,0:T(8,128)(2,1)S(1)}, u32[]{:S(2)}, u32[]{:S(2)}) collective-permute-start(bf16[432,768]{1,0:T(8,128)(2,1)S(1)} %copy-done.13), channel_id=1, source_target_pairs={{0,2},{1,3},{2,0},{3,1},{4,6},{5,7},{6,4},{7,5},{8,10},{9,11},{10,... | collective-permute-start | bytes 1990664 | tf_op jit(solution)/shard_map/ppermute | solution.py:348
  305.1 16.4 %collective-permute-start.32 = (bf16[432,768]{1,0:T(8,128)(2,1)S(1)}, bf16[432,768]{1,0:T(8,128)(2,1)S(1)}, u32[]{:S(2)}, u32[]{:S(2)}) collective-permute-start(bf16[432,768]{1,0:T(8,128)(2,1)S(1)} %copy-done.13), channel_id=1, source_target_pairs={{0,1},{1,0},{2,3},{3,2},{4,5},{5,4},{6,7},{7,6},{8,9},{9,8},{10,11... | collective-permute-start | bytes 1990664 | tf_op jit(solution)/shard_map/ppermute | solution.py:348
  321.0 20.3 %collective-permute-start.24 = (bf16[432,768]{1,0:T(8,128)(2,1)}, bf16[432,768]{1,0:T(8,128)(2,1)}, u32[]{:S(2)}, u32[]{:S(2)}) collective-permute-start(bf16[432,768]{1,0:T(8,128)(2,1)} %get-tuple-element.69), channel_id=1, source_target_pairs={{0,1},{1,0},{2,3},{3,2},{4,5},{5,4},{6,7},{7,6},{8,9},{9,8},{10,11... | collective-permute-start | bytes 1990664 | tf_op jit(solution)/shard_map/ppermute | solution.py:348
  340.8 22.3 %collective-permute-start.23 = (bf16[432,768]{1,0:T(8,128)(2,1)}, bf16[432,768]{1,0:T(8,128)(2,1)}, u32[]{:S(2)}, u32[]{:S(2)}) collective-permute-start(bf16[432,768]{1,0:T(8,128)(2,1)} %get-tuple-element.67), channel_id=1, source_target_pairs={{0,1},{1,0},{2,3},{3,2},{4,5},{5,4},{6,7},{7,6},{8,9},{9,8},{10,11... | collective-permute-start | bytes 1990664 | tf_op jit(solution)/shard_map/ppermute | solution.py:348
  343.4 18.1 %collective-permute-start.25 = (bf16[432,768]{1,0:T(8,128)(2,1)}, bf16[432,768]{1,0:T(8,128)(2,1)}, u32[]{:S(2)}, u32[]{:S(2)}) collective-permute-start(bf16[432,768]{1,0:T(8,128)(2,1)} %add_convert_fusion.4), channel_id=1, source_target_pairs={{0,2},{1,3},{2,0},{3,1},{4,6},{5,7},{6,4},{7,5},{8,10},{9,11},{10,... | collective-permute-start | bytes 1990664 | tf_op jit(solution)/shard_map/ppermute | solution.py:348
  344.8 20.9 %collective-permute-start.35 = (bf16[432,768]{1,0:T(8,128)(2,1)}, bf16[432,768]{1,0:T(8,128)(2,1)}, u32[]{:S(2)}, u32[]{:S(2)}) collective-permute-start(bf16[432,768]{1,0:T(8,128)(2,1)} %get-tuple-element.84), channel_id=1, source_target_pairs={{0,1},{1,0},{2,3},{3,2},{4,5},{5,4},{6,7},{7,6},{8,9},{9,8},{10,11... | collective-permute-start | bytes 1990664 | tf_op jit(solution)/shard_map/ppermute | solution.py:348
  347.2 28.4 %collective-permute-start.37 = (bf16[432,768]{1,0:T(8,128)(2,1)S(1)}, bf16[432,768]{1,0:T(8,128)(2,1)S(1)}, u32[]{:S(2)}, u32[]{:S(2)}) collective-permute-start(bf16[432,768]{1,0:T(8,128)(2,1)S(1)} %add_convert_fusion), channel_id=1, source_target_pairs={{0,2},{1,3},{2,0},{3,1},{4,6},{5,7},{6,4},{7,5},{8,10},{9,11},{10,... | collective-permute-start | bytes 1990664 | tf_op jit(solution)/shard_map/ppermute | solution.py:348
  350.2 51.5 %collective-permute-start.45 = (bf16[4,2,24,3200]{3,2,0,1:T(8,128)(2,1)S(1)}, bf16[4,2,24,3200]{3,2,0,1:T(8,128)(2,1)S(1)}, u32[]{:S(2)}, u32[]{:S(2)}) collective-permute-start(bf16[4,2,24,3200]{3,2,0,1:T(8,128)(2,1)S(1)} %dynamic-slice_bitcast_fusion), channel_id=1, source_target_pairs={{0,2},{1,3},{2,0},{3,1},{4,6},{5,7},{6,4},{7,5},{8,10},{9,11},{10,... | collective-permute-start | bytes 3686408 | tf_op jit(solution)/shard_map/ppermute | solution.py:348
  402.0 18.7 %collective-permute-start.46 = (bf16[4,24,3200]{2,1,0:T(8,128)(2,1)S(1)}, bf16[4,24,3200]{2,1,0:T(8,128)(2,1)S(1)}, u32[]{:S(2)}, u32[]{:S(2)}) collective-permute-start(bf16[4,24,3200]{2,1,0:T(8,128)(2,1)S(1)} %dynamic-slice_bitcast_fusion.2), channel_id=1, source_target_pairs={{0,4},{4,0},{8,12},{12,8},{16,20},{20,16},{24,28},{28,24},{1,5},{5... | collective-permute-start | bytes 1843208 | tf_op jit(solution)/shard_map/ppermute | solution.py:463
  404.0 24.4 %collective-permute-start.39 = (bf16[4,2,24,1536]{3,2,0,1:T(8,128)(2,1)S(1)}, bf16[4,2,24,1536]{3,2,0,1:T(8,128)(2,1)S(1)}, u32[]{:S(2)}, u32[]{:S(2)}) collective-permute-start(bf16[4,2,24,1536]{3,2,0,1:T(8,128)(2,1)S(1)} %dynamic-slice_bitcast_fusion.3), channel_id=1, source_target_pairs={{0,2},{1,3},{2,0},{3,1},{4,6},{5,7},{6,4},{7,5},{8,10},{9,11},{10,... | collective-permute-start | bytes 1769480 | tf_op jit(solution)/shard_map/ppermute | solution.py:348
  405.9 51.2 %collective-permute-start.51 = (bf16[4,2,24,1664]{3,2,0,1:T(8,128)(2,1)S(1)}, bf16[4,2,24,1664]{3,2,0,1:T(8,128)(2,1)S(1)}, u32[]{:S(2)}, u32[]{:S(2)}) collective-permute-start(bf16[4,2,24,1664]{3,2,0,1:T(8,128)(2,1)S(1)} %dynamic-slice_bitcast_fusion.1), channel_id=1, source_target_pairs={{0,4},{4,0},{8,12},{12,8},{16,20},{20,16},{24,28},{28,24},{1,5},{5... | collective-permute-start | bytes 1916936 | tf_op jit(solution)/shard_map/ppermute | solution.py:463
  421.0 13.9 %collective-permute-start.49 = (bf16[24,3200]{1,0:T(8,128)(2,1)S(1)}, bf16[24,3200]{1,0:T(8,128)(2,1)S(1)}, u32[]{:S(2)}, u32[]{:S(2)}) collective-permute-start(bf16[24,3200]{1,0:T(8,128)(2,1)S(1)} %get-tuple-element.119), channel_id=1, source_target_pairs={{0,24},{4,28},{8,0},{12,4},{16,8},{20,12},{24,16},{28,20},{1,25},{... | collective-permute-start | bytes 460808 | tf_op jit(solution)/shard_map/ppermute | solution.py:474
  424.3 32.5 %collective-permute-start.48 = (bf16[24,3200]{1,0:T(8,128)(2,1)S(1)}, bf16[24,3200]{1,0:T(8,128)(2,1)S(1)}, u32[]{:S(2)}, u32[]{:S(2)}) collective-permute-start(bf16[24,3200]{1,0:T(8,128)(2,1)S(1)} %get-tuple-element.120), channel_id=1, source_target_pairs={{0,16},{4,20},{8,24},{12,28},{16,0},{20,4},{24,8},{28,12},{1,17},{... | collective-permute-start | bytes 460808 | tf_op jit(solution)/shard_map/ppermute | solution.py:474
  426.4 30.4 %collective-permute-start.47 = (bf16[24,3200]{1,0:T(8,128)(2,1)S(1)}, bf16[24,3200]{1,0:T(8,128)(2,1)S(1)}, u32[]{:S(2)}, u32[]{:S(2)}) collective-permute-start(bf16[24,3200]{1,0:T(8,128)(2,1)S(1)} %get-tuple-element.118), channel_id=1, source_target_pairs={{0,8},{4,12},{8,16},{12,20},{16,24},{20,28},{24,0},{28,4},{1,9},{5... | collective-permute-start | bytes 460808 | tf_op jit(solution)/shard_map/ppermute | solution.py:474
  428.6 28.7 %collective-permute-start.40 = (bf16[4,24,1536]{2,1,0:T(8,128)(2,1)S(1)}, bf16[4,24,1536]{2,1,0:T(8,128)(2,1)S(1)}, u32[]{:S(2)}, u32[]{:S(2)}) collective-permute-start(bf16[4,24,1536]{2,1,0:T(8,128)(2,1)S(1)} %dynamic-slice_bitcast_fusion.5), channel_id=1, source_target_pairs={{0,4},{4,0},{8,12},{12,8},{16,20},{20,16},{24,28},{28,24},{1,5},{5... | collective-permute-start | bytes 884744 | tf_op jit(solution)/shard_map/ppermute | solution.py:463
  457.5 15.8 %collective-permute-start.42 = (bf16[24,1536]{1,0:T(8,128)(2,1)S(1)}, bf16[24,1536]{1,0:T(8,128)(2,1)S(1)}, u32[]{:S(2)}, u32[]{:S(2)}) collective-permute-start(bf16[24,1536]{1,0:T(8,128)(2,1)S(1)} %get-tuple-element.142), channel_id=1, source_target_pairs={{0,16},{4,20},{8,24},{12,28},{16,0},{20,4},{24,8},{28,12},{1,17},{... | collective-permute-start | bytes 221192 | tf_op jit(solution)/shard_map/ppermute | solution.py:474
  459.0 14.3 %collective-permute-start.41 = (bf16[24,1536]{1,0:T(8,128)(2,1)S(1)}, bf16[24,1536]{1,0:T(8,128)(2,1)S(1)}, u32[]{:S(2)}, u32[]{:S(2)}) collective-permute-start(bf16[24,1536]{1,0:T(8,128)(2,1)S(1)} %get-tuple-element.140), channel_id=1, source_target_pairs={{0,8},{4,12},{8,16},{12,20},{16,24},{20,28},{24,0},{28,4},{1,9},{5... | collective-permute-start | bytes 221192 | tf_op jit(solution)/shard_map/ppermute | solution.py:474
  460.9 13.1 %collective-permute-start.52 = (bf16[4,24,1664]{2,1,0:T(8,128)(2,1)S(1)}, bf16[4,24,1664]{2,1,0:T(8,128)(2,1)S(1)}, u32[]{:S(2)}, u32[]{:S(2)}) collective-permute-start(bf16[4,24,1664]{2,1,0:T(8,128)(2,1)S(1)} %dynamic-slice_bitcast_fusion.4), channel_id=1, source_target_pairs={{0,2},{1,3},{2,0},{3,1},{4,6},{5,7},{6,4},{7,5},{8,10},{9,11},{10,... | collective-permute-start | bytes 958472 | tf_op jit(solution)/shard_map/ppermute | solution.py:348
  474.2 8.6 %collective-permute-start.54 = (bf16[24,1664]{1,0:T(8,128)(2,1)S(1)}, bf16[24,1664]{1,0:T(8,128)(2,1)S(1)}, u32[]{:S(2)}, u32[]{:S(2)}) collective-permute-start(bf16[24,1664]{1,0:T(8,128)(2,1)S(1)} %get-tuple-element.135), channel_id=1, source_target_pairs={{0,16},{4,20},{8,24},{12,28},{16,0},{20,4},{24,8},{28,12},{1,17},{... | collective-permute-start | bytes 239624 | tf_op jit(solution)/shard_map/ppermute | solution.py:474
  (44 other events, 251.6 us)
Sparse Core Ops, SparseCore 0:
  10.9 85.0 all-gather.2
  98.2 116.1 all-gather.4
  253.1 132.5 reduce-scatter.4
  389.7 149.5 reduce-scatter.2

commit v3 on v2

--- a/solution.py
+++ b/solution.py
@@ -152,10 +152,10 @@
         weight_ref,
     ) = refs[:11]
     slots_ref = None
-    if last:
-        grad_out_ref, first_grad_ref, second_grad_ref, context_grad_ref, triple_grad_ref = refs[11:]
-    else:
-        grad_out_ref, first_grad_ref, slots_ref, context_grad_ref, triple_grad_ref = refs[11:]
+    grad_out_ref, weight_grad_ref = refs[11:13]
+    if not last:
+        slots_ref = refs[13]
+    context_grad_ref, triple_grad_ref = refs[-2:]
     width = rows_ref.shape[1]
     gains = weight_ref[:, 4 * width :].astype(f32).T
     spot = spot_ref[...]
@@ -168,10 +168,7 @@
     branch = hidden_grad.astype(bf16)
     context_grad_ref[...] = contract_cols(branch, weight_ref[:, 3 * width : 4 * width]).astype(bf16)
     output_grad = contract_rows(context_ref[...], branch).astype(bf16)
-    if last:
-        second_grad_ref[:, width : 2 * width] = output_grad
-    else:
-        first_grad_ref[:, 3 * width : 4 * width] = output_grad
+    weight_grad_ref[:, 3 * width : 4 * width] = output_grad
     lane = lax.broadcasted_iota(jnp.int32, (row_count, PAIR), 1)
 
     def one_pair(pair, carry):
@@ -212,11 +209,7 @@
     unit, rate = norm_parts(rows_ref[...].astype(f32))
     normed = (unit * gains[0:1, :]).astype(bf16)
     triple_grad = triple_grad_ref[...]
-    if last:
-        first_grad_ref[...] = contract_rows(normed, triple_grad[:, : 2 * width]).astype(bf16)
-        second_grad_ref[:, :width] = contract_rows(normed, triple_grad[:, 2 * width :]).astype(bf16)
-    else:
-        first_grad_ref[:, : 3 * width] = contract_rows(normed, triple_grad).astype(bf16)
+    weight_grad_ref[:, : 3 * width] = contract_rows(normed, triple_grad).astype(bf16)
     normed_grad = contract_cols(triple_grad, weight_ref[:, : 3 * width])
     first_gain_grad = jnp.sum(normed_grad * unit, 0, keepdims=True)
     out_grad = grad_out_ref[...] + norm_back(unit, rate, normed_grad * gains[0:1, :])
@@ -227,10 +220,7 @@
     gain_rows = jnp.where(
         which == 0, first_gain_grad, jnp.where(which == 1, second_gain_grad, 0.0)
     )
-    if last:
-        second_grad_ref[:, 2 * width :] = gain_rows.T.astype(bf16)
-    else:
-        first_grad_ref[:, 4 * width :] = gain_rows.T.astype(bf16)
+    weight_grad_ref[:, 4 * width :] = gain_rows.T.astype(bf16)
 
 
 def expert_forward_body(*refs):
@@ -253,11 +243,10 @@
 
 
 def expert_backward_body(split, *refs):
-    if split:
-        place_ref, *refs = refs
+    place_ref, *refs = refs
     grad_refs, block_refs = refs[:4], refs[4:8]
     active_ref, slope_ref, weight_ref = refs[8:11]
-    out_refs = refs[11:15]
+    out_refs, total_refs = refs[11:15], refs[15:]
     units = weight_ref.shape[1] // 2
     grads = jnp.concatenate([ref[...] for ref in grad_refs], 0)
     rows = jnp.concatenate([ref[...] for ref in block_refs], 0)
@@ -266,27 +255,55 @@
     sums = contract_cols(before_grad, weight_ref[:, :units]).astype(bf16)
     for place in range(4):
         out_refs[place][...] = sums[place * MOST : (place + 1) * MOST]
-    pieces = ((rows, before_grad, 0), (grads, active_ref[...], units))
-    if not split:
-        for left, right, start in pieces:
-            refs[15][:, start : start + units] = contract_rows(left, right).astype(bf16)
-        return
-    ring, mine = place_ref[0], place_ref[1]
-    outer, count = refs[15].shape[:2]
-    for left, right, start in pieces:
+    step = pl.program_id(0)
+    for left, right, start in ((rows, before_grad, 0), (grads, active_ref[...], units)):
         grad = contract_rows(left, right).astype(bf16)
+        span = slice(start, start + units)
+        if not split:
+            total_refs[0][:, span] = grad
+            continue
+        ring, mine = place_ref[0], place_ref[1]
+        outer, count = total_refs[0].shape[:2]
+
+        def piece(block, half):
+            first = (2 * block + half) * count
+            return grad[first : first + count]
+
         for expert in range(EXPERTS):
-            kept_ref, sent_ref = refs[15 + 2 * expert], refs[16 + 2 * expert]
             for half in range(2):
 
-                @pl.when((pl.program_id(0) == expert) & (mine == half))
+                @pl.when((step == expert) & (mine == half))
                 def _():
                     for block in range(outer):
                         at = lax.rem(block - ring + outer, outer)
-                        low = (2 * block + half) * count
-                        high = (2 * block + 1 - half) * count
-                        kept_ref[at, :, start : start + units] = grad[low : low + count]
-                        sent_ref[at, :, start : start + units] = grad[high : high + count]
+                        kept_ref, sent_ref = total_refs[2 * expert : 2 * expert + 2]
+                        kept_ref[at, :, span] = piece(block, half)
+                        sent_ref[at, :, span] = piece(block, 1 - half)
+
+
+def finish_body(places, *refs):
+    outs = refs[-8:]
+    at = 0
+    units = outs[6].shape[3]
+    for layer, experts in enumerate(places):
+        for expert, (source, start) in enumerate(experts):
+            values = refs[at + source]
+            outs[6][layer, expert] = values[:, start : start + units].astype(f32)
+            outs[7][layer, expert] = values[:, start + units : start + 2 * units].astype(f32)
+        at += max(source for source, _ in experts) + 1
+        sums = refs[at][...].astype(f32)
+        at += 1
+        rows, width = outs[0].shape[1:]
+        for place in range(4):
+            outs[place][layer] = sums[:, place * width : (place + 1) * width]
+        diagonal = lax.broadcasted_iota(jnp.int32, (rows, rows), 0) == lax.broadcasted_iota(
+            jnp.int32, (rows, rows), 1
+        )
+        for place in range(2):
+            column = sums[:, 4 * width + place : 4 * width + place + 1]
+            outs[4 + place][layer : layer + 1, :] = jnp.sum(
+                jnp.where(diagonal, column, 0.0), 0, keepdims=True
+            )
 
 
 def expert_forward(blocks, weights):
@@ -311,26 +328,23 @@
 def expert_backward(grads, blocks, active, slope, weights, split):
     width = blocks[0].shape[1]
     units = weights.shape[1] // (2 * EXPERTS)
+    count, me = lax.axis_size("dp"), lax.axis_index("dp")
     block = pl.BlockSpec((MOST, width), lambda e, *_: (e, 0))
     kept = pl.BlockSpec((4 * MOST, units), lambda e, *_: (e, 0))
     square = pl.BlockSpec((width, 2 * units), lambda e, *_: (0, e))
     out_specs = [block] * 4
     out_shape = [jax.ShapeDtypeStruct((SLOTS, width), bf16)] * 4
-    places = []
     if split:
-        count = lax.axis_size("dp")
-        me = lax.axis_index("dp")
-        places = [jnp.stack([me // 2, lax.rem(me, 2)]).astype(jnp.int32)]
-        shape = (count // 2, width // count, 2 * units)
-        out_specs += [pl.BlockSpec(shape, lambda e, *_: (0, 0, 0))] * (2 * EXPERTS)
-        out_shape += [jax.ShapeDtypeStruct(shape, bf16)] * (2 * EXPERTS)
+        pair = (count // 2, width // count, 2 * units)
+        out_specs += [pl.BlockSpec(pair, lambda e, *_: (0, 0, 0))] * (2 * EXPERTS)
+        out_shape += [jax.ShapeDtypeStruct(pair, bf16)] * (2 * EXPERTS)
     else:
         out_specs += [square]
         out_shape += [jax.ShapeDtypeStruct(weights.shape, bf16)]
     outs = pl.pallas_call(
         partial(expert_backward_body, split),
         grid_spec=pltpu.PrefetchScalarGridSpec(
-            num_scalar_prefetch=len(places),
+            num_scalar_prefetch=1,
             grid=(EXPERTS,),
             in_specs=[block] * 8 + [kept] * 2 + [square],
             out_specs=out_specs,
@@ -339,7 +353,14 @@
         compiler_params=pltpu.CompilerParams(vmem_limit_bytes=VMEM_BYTES),
         cost_estimate=cost(16),
         name="expert_backward",
-    )(*places, *grads, *blocks, active, slope, weights)
+    )(
+        jnp.stack([me // 2, lax.rem(me, 2)]).astype(jnp.int32),
+        *grads,
+        *blocks,
+        active,
+        slope,
+        weights,
+    )
     return outs[:4], outs[4:]
 
 
@@ -355,14 +376,18 @@
     return [slots, beside, across, corner]
 
 
-def collect_slots(parts):
+def collect_core(parts):
     own, beside, across, corner = parts
     corner_in = swap(corner, 1)
     beside_in = swap(beside, 1)
     far = (across.astype(f32) + corner_in.astype(f32)).astype(bf16)
-    far_in = swap(far, 2)
     near = (own.astype(f32) + beside_in.astype(f32)).astype(bf16)
-    return near, far_in
+    return near, far
+
+
+def collect_slots(parts):
+    near, far = collect_core(parts)
+    return near, swap(far, 2)
 
 
 def pair_perm(count):
@@ -373,22 +398,28 @@
     return [(i, (i + 2) % count) for i in range(count)]
 
 
-def gather_rows(shard, line_done, pair_done):
+def gather_rows(shard, events):
     count = lax.axis_size("dp")
     if count > RING_MOST:
         return lax.all_gather(shard, "dp", axis=0, tiled=True)
+    line_done, pair_done, all_done = events
     me = lax.axis_index("dp")
     rows, cols = shard.shape
     full = jnp.zeros((count * rows, cols), shard.dtype)
     moving, _ = tie(shard, line_done)
     for step in range(count // 2):
         source = lax.rem(me - 2 * step + count, count)
-        mate, _ = tie(moving, pair_done) if step == 0 else (moving, None)
+        mate = moving
+        if step == 0:
+            mate, _ = tie(mate, pair_done)
         mate = lax.ppermute(mate, "dp", pair_perm(count))
+        mate, _ = tie(mate, all_done)
         full = lax.dynamic_update_slice(full, moving, (source * rows, 0))
         full = lax.dynamic_update_slice(full, mate, ((source ^ 1) * rows, 0))
         if step + 1 < count // 2:
             moving = lax.ppermute(moving, "dp", ring_perm(count))
+            if step > 0:
+                moving, _ = tie(moving, all_done)
     return full
 
 
@@ -413,12 +444,12 @@
 
 
 def gather_attention(shard):
-    count, sides = lax.axis_size("dp"), lax.axis_size("expert")
+    count = lax.axis_size("dp")
     if count > RING_MOST:
-        return lax.all_gather(shard, ("dp", "expert"), axis=0, tiled=True), None, None
+        return lax.all_gather(shard, ("dp", "expert"), axis=0, tiled=True), (shard,) * 3
     rows, cols = shard.shape
     outer = count // 2
-    me, side = lax.axis_index("dp"), lax.axis_index("expert")
+    me = lax.axis_index("dp")
     line = me // 2
     quad = put(jnp.zeros((outer, rows, cols), shard.dtype), shard, line, 0)
     for step in range(1, outer):
@@ -428,22 +459,37 @@
     both = jnp.zeros((outer, 2, rows, cols), shard.dtype)
     both = put(put(both, quad, lax.rem(me, 2), 1), mate, 1 - lax.rem(me, 2), 1)
     across = swap(both, 2)
-    full = jnp.zeros((outer, 2, sides, rows, cols), shard.dtype)
+    full, corner = join_sides(both, across)
+    return full, (got, mate, corner)
+
+
+def join_sides(both, across):
+    outer, _, rows, cols = both.shape
+    sides, side = lax.axis_size("expert"), lax.axis_index("expert")
+    full = jnp.zeros((outer, 2, sides, rows, cols), both.dtype)
+    corner = swap(across, 1)
     full = put(full, both, side, 2)
     full = put(full, swap(both, 1), side ^ 1, 2)
     full = put(full, across, side ^ 2, 2)
-    full = put(full, swap(across, 1), side ^ 3, 2)
-    return full.reshape(-1, cols), got, mate
-
-
-def reduce_pairs(kept, got):
-    count = lax.axis_size("dp")
-    outer = count // 2
-    total = add(kept[0], got[0])
-    for step in range(1, outer):
-        sent = add(kept[step], got[step]).astype(bf16)
-        total = total + lax.ppermute(sent, "dp", shift_perm(count, step)).astype(f32)
-    return total
+    full = put(full, corner, side ^ 3, 2)
+    return full.reshape(-1, cols), corner
+
+
+def swap_pair(values):
+    return lax.ppermute(values, "dp", pair_perm(lax.axis_size("dp")))
+
+
+def ring_step(values):
+    return lax.ppermute(values, "dp", ring_perm(lax.axis_size("dp")))
+
+
+def ring_total(blocks):
+    moving = blocks(lax.axis_size("dp") // 2 - 1)
+    for step in reversed(range(lax.axis_size("dp") // 2 - 1)):
+        moving = add(ring_step(moving), blocks(step))
+        if step:
+            moving = moving.astype(bf16)
+    return moving
 
 
 def halve_core(blocks, axis):
@@ -475,19 +521,12 @@
     return total
 
 
-def reduce_attention(values, pair_first, after=None):
-    dp, sides = lax.axis_size("dp"), lax.axis_size("expert")
-    cols = values.shape[1]
-    if dp > RING_MOST:
-        return lax.psum_scatter(values, ("dp", "expert"), scatter_dimension=0, tiled=True).astype(f32)
-    blocks = halve_core(values.reshape(dp // 2, 2, sides // 2, 2, -1, cols), 3)
-    if after is not None:
-        blocks, _ = tie(blocks, after)
-    if pair_first:
-        blocks = halve_line(halve_pair(blocks, 1), 1)
-    else:
-        blocks = halve_pair(halve_line(blocks, 2), 1)
-    return reduce_line(blocks)
+def attention_blocks(values):
+    return values.reshape(lax.axis_size("dp") // 2, 2, lax.axis_size("expert") // 2, 2, -1, values.shape[1])
+
+
+def reduce_everywhere(values):
+    return lax.psum_scatter(values, ("dp", "expert"), scatter_dimension=0, tiled=True).astype(f32)
 
 
 def on_device(
@@ -523,13 +562,15 @@
         )
         return jnp.transpose(pieces, (1, 0, 2)).reshape(shard_rows, EXPERTS * 2 * units)
 
-    attention_first, line_done, pair_done = gather_attention(attention_shards[0])
+    count = lax.axis_size("dp")
+    small = count <= RING_MOST
+    attention_first, events = gather_attention(attention_shards[0])
     attention_all = [
         attention_first,
         lax.all_gather(attention_shards[1], both, axis=0, tiled=True),
     ]
     experts_all = [
-        gather_rows(expert_shard(0), line_done, pair_done),
+        gather_rows(expert_shard(0), events),
         lax.all_gather(expert_shard(1), "dp", axis=0, tiled=True),
     ]
 
@@ -544,7 +585,9 @@
     )
     bias = jnp.where(allowed, 0.0, FAR).astype(f32)
 
-    last_grads = spread_slots(contract_rows(spot, cotangent.astype(bf16)).astype(bf16))
+    last_slots = contract_rows(spot, cotangent.astype(bf16)).astype(bf16)
+    last_slots, _ = tie(last_slots, events[2])
+    last_grads = spread_slots(last_slots)
 
     def shape_of(rows, cols, kind):
         return jax.ShapeDtypeStruct((rows, cols), kind)
@@ -569,31 +612,27 @@
         )(*([rows] if first else [rows, *parts]), spot, bias, weight)
         triple, logs, context, hidden, slots = outs[:5]
         inputs = tokens if first else outs[5]
+        if first:
+            slots, _ = tie(slots, last_grads[2])
         blocks = spread_slots(slots)
         sums, active, slope = expert_forward(blocks, experts_all[layer])
-        parts = collect_slots(sums)
+        if layer + 1 < LAYERS:
+            parts = collect_slots(sums)
         rows = hidden
         saved.append((inputs, triple, logs, context, hidden, blocks, active, slope, weight))
-    mixed = (rows + mat(spot, parts[0]) + mat(spot, parts[1])).astype(bf16)
-
-    grad = cotangent
-    grad_blocks = last_grads
-    results = [None] * LAYERS
-    for layer in reversed(range(LAYERS)):
-        inputs, triple, logs, context, hidden, blocks, active, slope, weight = saved[layer]
+    final_near, final_far = collect_core(sums)
+
+    def expert_part(layer, grads, split):
+        blocks, active, slope = saved[layer][5:8]
+        return expert_backward(grads, blocks, active, slope, experts_all[layer], split)
+
+    def attend_part(layer, parts, grad):
+        inputs, triple, logs, context, hidden = saved[layer][:5]
+        weight = saved[layer][8]
         last = layer == 0
-        sums, expert_grads = expert_backward(
-            grad_blocks, blocks, active, slope, experts_all[layer], False
-        )
-        total = lax.psum_scatter(expert_grads[0], "dp", scatter_dimension=0, tiled=True)
-        total = total.astype(f32).reshape(shard_rows, EXPERTS, 2 * units)
-        expert_totals = [total[:, expert] for expert in range(EXPERTS)]
-        parts = collect_slots(sums)
-        grad_widths = [2 * width, 2 * width + PAIR] if last else [4 * width + PAIR]
-        outs = whole_call(
+        return whole_call(
             partial(attend_backward_body, last),
-            [shape_of(row_count, width, f32)]
-            + [shape_of(width, cols, bf16) for cols in grad_widths]
+            [shape_of(row_count, width, f32), shape_of(width, 4 * width + PAIR, bf16)]
             + ([] if last else [shape_of(SLOTS, width, bf16)]),
             scratch_shapes=[
                 pltpu.VMEM((row_count, width), bf16),
@@ -601,34 +640,74 @@
             ],
             name="attend_backward",
         )(*parts, grad, hidden, inputs, triple, logs, context, spot, bias, weight)
-        grad = outs[0]
-        if last:
-            attention_total = jnp.concatenate(
-                [reduce_attention(outs[1], False), reduce_attention(outs[2], True)], 1
-            )
-        else:
-            grad_blocks = spread_slots(outs[2])
-            attention_total = reduce_attention(outs[1], False, grad_blocks[2])
-        results[layer] = (attention_total, expert_totals)
-
-    def columns(layer, start, stop):
-        return results[layer][0][:, start:stop]
-
-    deltas = [
-        jnp.stack([columns(layer, i * width, (i + 1) * width) for layer in range(LAYERS)])
-        for i in range(4)
-    ]
-    gain_deltas = [
-        jnp.stack([columns(layer, 4 * width + i, 4 * width + i + 1)[:, 0] for layer in range(LAYERS)])
-        for i in range(2)
-    ]
-    delta_in = jnp.stack(
-        [jnp.stack([piece[:, :units] for piece in results[layer][1]]) for layer in range(LAYERS)]
-    )
-    delta_out = jnp.stack(
-        [jnp.stack([piece[:, units:].T for piece in results[layer][1]]) for layer in range(LAYERS)]
-    )
-    return (mixed, grad, *deltas, *gain_deltas, delta_in, delta_out)
+
+    def offload(values):
+        return lax.psum_scatter(values, "dp", scatter_dimension=0, tiled=True)
+
+    together = tuple((0, 2 * units * expert) for expert in range(EXPERTS))
+    if small:
+        sums, (whole,) = expert_part(1, last_grads, False)
+        second_experts = offload(whole)
+        parts = collect_slots(sums)
+        outs = attend_part(1, parts, cotangent)
+        held = halve_core(attention_blocks(outs[1]), 3)
+        grad_blocks = spread_slots(outs[2])
+        *grad_blocks, held = tie(*grad_blocks, held)
+        held = halve_line(held, 2)
+        sums, pairs = expert_part(0, grad_blocks, True)
+        *sums, held = tie(*sums, held)
+        kepts = list(pairs[::2])
+        gots = [swap_pair(sent) for sent in pairs[1::2]]
+        parts = collect_slots(sums)
+        outs = attend_part(0, parts, outs[0])
+        whole, held, gots[0], gots[1], second_experts = tie(
+            outs[1], held, gots[0], gots[1], second_experts
+        )
+        second_total = reduce_line(halve_pair(held, 1))
+
+        def block(expert, step):
+            return add(kepts[expert][step], gots[expert][step]).astype(bf16)
+
+        def onward(expert, moving, step):
+            return add(moving, block(expert, step)).astype(bf16)
+
+        blocks = halve_core(attention_blocks(whole), 3)
+        blocks, kepts[0] = tie(blocks, kepts[0])
+        blocks = halve_line(blocks, 2)
+        one = ring_step(block(0, 3))
+        one, kepts[1] = tie(one, kepts[1])
+        one = ring_step(onward(0, one, 2))
+        two = ring_step(block(1, 3))
+        two, kepts[2], final_far = tie(two, kepts[2], final_far)
+        final_far = swap(final_far, 2)
+        first_total = reduce_line(halve_pair(blocks, 1))
+        one = add(ring_step(onward(0, one, 1)), block(0, 0))
+        two = ring_step(onward(1, two, 2))
+        two = add(ring_step(onward(1, two, 1)), block(1, 0))
+        three = ring_step(block(2, 3))
+        three = ring_step(onward(2, three, 2))
+        three = add(ring_step(onward(2, three, 1)), block(2, 0))
+        first_experts = [one, two, three]
+        places = (tuple((expert, 0) for expert in range(EXPERTS)), together)
+    else:
+        sums, (whole,) = expert_part(1, last_grads, False)
+        second_experts = offload(whole)
+        outs = attend_part(1, collect_slots(sums), cotangent)
+        second_total = reduce_everywhere(outs[1])
+        sums, (whole,) = expert_part(0, spread_slots(outs[2]), False)
+        first_experts = [offload(whole)]
+        outs = attend_part(0, collect_slots(sums), outs[0])
+        first_total = reduce_everywhere(outs[1])
+        final_far = swap(final_far, 2)
+        places = (together, together)
+    mixed = (rows + mat(spot, final_near) + mat(spot, final_far)).astype(bf16)
+    square = jax.ShapeDtypeStruct((LAYERS, own_rows, width), f32)
+    line = jax.ShapeDtypeStruct((LAYERS, own_rows), f32)
+    wide = jax.ShapeDtypeStruct((LAYERS, EXPERTS, shard_rows, units), f32)
+    deltas = whole_call(
+        partial(finish_body, places), [square] * 4 + [line] * 2 + [wide] * 2, name="finish"
+    )(*first_experts, first_total, second_experts, second_total)
+    return (mixed, outs[0], *deltas[:7], jnp.swapaxes(deltas[7], 2, 3))
 
 
 def solution(mesh):

time: 560 us -> 535 us (0.955)
  waiting for transfers between devices: 279 us -> 254 us
  local copies, waits for them, and re-layouts: 46.4 us -> 33.6 us
  Pallas kernels: 130 us -> 139 us
  starting transfers between devices: 56.2 us -> 62.9 us
    ppermute x0 -> x12, waiting for transfers between devices: none -> 63.2 us  [the longest x9 43.2 us: ring_step(): return lax.ppermute(values, 'dp', ring_perm(lax.axis_size('dp')))]
    reduce_scatter x2 -> x1, waiting for transfers between devices: 47.9 us -> 0.01 us  [offload(): return lax.psum_scatter(values, 'dp', scatter_dimension=0, tiled=True)]
    ppermute x9 -> x6, waiting for transfers between devices: 44.8 us -> 13.2 us  [reduce_line(): lax.ppermute(sent, 'dp', shift_perm(count, step)).astype(f32)]
    ppermute x3, waiting for transfers between devices: 40.8 us -> 28.5 us  [gather_rows(): moving = lax.ppermute(moving, 'dp', ring_perm(count))]
    ppermute x0 -> x12, starting transfers between devices: none -> 11.1 us  [the longest x9 8.24 us: ring_step(): return lax.ppermute(values, 'dp', ring_perm(lax.axis_size('dp')))]
    ppermute x33 -> x31, waiting for transfers between devices: 97.6 us -> 106 us  [swap(): return lax.ppermute(values, 'expert', [(i, i ^ flip) for i in range(count)])]
    dynamic_update_slice x10, local copies, waits for them, and re-layouts: 8.51 us -> 0.86 us  [put(): return lax.dynamic_update_index_in_dim(values, piece, at, axis)]
    another operation x12 -> x1, other arithmetic: 7.67 us -> 0.58 us  [expert_backward(): jnp.stack([me // 2, lax.rem(me, 2)]).astype(jnp.int32)]
  transfers between devices with their start and end apart: 60 -> 65, of which waited for: 27 -> 34; matrix products, arithmetic and copies ran while one was open for 10% -> 8% of each run, Pallas kernels for 20% -> 22%
where the time goes in v3:
time: 535 us; the launch traced here: 529 us
  waiting for transfers between devices  254 us (47%)
  Pallas kernels  139 us (26%)
  starting transfers between devices  62.9 us (12%)
  local copies, waits for them, and re-layouts  33.6 us (6%)
  other arithmetic  20.5 us (4%)
  between operations  14.9 us (3%)
    ppermute x31, waiting for transfers between devices, swap(): return lax.ppermute(values, 'expert', [(i, i ^ flip) for i in range(count)])  106 us
    pallas_call x2, Pallas kernels, attend_part(): whole_call(partial(attend_backward_body, last), [shape_of(row_count, widt...  47 us
    ppermute x9, waiting for transfers between devices, ring_step(): return lax.ppermute(values, 'dp', ring_perm(lax.axis_size('dp')))  43.2 us
    pallas_call x2, Pallas kernels, expert_backward(): pl.pallas_call(partial(expert_backward_body, split), grid_spec=pltpu.Pref...  36.9 us
    pallas_call x2, Pallas kernels, on_device(): whole_call(partial(attend_forward_body, first), [shape_of(row_count, 3 *...  29.2 us
    ppermute x3, waiting for transfers between devices, gather_rows(): moving = lax.ppermute(moving, 'dp', ring_perm(count))  28.5 us
    pallas_call x2, Pallas kernels, expert_forward(): pl.pallas_call(expert_forward_body, grid=(EXPERTS,), in_specs=[block] * 4...  20.6 us
    ppermute x3, waiting for transfers between devices, swap_pair(): return lax.ppermute(values, 'dp', pair_perm(lax.axis_size('dp')))  20.1 us
  transfers between devices with their start and end apart: 65, of which 34 were waited for; matrix products, arithmetic and copies ran while one was open for 8% of the time, Pallas kernels for 22%

profile of v3, /device:TPU:0, one launch (start us, length us, event | category | flops | bytes accessed | tf_op | source)
XLA Modules:
  0.0 528.9 jit_solution(1667290290102275706)
XLA Ops:
  9.2 3.1 collective-permute-start
  12.3 2.6 collective-permute-start.1
  26.8 5.0 collective-permute-start.12
  32.0 9.0 %collective-permute-done.3 = bf16[4,24,3200]{2,1,0:T(8,128)(2,1)S(1)} collective-permute-done((bf16[4,24,3200]{2,1,0:T(8,128)(2,1)S(1)}, bf16[4,24,3200]{2,1,0:T(8,128)(2,1)S(1)}, u32[]{:S(2)}, u32[]{:S(2)}) %collective-permute-start.3) | collective-permute-done | bytes 614432 | tf_op jit(solution)/shard_map/ppermute | solution.py:458
  47.0 11.9 %collective-permute-done.12 = bf16[96,4608]{1,0:T(8,128)(2,1)S(1)} collective-permute-done((bf16[96,4608]{1,0:T(8,128)(2,1)}, bf16[96,4608]{1,0:T(8,128)(2,1)S(1)}, u32[]{:S(2)}, u32[]{:S(2)}) %collective-permute-start.12) | collective-permute-done | bytes 884768 | tf_op jit(solution)/shard_map/ppermute | solution.py:420
  60.9 20.2 %collective-permute-done.5 = bf16[4,2,24,3200]{3,2,1,0:T(8,128)(2,1)S(1)} collective-permute-done((bf16[4,2,24,3200]{3,2,1,0:T(8,128)(2,1)S(1)}, bf16[4,2,24,3200]{3,2,1,0:T(8,128)(2,1)S(1)}, u32[]{:S(2)}, u32[]{:S(2)}) %collective-permute-start.5) | collective-permute-done | bytes 1228832 | tf_op jit(solution)/shard_map/ppermute | solution.py:369
  81.5 13.0 %collective-permute-done.14 = bf16[96,4608]{1,0:T(8,128)(2,1)} collective-permute-done((bf16[96,4608]{1,0:T(8,128)(2,1)S(1)}, bf16[96,4608]{1,0:T(8,128)(2,1)}, u32[]{:S(2)}, u32[]{:S(2)}) %collective-permute-start.14) | collective-permute-done | bytes 884768 | tf_op jit(solution)/shard_map/ppermute | solution.py:420
  100.1 14.1 %attend_forward.2 = (bf16[384,2304]{1,0:T(8,128)(2,1)}, f32[384,128]{1,0:T(8,128)}, bf16[384,768]{1,0:T(8,128)(2,1)}, f32[384,768]{1,0:T(8,128)}, bf16[432,768]{1,0:T(8,128)(2,1)}) custom-call(bf16[384,768]{1,0:T(8,128)(2,1)} %refs_4_.3, bf16[384,432]{1,0:T(8,128)(2,1)} %fusion.9.refs_1_.refs_3_.refs_8_, f32[384,384]{1,0:T(8,128)} %fusion.20.refs_2_.refs_4_.refs_9_, ...), custom_call_target="tpu_custom_call" | custom-call | flops 1500000 | bytes 1500 | tf_op jit(solution)/shard_map/attend_forward/pallas_call | solution.py:601
  117.1 7.4 %collective-permute-done.15 = bf16[96,4608]{1,0:T(8,128)(2,1)} collective-permute-done((bf16[96,4608]{1,0:T(8,128)(2,1)}, bf16[96,4608]{1,0:T(8,128)(2,1)}, u32[]{:S(2)}, u32[]{:S(2)}) %collective-permute-start.15) | collective-permute-done | bytes 884768 | tf_op jit(solution)/shard_map/ppermute | solution.py:415
  124.5 3.6 collective-permute-done.16
  131.2 11.0 %collective-permute-done.17 = bf16[96,4608]{1,0:T(8,128)(2,1)S(1)} collective-permute-done((bf16[96,4608]{1,0:T(8,128)(2,1)}, bf16[96,4608]{1,0:T(8,128)(2,1)S(1)}, u32[]{:S(2)}, u32[]{:S(2)}) %collective-permute-start.17) | collective-permute-done | bytes 884768 | tf_op jit(solution)/shard_map/ppermute | solution.py:415
  143.1 2.2 copy-done
  145.3 10.4 %expert_forward.2 = (bf16[432,768]{1,0:T(8,128)(2,1)}, bf16[432,768]{1,0:T(8,128)(2,1)}, bf16[432,768]{1,0:T(8,128)(2,1)}, bf16[432,768]{1,0:T(8,128)(2,1)}, bf1...) custom-call(bf16[432,768]{1,0:T(8,128)(2,1)} %get-tuple-element.99.refs_0_.refs_5_, bf16[432,768]{1,0:T(8,128)(2,1)} %copy-done.8, ...), custom_call_target="tpu_custom_call" | custom-call | flops 1000000 | bytes 1000 | tf_op jit(solution)/shard_map/expert_forward/pallas_call | solution.py:314
  162.1 14.3 %collective-permute-done.20.refs_2_ = bf16[432,768]{1,0:T(8,128)(2,1)S(1)} collective-permute-done((bf16[432,768]{1,0:T(8,128)(2,1)S(1)}, bf16[432,768]{1,0:T(8,128)(2,1)S(1)}, u32[]{:S(2)}, u32[]{:S(2)}) %collective-permute-start.20) | collective-permute-done | bytes 663584 | tf_op jit(solution)/shard_map/ppermute | solution.py:369
  177.3 15.0 %attend_forward.3 = (bf16[384,2304]{1,0:T(8,128)(2,1)}, f32[384,128]{1,0:T(8,128)}, bf16[384,768]{1,0:T(8,128)(2,1)}, f32[384,768]{1,0:T(8,128)}, bf16[432,768]{1,0:T(8,128)(2,1)}, /*index=5*/f32[384,768]{1,0:T(8,128)}) custom-call(f32[384,768]{1,0:T(8,128)} %get-tuple-element.96.refs_0_.refs_3_, bf16[432,768]{1,0:T(8,128)(2,1)} %add_convert_fusion.7.refs_1_, ...), custom_call_target="tpu_custom_call" | custom-call | flops 1500000 | bytes 1500 | tf_op jit(solution)/shard_map/attend_forward/pallas_call | solution.py:601
  193.9 14.8 %collective-permute-done.22.refs_2_.refs_7_ = bf16[432,768]{1,0:T(8,128)(2,1)S(1)} collective-permute-done((bf16[432,768]{1,0:T(8,128)(2,1)}, bf16[432,768]{1,0:T(8,128)(2,1)S(1)}, u32[]{:S(2)}, u32[]{:S(2)}) %collective-permute-start.22) | collective-permute-done | bytes 663584 | tf_op jit(solution)/shard_map/ppermute | solution.py:369
  212.6 10.1 %expert_forward.3 = (bf16[432,768]{1,0:T(8,128)(2,1)}, bf16[432,768]{1,0:T(8,128)(2,1)}, bf16[432,768]{1,0:T(8,128)(2,1)}, bf16[432,768]{1,0:T(8,128)(2,1)}, bf1...) custom-call(bf16[432,768]{1,0:T(8,128)(2,1)} %get-tuple-element.114.refs_0_.refs_5_, bf16[432,768]{1,0:T(8,128)(2,1)} %copy-done.10, ...), custom_call_target="tpu_custom_call" | custom-call | flops 1000000 | bytes 1000 | tf_op jit(solution)/shard_map/expert_forward/pallas_call | solution.py:314
  223.9 16.0 %expert_backward.2 = (bf16[432,768]{1,0:T(8,128)(2,1)}, bf16[432,768]{1,0:T(8,128)(2,1)}, bf16[432,768]{1,0:T(8,128)(2,1)}, bf16[432,768]{1,0:T(8,128)(2,1)}, bf16[768,4608]{1,0:T(8,128)(2,1)}) custom-call(s32[2]{0:T(128)} %pad_add_fusion.refs_0_, bf16[432,768]{1,0:T(8,128)(2,1)} %convolution_convert_fusion.refs_1_, bf16[432,768]{1,0:T(8,128)(2,1)} %copy-done.19, ...), custom_call_target="tpu_custom_call" | custom-call | flops 1600000 | bytes 1600 | tf_op jit(solution)/shard_map/expert_backward/pallas_call | solution.py:344
  246.0 14.3 %collective-permute-done.29.refs_1_ = bf16[432,768]{1,0:T(8,128)(2,1)S(1)} collective-permute-done((bf16[432,768]{1,0:T(8,128)(2,1)S(1)}, bf16[432,768]{1,0:T(8,128)(2,1)S(1)}, u32[]{:S(2)}, u32[]{:S(2)}) %collective-permute-start.29) | collective-permute-done | bytes 663584 | tf_op jit(solution)/shard_map/ppermute | solution.py:369
  261.1 24.3 %attend_backward.2 = (f32[384,768]{1,0:T(8,128)}, bf16[768,3200]{1,0:T(8,128)(2,1)}, bf16[432,768]{1,0:T(8,128)(2,1)}) custom-call(bf16[432,768]{1,0:T(8,128)(2,1)} %add_convert_fusion.4.refs_0_, bf16[432,768]{1,0:T(8,128)(2,1)} %copy-done.21, f32[384,768]{1,0:T(8,128)} %refs_2_.3, f32[384,768]{1,0:T(8,128)} %get-tuple-element.113.refs_3_, ...), custom_call_target="tpu_custom_call" | custom-call | flops 1500000 | bytes 1500 | tf_op jit(solution)/shard_map/attend_backward/pallas_call | solution.py:633
  285.4 3.0 constant_dynamic-slice_fusion.3
  291.9 15.6 %collective-permute-done.31.refs_3_ = bf16[432,768]{1,0:T(8,128)(2,1)} collective-permute-done((bf16[432,768]{1,0:T(8,128)(2,1)S(1)}, bf16[432,768]{1,0:T(8,128)(2,1)}, u32[]{:S(2)}, u32[]{:S(2)}) %collective-permute-start.31) | collective-permute-done | bytes 663584 | tf_op jit(solution)/shard_map/ppermute | solution.py:369
  307.5 2.3 fusion.1
  313.7 20.9 %expert_backward.3 = (bf16[432,768]{1,0:T(8,128)(2,1)}, bf16[432,768]{1,0:T(8,128)(2,1)}, bf16[432,768]{1,0:T(8,128)(2,1)}, bf16[432,768]{1,0:T(8,128)(2,1)}, bf...) custom-call(s32[2]{0:T(128)} %pad_add_fusion.refs_0_, ...), custom_call_target="tpu_custom_call" | custom-call | flops 1600000 | bytes 1600 | tf_op jit(solution)/shard_map/expert_backward/pallas_call | solution.py:344
  334.7 7.0 %collective-permute-done.34 = bf16[4,2,24,3200]{3,2,0,1:T(8,128)(2,1)S(1)} collective-permute-done((bf16[4,2,24,3200]{3,2,0,1:T(8,128)(2,1)S(1)}, bf16[4,2,24,3200]{3,2,0,1:T(8,128)(2,1)S(1)}, u32[]{:S(2)}, u32[]{:S(2)}) %collective-permute-start.34) | collective-permute-done | bytes 1228832 | tf_op jit(solution)/shard_map/ppermute | solution.py:369
  347.3 14.5 %collective-permute-done.37.refs_1_ = bf16[432,768]{1,0:T(8,128)(2,1)S(1)} collective-permute-done((bf16[432,768]{1,0:T(8,128)(2,1)S(1)}, bf16[432,768]{1,0:T(8,128)(2,1)S(1)}, u32[]{:S(2)}, u32[]{:S(2)}) %collective-permute-start.37) | collective-permute-done | bytes 663584 | tf_op jit(solution)/shard_map/ppermute | solution.py:369
  362.6 22.8 %attend_backward.3 = (f32[384,768]{1,0:T(8,128)}, bf16[768,3200]{1,0:T(8,128)(2,1)}) custom-call(bf16[432,768]{1,0:T(8,128)(2,1)} %add_convert_fusion.2.refs_0_, bf16[432,768]{1,0:T(8,128)(2,1)} %copy-done.29, f32[384,768]{1,0:T(8,128)} %get-tuple-element.144.refs_2_, f32[384,768]{1,0:T(8,128)} %get-tuple-element.96.refs_0_.refs_3_, ...), custom_call_target="tpu_custom_call" | custom-call | flops 1500000 | bytes 1500 | tf_op jit(solution)/shard_map/attend_backward/pallas_call | solution.py:633
  385.4 20.1 %collective-permute-done.39 = bf16[4,96,1536]{2,1,0:T(8,128)(2,1)S(1)} collective-permute-done((bf16[4,96,1536]{2,1,0:T(8,128)(2,1)}, bf16[4,96,1536]{2,1,0:T(8,128)(2,1)S(1)}, u32[]{:S(2)}, u32[]{:S(2)}) %collective-permute-start.39) | collective-permute-done | bytes 1179680 | tf_op jit(solution)/shard_map/ppermute | solution.py:479
  407.7 2.8 constant_dynamic-slice_fusion.1
  410.8 10.6 %collective-permute-done.58 = bf16[4,24,3200]{2,1,0:T(8,128)(2,1)S(1)} collective-permute-done((bf16[4,24,3200]{2,1,0:T(8,128)(2,1)S(1)}, bf16[4,24,3200]{2,1,0:T(8,128)(2,1)S(1)}, u32[]{:S(2)}, u32[]{:S(2)}) %collective-permute-start.58) | collective-permute-done | bytes 614432 | tf_op jit(solution)/shard_map/ppermute | solution.py:509
  421.5 2.9 collective-permute-start.59
  424.5 2.3 collective-permute-start.60
  428.4 2.9 collective-permute-done.59
  432.1 4.0 collective-permute-done.60
  439.3 3.8 collective-permute-start.41
  444.7 5.2 collective-permute-done.41
  453.5 8.3 %collective-permute-done.42 = bf16[96,1536]{1,0:T(8,128)(2,1)S(1)} collective-permute-done((bf16[96,1536]{1,0:T(8,128)(2,1)S(1)}, bf16[96,1536]{1,0:T(8,128)(2,1)S(1)}, u32[]{:S(2)}, u32[]{:S(2)}) %collective-permute-start.42) | collective-permute-done | bytes 294944 | tf_op jit(solution)/shard_map/ppermute | solution.py:483
  462.7 5.5 %collective-permute-done.45 = bf16[96,1536]{1,0:T(8,128)(2,1)S(1)} collective-permute-done((bf16[96,1536]{1,0:T(8,128)(2,1)S(1)}, bf16[96,1536]{1,0:T(8,128)(2,1)S(1)}, u32[]{:S(2)}, u32[]{:S(2)}) %collective-permute-start.45) | collective-permute-done | bytes 294944 | tf_op jit(solution)/shard_map/ppermute | solution.py:483
  469.7 4.7 collective-permute-done.50
  476.0 4.7 collective-permute-done.47
  481.2 5.9 %collective-permute-done.46 = bf16[96,1536]{1,0:T(8,128)(2,1)S(1)} collective-permute-done((bf16[96,1536]{1,0:T(8,128)(2,1)S(1)}, bf16[96,1536]{1,0:T(8,128)(2,1)S(1)}, u32[]{:S(2)}, u32[]{:S(2)}) %collective-permute-start.46) | collective-permute-done | bytes 294944 | tf_op jit(solution)/shard_map/ppermute | solution.py:483
  489.2 4.2 collective-permute-done.51
  495.2 4.6 collective-permute-done.48
  502.7 3.5 collective-permute-done.54
  507.4 2.4 collective-permute-start.56
  511.3 2.3 collective-permute-done.55
  513.6 4.0 collective-permute-done.56
  518.3 3.9 finish.1
  (252 shorter events, 97.3 us)
Async XLA Ops:
  7.2 169.2 %all-gather.3.cloned.1.call-start = ((), (), s32[]{:S(2)}) async-start(), calls=%async_computation.1 | async-start | bytes 5068800 | tf_op jit(solution)/shard_map/all_gather | solution.py:570
  9.1 202.6 %all-gather.5.cloned.1.call-start = ((), (), s32[]{:S(2)}) async-start(), calls=%async_computation.2 | async-start | bytes 7962624 | tf_op jit(solution)/shard_map/all_gather | solution.py:574
  9.2 14.5 %collective-permute-start = (bf16[24,3200]{1,0:T(8,128)(2,1)}, bf16[24,3200]{1,0:T(8,128)(2,1)S(1)}, u32[]{:S(2)}, u32[]{:S(2)}) collective-permute-start(bf16[24,3200]{1,0:T(8,128)(2,1)} %get-tuple-element.95), channel_id=1, source_target_pairs={{0,8},{4,12},{8,16},{12,20},{16,24},{20,28},{24,0},{28,4},{1,9},{5... | collective-permute-start | bytes 460808 | tf_op jit(solution)/shard_map/ppermute | solution.py:456
  12.3 12.9 %collective-permute-start.1 = (bf16[24,3200]{1,0:T(8,128)(2,1)}, bf16[24,3200]{1,0:T(8,128)(2,1)S(1)}, u32[]{:S(2)}, u32[]{:S(2)}) collective-permute-start(bf16[24,3200]{1,0:T(8,128)(2,1)} %get-tuple-element.95), channel_id=1, source_target_pairs={{0,16},{4,20},{8,24},{12,28},{16,0},{20,4},{24,8},{28,12},{1,17},{... | collective-permute-start | bytes 460808 | tf_op jit(solution)/shard_map/ppermute | solution.py:456
  18.7 386.8 %reduce-scatter.2.cloned.1.call-start = ((), (), s32[]{:S(2)}) async-start(), calls=%async_computation.3 | async-start | bytes 7962624 | tf_op jit(solution)/shard_map/reduce_scatter | solution.py:645
  25.2 15.8 %collective-permute-start.3 = (bf16[4,24,3200]{2,1,0:T(8,128)(2,1)S(1)}, bf16[4,24,3200]{2,1,0:T(8,128)(2,1)S(1)}, u32[]{:S(2)}, u32[]{:S(2)}) collective-permute-start(bf16[4,24,3200]{2,1,0:T(8,128)(2,1)S(1)} %bitcast_dynamic-update-slice_fusion.6), channel_id=1, source_target_pairs={{0,4},{4,0},{8,12},{12,8},{16,20},{20,16},{24,28},{28,24},{1,5},{5... | collective-permute-start | bytes 1843208 | tf_op jit(solution)/shard_map/ppermute | solution.py:458
  26.8 32.2 %collective-permute-start.12 = (bf16[96,4608]{1,0:T(8,128)(2,1)}, bf16[96,4608]{1,0:T(8,128)(2,1)S(1)}, u32[]{:S(2)}, u32[]{:S(2)}) collective-permute-start(bf16[96,4608]{1,0:T(8,128)(2,1)} %bitcast.84), channel_id=1, source_target_pairs={{0,8},{4,12},{8,16},{12,20},{16,24},{20,28},{24,0},{28,4},{1,9},{5... | collective-permute-start | bytes 2654216 | tf_op jit(solution)/shard_map/ppermute | solution.py:420
  41.1 40.0 %collective-permute-start.5 = (bf16[4,2,24,3200]{3,2,1,0:T(8,128)(2,1)S(1)}, bf16[4,2,24,3200]{3,2,1,0:T(8,128)(2,1)S(1)}, u32[]{:S(2)}, u32[]{:S(2)}) collective-permute-start(bf16[4,2,24,3200]{3,2,1,0:T(8,128)(2,1)S(1)} %bitcast_dynamic-update-slice_fusion.5), channel_id=1, source_target_pairs={{0,2},{1,3},{2,0},{3,1},{4,6},{5,7},{6,4},{7,5},{8,10},{9,11},{10,... | collective-permute-start | bytes 3686408 | tf_op jit(solution)/shard_map/ppermute | solution.py:369
  42.6 38.6 %collective-permute-start.4 = (bf16[4,2,24,3200]{3,2,1,0:T(8,128)(2,1)S(1)}, bf16[4,2,24,3200]{3,2,1,0:T(8,128)(2,1)S(1)}, u32[]{:S(2)}, u32[]{:S(2)}) collective-permute-start(bf16[4,2,24,3200]{3,2,1,0:T(8,128)(2,1)S(1)} %bitcast_dynamic-update-slice_fusion.5), channel_id=1, source_target_pairs={{0,1},{1,0},{2,3},{3,2},{4,5},{5,4},{6,7},{7,6},{8,9},{9,8},{10,11... | collective-permute-start | bytes 3686408 | tf_op jit(solution)/shard_map/ppermute | solution.py:369
  44.3 51.8 %collective-permute-start.11 = (bf16[96,4608]{1,0:T(8,128)(2,1)}, bf16[96,4608]{1,0:T(8,128)(2,1)S(1)}, u32[]{:S(2)}, u32[]{:S(2)}) collective-permute-start(bf16[96,4608]{1,0:T(8,128)(2,1)} %bitcast.84), channel_id=1, source_target_pairs={{0,4},{4,0},{8,12},{12,8},{16,20},{20,16},{24,28},{28,24},{1,5},{5... | collective-permute-start | bytes 2654216 | tf_op jit(solution)/shard_map/ppermute | solution.py:415
  58.9 41.1 %collective-permute-start.13 = (bf16[96,4608]{1,0:T(8,128)(2,1)S(1)}, bf16[96,4608]{1,0:T(8,128)(2,1)}, u32[]{:S(2)}, u32[]{:S(2)}) collective-permute-start(bf16[96,4608]{1,0:T(8,128)(2,1)S(1)} %collective-permute-done.12), channel_id=1, source_target_pairs={{0,4},{4,0},{8,12},{12,8},{16,20},{20,16},{24,28},{28,24},{1,5},{5... | collective-permute-start | bytes 2654216 | tf_op jit(solution)/shard_map/ppermute | solution.py:415
  59.6 34.8 %collective-permute-start.14 = (bf16[96,4608]{1,0:T(8,128)(2,1)S(1)}, bf16[96,4608]{1,0:T(8,128)(2,1)}, u32[]{:S(2)}, u32[]{:S(2)}) collective-permute-start(bf16[96,4608]{1,0:T(8,128)(2,1)S(1)} %collective-permute-done.12), channel_id=1, source_target_pairs={{0,8},{4,12},{8,16},{12,20},{16,24},{20,28},{24,0},{28,4},{1,9},{5... | collective-permute-start | bytes 2654216 | tf_op jit(solution)/shard_map/ppermute | solution.py:420
  81.1 13.3 %collective-permute-start.6 = (bf16[4,2,24,3200]{3,2,1,0:T(8,128)(2,1)S(1)}, bf16[4,2,24,3200]{3,2,1,0:T(8,128)(2,1)S(1)}, u32[]{:S(2)}, u32[]{:S(2)}) collective-permute-start(bf16[4,2,24,3200]{3,2,1,0:T(8,128)(2,1)S(1)} %collective-permute-done.5), channel_id=1, source_target_pairs={{0,1},{1,0},{2,3},{3,2},{4,5},{5,4},{6,7},{7,6},{8,9},{9,8},{10,11... | collective-permute-start | bytes 3686408 | tf_op jit(solution)/shard_map/ppermute | solution.py:369
  94.4 30.0 %collective-permute-start.15 = (bf16[96,4608]{1,0:T(8,128)(2,1)}, bf16[96,4608]{1,0:T(8,128)(2,1)}, u32[]{:S(2)}, u32[]{:S(2)}) collective-permute-start(bf16[96,4608]{1,0:T(8,128)(2,1)} %collective-permute-done.14), channel_id=1, source_target_pairs={{0,4},{4,0},{8,12},{12,8},{16,20},{20,16},{24,28},{28,24},{1,5},{5... | collective-permute-start | bytes 2654216 | tf_op jit(solution)/shard_map/ppermute | solution.py:415
  96.1 31.9 %collective-permute-start.16 = (bf16[96,4608]{1,0:T(8,128)(2,1)}, bf16[96,4608]{1,0:T(8,128)(2,1)}, u32[]{:S(2)}, u32[]{:S(2)}) collective-permute-start(bf16[96,4608]{1,0:T(8,128)(2,1)} %collective-permute-done.14), channel_id=1, source_target_pairs={{0,8},{4,12},{8,16},{12,20},{16,24},{20,28},{24,0},{28,4},{1,9},{5... | collective-permute-start | bytes 2654216 | tf_op jit(solution)/shard_map/ppermute | solution.py:420
  96.1 19.3 %collective-permute-start.7 = (bf16[432,768]{1,0:T(8,128)(2,1)}, bf16[432,768]{1,0:T(8,128)(2,1)}, u32[]{:S(2)}, u32[]{:S(2)}) collective-permute-start(bf16[432,768]{1,0:T(8,128)(2,1)} %convolution_convert_fusion.refs_1_), channel_id=1, source_target_pairs={{0,2},{1,3},{2,0},{3,1},{4,6},{5,7},{6,4},{7,5},{8,10},{9,11},{10,... | collective-permute-start | bytes 1990664 | tf_op jit(solution)/shard_map/ppermute | solution.py:369
  115.5 14.2 %collective-permute-start.9 = (bf16[432,768]{1,0:T(8,128)(2,1)S(1)}, bf16[432,768]{1,0:T(8,128)(2,1)S(1)}, u32[]{:S(2)}, u32[]{:S(2)}) collective-permute-start(bf16[432,768]{1,0:T(8,128)(2,1)S(1)} %copy-done.6), channel_id=1, source_target_pairs={{0,2},{1,3},{2,0},{3,1},{4,6},{5,7},{6,4},{7,5},{8,10},{9,11},{10,... | collective-permute-start | bytes 1990664 | tf_op jit(solution)/shard_map/ppermute | solution.py:369
  117.0 25.2 %collective-permute-start.8 = (bf16[432,768]{1,0:T(8,128)(2,1)S(1)}, bf16[432,768]{1,0:T(8,128)(2,1)S(1)}, u32[]{:S(2)}, u32[]{:S(2)}) collective-permute-start(bf16[432,768]{1,0:T(8,128)(2,1)S(1)} %copy-done.6), channel_id=1, source_target_pairs={{0,1},{1,0},{2,3},{3,2},{4,5},{5,4},{6,7},{7,6},{8,9},{9,8},{10,11... | collective-permute-start | bytes 1990664 | tf_op jit(solution)/shard_map/ppermute | solution.py:369
  128.0 14.1 %collective-permute-start.17 = (bf16[96,4608]{1,0:T(8,128)(2,1)}, bf16[96,4608]{1,0:T(8,128)(2,1)S(1)}, u32[]{:S(2)}, u32[]{:S(2)}) collective-permute-start(bf16[96,4608]{1,0:T(8,128)(2,1)} %collective-permute-done.16), channel_id=1, source_target_pairs={{0,4},{4,0},{8,12},{12,8},{16,20},{20,16},{24,28},{28,24},{1,5},{5... | collective-permute-start | bytes 2654216 | tf_op jit(solution)/shard_map/ppermute | solution.py:415
  129.7 13.4 %collective-permute-start.10 = (bf16[432,768]{1,0:T(8,128)(2,1)S(1)}, bf16[432,768]{1,0:T(8,128)(2,1)}, u32[]{:S(2)}, u32[]{:S(2)}) collective-permute-start(bf16[432,768]{1,0:T(8,128)(2,1)S(1)} %collective-permute-done.9.refs_2_.refs_7_), channel_id=1, source_target_pairs={{0,1},{1,0},{2,3},{3,2},{4,5},{5,4},{6,7},{7,6},{8,9},{9,8},{10,11... | collective-permute-start | bytes 1990664 | tf_op jit(solution)/shard_map/ppermute | solution.py:369
  159.4 17.0 %collective-permute-start.20 = (bf16[432,768]{1,0:T(8,128)(2,1)S(1)}, bf16[432,768]{1,0:T(8,128)(2,1)S(1)}, u32[]{:S(2)}, u32[]{:S(2)}) collective-permute-start(bf16[432,768]{1,0:T(8,128)(2,1)S(1)} %add_convert_fusion.6), channel_id=1, source_target_pairs={{0,2},{1,3},{2,0},{3,1},{4,6},{5,7},{6,4},{7,5},{8,10},{9,11},{10,... | collective-permute-start | bytes 1990664 | tf_op jit(solution)/shard_map/ppermute | solution.py:369
  192.3 16.4 %collective-permute-start.22 = (bf16[432,768]{1,0:T(8,128)(2,1)}, bf16[432,768]{1,0:T(8,128)(2,1)S(1)}, u32[]{:S(2)}, u32[]{:S(2)}) collective-permute-start(bf16[432,768]{1,0:T(8,128)(2,1)} %get-tuple-element.114.refs_0_.refs_5_), channel_id=1, source_target_pairs={{0,2},{1,3},{2,0},{3,1},{4,6},{5,7},{6,4},{7,5},{8,10},{9,11},{10,... | collective-permute-start | bytes 1990664 | tf_op jit(solution)/shard_map/ppermute | solution.py:369
  193.9 15.9 %collective-permute-start.21 = (bf16[432,768]{1,0:T(8,128)(2,1)}, bf16[432,768]{1,0:T(8,128)(2,1)S(1)}, u32[]{:S(2)}, u32[]{:S(2)}) collective-permute-start(bf16[432,768]{1,0:T(8,128)(2,1)} %get-tuple-element.114.refs_0_.refs_5_), channel_id=1, source_target_pairs={{0,1},{1,0},{2,3},{3,2},{4,5},{5,4},{6,7},{7,6},{8,9},{9,8},{10,11... | collective-permute-start | bytes 1990664 | tf_op jit(solution)/shard_map/ppermute | solution.py:369
  208.7 14.0 %collective-permute-start.25 = (bf16[432,768]{1,0:T(8,128)(2,1)}, bf16[432,768]{1,0:T(8,128)(2,1)S(1)}, u32[]{:S(2)}, u32[]{:S(2)}) collective-permute-start(bf16[432,768]{1,0:T(8,128)(2,1)} %convolution_convert_fusion.refs_1_), channel_id=1, source_target_pairs={{0,1},{1,0},{2,3},{3,2},{4,5},{5,4},{6,7},{7,6},{8,9},{9,8},{10,11... | collective-permute-start | bytes 1990664 | tf_op jit(solution)/shard_map/ppermute | solution.py:369
  209.2 13.5 %collective-permute-start.26 = (bf16[432,768]{1,0:T(8,128)(2,1)}, bf16[432,768]{1,0:T(8,128)(2,1)S(1)}, u32[]{:S(2)}, u32[]{:S(2)}) collective-permute-start(bf16[432,768]{1,0:T(8,128)(2,1)} %collective-permute-done.7.refs_3_), channel_id=1, source_target_pairs={{0,1},{1,0},{2,3},{3,2},{4,5},{5,4},{6,7},{7,6},{8,9},{9,8},{10,11... | collective-permute-start | bytes 1990664 | tf_op jit(solution)/shard_map/ppermute | solution.py:369
  243.3 17.0 %collective-permute-start.29 = (bf16[432,768]{1,0:T(8,128)(2,1)S(1)}, bf16[432,768]{1,0:T(8,128)(2,1)S(1)}, u32[]{:S(2)}, u32[]{:S(2)}) collective-permute-start(bf16[432,768]{1,0:T(8,128)(2,1)S(1)} %add_convert_fusion.3), channel_id=1, source_target_pairs={{0,2},{1,3},{2,0},{3,1},{4,6},{5,7},{6,4},{7,5},{8,10},{9,11},{10,... | collective-permute-start | bytes 1990664 | tf_op jit(solution)/shard_map/ppermute | solution.py:369
  290.1 17.4 %collective-permute-start.33 = (bf16[4,2,2,24,3200]{4,3,0,1,2:T(8,128)(2,1)}, bf16[4,2,2,24,3200]{4,3,0,1,2:T(8,128)(2,1)}, u32[]{:S(2)}, u32[]{:S(2)}) collective-permute-start(bf16[4,2,2,24,3200]{4,3,0,1,2:T(8,128)(2,1)} %bitcast.159), channel_id=1, source_target_pairs={{0,1},{1,0},{2,3},{3,2},{4,5},{5,4},{6,7},{7,6},{8,9},{9,8},{10,11... | collective-permute-start | bytes 7372808 | tf_op jit(solution)/shard_map/ppermute | solution.py:369
  290.1 17.4 %collective-permute-start.31 = (bf16[432,768]{1,0:T(8,128)(2,1)S(1)}, bf16[432,768]{1,0:T(8,128)(2,1)}, u32[]{:S(2)}, u32[]{:S(2)}) collective-permute-start(bf16[432,768]{1,0:T(8,128)(2,1)S(1)} %copy-done.16), channel_id=1, source_target_pairs={{0,2},{1,3},{2,0},{3,1},{4,6},{5,7},{6,4},{7,5},{8,10},{9,11},{10,... | collective-permute-start | bytes 1990664 | tf_op jit(solution)/shard_map/ppermute | solution.py:369
  291.6 18.1 %collective-permute-start.30 = (bf16[432,768]{1,0:T(8,128)(2,1)S(1)}, bf16[432,768]{1,0:T(8,128)(2,1)S(1)}, u32[]{:S(2)}, u32[]{:S(2)}) collective-permute-start(bf16[432,768]{1,0:T(8,128)(2,1)S(1)} %copy-done.16), channel_id=1, source_target_pairs={{0,1},{1,0},{2,3},{3,2},{4,5},{5,4},{6,7},{7,6},{8,9},{9,8},{10,11... | collective-permute-start | bytes 1990664 | tf_op jit(solution)/shard_map/ppermute | solution.py:369
  312.2 29.5 %collective-permute-start.34 = (bf16[4,2,24,3200]{3,2,0,1:T(8,128)(2,1)S(1)}, bf16[4,2,24,3200]{3,2,0,1:T(8,128)(2,1)S(1)}, u32[]{:S(2)}, u32[]{:S(2)}) collective-permute-start(bf16[4,2,24,3200]{3,2,0,1:T(8,128)(2,1)S(1)} %dynamic-slice_bitcast_fusion.1), channel_id=1, source_target_pairs={{0,2},{1,3},{2,0},{3,1},{4,6},{5,7},{6,4},{7,5},{8,10},{9,11},{10,... | collective-permute-start | bytes 3686408 | tf_op jit(solution)/shard_map/ppermute | solution.py:369
  342.1 43.3 %collective-permute-start.38 = (bf16[4,96,1536]{2,1,0:T(8,128)(2,1)}, bf16[4,96,1536]{2,1,0:T(8,128)(2,1)}, u32[]{:S(2)}, u32[]{:S(2)}) collective-permute-start(bf16[4,96,1536]{2,1,0:T(8,128)(2,1)} %get-tuple-element.150), channel_id=1, source_target_pairs={{0,4},{4,0},{8,12},{12,8},{16,20},{20,16},{24,28},{28,24},{1,5},{5... | collective-permute-start | bytes 3538952 | tf_op jit(solution)/shard_map/ppermute | solution.py:479
  343.8 61.6 %collective-permute-start.39 = (bf16[4,96,1536]{2,1,0:T(8,128)(2,1)}, bf16[4,96,1536]{2,1,0:T(8,128)(2,1)S(1)}, u32[]{:S(2)}, u32[]{:S(2)}) collective-permute-start(bf16[4,96,1536]{2,1,0:T(8,128)(2,1)} %get-tuple-element.151), channel_id=1, source_target_pairs={{0,4},{4,0},{8,12},{12,8},{16,20},{20,16},{24,28},{28,24},{1,5},{5... | collective-permute-start | bytes 3538952 | tf_op jit(solution)/shard_map/ppermute | solution.py:479
  344.3 17.4 %collective-permute-start.37 = (bf16[432,768]{1,0:T(8,128)(2,1)S(1)}, bf16[432,768]{1,0:T(8,128)(2,1)S(1)}, u32[]{:S(2)}, u32[]{:S(2)}) collective-permute-start(bf16[432,768]{1,0:T(8,128)(2,1)S(1)} %add_convert_fusion.1), channel_id=1, source_target_pairs={{0,2},{1,3},{2,0},{3,1},{4,6},{5,7},{6,4},{7,5},{8,10},{9,11},{10,... | collective-permute-start | bytes 1990664 | tf_op jit(solution)/shard_map/ppermute | solution.py:369
  405.5 15.9 %collective-permute-start.58 = (bf16[4,24,3200]{2,1,0:T(8,128)(2,1)S(1)}, bf16[4,24,3200]{2,1,0:T(8,128)(2,1)S(1)}, u32[]{:S(2)}, u32[]{:S(2)}) collective-permute-start(bf16[4,24,3200]{2,1,0:T(8,128)(2,1)S(1)} %dynamic-slice_bitcast_fusion.2), channel_id=1, source_target_pairs={{0,4},{4,0},{8,12},{12,8},{16,20},{20,16},{24,28},{28,24},{1,5},{5... | collective-permute-start | bytes 1843208 | tf_op jit(solution)/shard_map/ppermute | solution.py:509
  407.2 19.6 %collective-permute-start.43 = (bf16[432,768]{1,0:T(8,128)(2,1)}, bf16[432,768]{1,0:T(8,128)(2,1)S(1)}, u32[]{:S(2)}, u32[]{:S(2)}) collective-permute-start(bf16[432,768]{1,0:T(8,128)(2,1)} %get-tuple-element.162), channel_id=1, source_target_pairs={{0,1},{1,0},{2,3},{3,2},{4,5},{5,4},{6,7},{7,6},{8,9},{9,8},{10,11... | collective-permute-start | bytes 1990664 | tf_op jit(solution)/shard_map/ppermute | solution.py:369
  407.2 94.0 %collective-permute-start.24 = (bf16[432,768]{1,0:T(8,128)(2,1)S(1)}, bf16[432,768]{1,0:T(8,128)(2,1)S(1)}, u32[]{:S(2)}, u32[]{:S(2)}) collective-permute-start(bf16[432,768]{1,0:T(8,128)(2,1)S(1)} %copy-done.36), channel_id=1, source_target_pairs={{0,1},{1,0},{2,3},{3,2},{4,5},{5,4},{6,7},{7,6},{8,9},{9,8},{10,11... | collective-permute-start | bytes 1990664 | tf_op jit(solution)/shard_map/ppermute | solution.py:369
  410.7 26.2 %collective-permute-start.40 = (bf16[4,2,2,24,3200]{4,3,0,1,2:T(8,128)(2,1)S(1)}, bf16[4,2,2,24,3200]{4,3,0,1,2:T(8,128)(2,1)S(1)}, u32[]{:S(2)}, u32[]{:S(2)}) collective-permute-start(bf16[4,2,2,24,3200]{4,3,0,1,2:T(8,128)(2,1)S(1)} %bitcast.165), channel_id=1, source_target_pairs={{0,1},{1,0},{2,3},{3,2},{4,5},{5,4},{6,7},{7,6},{8,9},{9,8},{10,11... | collective-permute-start | bytes 7372808 | tf_op jit(solution)/shard_map/ppermute | solution.py:369
  431.3 30.5 %collective-permute-start.49 = (bf16[4,96,1536]{2,1,0:T(8,128)(2,1)S(1)}, bf16[4,96,1536]{2,1,0:T(8,128)(2,1)S(1)}, u32[]{:S(2)}, u32[]{:S(2)}) collective-permute-start(bf16[4,96,1536]{2,1,0:T(8,128)(2,1)S(1)} %copy-done.35), channel_id=1, source_target_pairs={{0,4},{4,0},{8,12},{12,8},{16,20},{20,16},{24,28},{28,24},{1,5},{5... | collective-permute-start | bytes 3538952 | tf_op jit(solution)/shard_map/ppermute | solution.py:479
  443.2 50.7 %collective-permute-start.53 = (bf16[4,2,24,3200]{3,2,0,1:T(8,128)(2,1)S(1)}, bf16[4,2,24,3200]{3,2,0,1:T(8,128)(2,1)S(1)}, u32[]{:S(2)}, u32[]{:S(2)}) collective-permute-start(bf16[4,2,24,3200]{3,2,0,1:T(8,128)(2,1)S(1)} %dynamic-slice_bitcast_fusion), channel_id=1, source_target_pairs={{0,2},{1,3},{2,0},{3,1},{4,6},{5,7},{6,4},{7,5},{8,10},{9,11},{10,... | collective-permute-start | bytes 3686408 | tf_op jit(solution)/shard_map/ppermute | solution.py:369
  453.2 14.9 %collective-permute-start.45 = (bf16[96,1536]{1,0:T(8,128)(2,1)S(1)}, bf16[96,1536]{1,0:T(8,128)(2,1)S(1)}, u32[]{:S(2)}, u32[]{:S(2)}) collective-permute-start(bf16[96,1536]{1,0:T(8,128)(2,1)S(1)} %fusion.15), channel_id=1, source_target_pairs={{0,8},{4,12},{8,16},{12,20},{16,24},{20,28},{24,0},{28,4},{1,9},{5... | collective-permute-start | bytes 884744 | tf_op jit(solution)/shard_map/ppermute | solution.py:483
  461.9 12.6 %collective-permute-start.50 = (bf16[96,1536]{1,0:T(8,128)(2,1)S(1)}, bf16[96,1536]{1,0:T(8,128)(2,1)S(1)}, u32[]{:S(2)}, u32[]{:S(2)}) collective-permute-start(bf16[96,1536]{1,0:T(8,128)(2,1)S(1)} %fusion.36), channel_id=1, source_target_pairs={{0,8},{4,12},{8,16},{12,20},{16,24},{20,28},{24,0},{28,4},{1,9},{5... | collective-permute-start | bytes 884744 | tf_op jit(solution)/shard_map/ppermute | solution.py:483
  462.3 18.5 %collective-permute-start.47 = (bf16[96,1536]{1,0:T(8,128)(2,1)S(1)}, bf16[96,1536]{1,0:T(8,128)(2,1)S(1)}, u32[]{:S(2)}, u32[]{:S(2)}) collective-permute-start(bf16[96,1536]{1,0:T(8,128)(2,1)S(1)} %fusion.13), channel_id=1, source_target_pairs={{0,8},{4,12},{8,16},{12,20},{16,24},{20,28},{24,0},{28,4},{1,9},{5... | collective-permute-start | bytes 884744 | tf_op jit(solution)/shard_map/ppermute | solution.py:483
  469.2 17.9 %collective-permute-start.46 = (bf16[96,1536]{1,0:T(8,128)(2,1)S(1)}, bf16[96,1536]{1,0:T(8,128)(2,1)S(1)}, u32[]{:S(2)}, u32[]{:S(2)}) collective-permute-start(bf16[96,1536]{1,0:T(8,128)(2,1)S(1)} %fusion.14), channel_id=1, source_target_pairs={{0,8},{4,12},{8,16},{12,20},{16,24},{20,28},{24,0},{28,4},{1,9},{5... | collective-permute-start | bytes 884744 | tf_op jit(solution)/shard_map/ppermute | solution.py:483
  474.5 26.2 %collective-permute-start.44 = (bf16[432,768]{1,0:T(8,128)(2,1)S(1)}, bf16[432,768]{1,0:T(8,128)(2,1)S(1)}, u32[]{:S(2)}, u32[]{:S(2)}) collective-permute-start(bf16[432,768]{1,0:T(8,128)(2,1)S(1)} %add_convert_fusion), channel_id=1, source_target_pairs={{0,2},{1,3},{2,0},{3,1},{4,6},{5,7},{6,4},{7,5},{8,10},{9,11},{10,... | collective-permute-start | bytes 1990664 | tf_op jit(solution)/shard_map/ppermute | solution.py:369
  480.8 12.6 %collective-permute-start.51 = (bf16[96,1536]{1,0:T(8,128)(2,1)S(1)}, bf16[96,1536]{1,0:T(8,128)(2,1)S(1)}, u32[]{:S(2)}, u32[]{:S(2)}) collective-permute-start(bf16[96,1536]{1,0:T(8,128)(2,1)S(1)} %fusion.11), channel_id=1, source_target_pairs={{0,8},{4,12},{8,16},{12,20},{16,24},{20,28},{24,0},{28,4},{1,9},{5... | collective-permute-start | bytes 884744 | tf_op jit(solution)/shard_map/ppermute | solution.py:483
  487.1 12.6 %collective-permute-start.48 = (bf16[96,1536]{1,0:T(8,128)(2,1)S(1)}, bf16[96,1536]{1,0:T(8,128)(2,1)S(1)}, u32[]{:S(2)}, u32[]{:S(2)}) collective-permute-start(bf16[96,1536]{1,0:T(8,128)(2,1)S(1)} %fusion.12), channel_id=1, source_target_pairs={{0,8},{4,12},{8,16},{12,20},{16,24},{20,28},{24,0},{28,4},{1,9},{5... | collective-permute-start | bytes 884744 | tf_op jit(solution)/shard_map/ppermute | solution.py:483
  493.5 16.8 %collective-permute-start.52 = (bf16[96,1536]{1,0:T(8,128)(2,1)S(1)}, bf16[96,1536]{1,0:T(8,128)(2,1)S(1)}, u32[]{:S(2)}, u32[]{:S(2)}) collective-permute-start(bf16[96,1536]{1,0:T(8,128)(2,1)S(1)} %fusion.10), channel_id=1, source_target_pairs={{0,8},{4,12},{8,16},{12,20},{16,24},{20,28},{24,0},{28,4},{1,9},{5... | collective-permute-start | bytes 884744 | tf_op jit(solution)/shard_map/ppermute | solution.py:483
  494.2 11.9 %collective-permute-start.54 = (bf16[4,24,3200]{2,1,0:T(8,128)(2,1)S(1)}, bf16[4,24,3200]{2,1,0:T(8,128)(2,1)S(1)}, u32[]{:S(2)}, u32[]{:S(2)}) collective-permute-start(bf16[4,24,3200]{2,1,0:T(8,128)(2,1)S(1)} %dynamic-slice_bitcast_fusion.3), channel_id=1, source_target_pairs={{0,4},{4,0},{8,12},{12,8},{16,20},{20,16},{24,28},{28,24},{1,5},{5... | collective-permute-start | bytes 1843208 | tf_op jit(solution)/shard_map/ppermute | solution.py:509
  (58 other events, 357.7 us)
Sparse Core Ops, SparseCore 0:
  10.9 83.7 all-gather.2
  97.0 114.5 all-gather.4
  240.1 139.7 reduce-scatter.1

commit v4 on v3

--- a/solution.py
+++ b/solution.py
@@ -649,21 +649,20 @@
         sums, (whole,) = expert_part(1, last_grads, False)
         second_experts = offload(whole)
         parts = collect_slots(sums)
+        *parts, final_near, final_far = tie(*parts, final_near, final_far)
         outs = attend_part(1, parts, cotangent)
         held = halve_core(attention_blocks(outs[1]), 3)
         grad_blocks = spread_slots(outs[2])
         *grad_blocks, held = tie(*grad_blocks, held)
         held = halve_line(held, 2)
         sums, pairs = expert_part(0, grad_blocks, True)
-        *sums, held = tie(*sums, held)
+        held = halve_pair(held, 1)
         kepts = list(pairs[::2])
         gots = [swap_pair(sent) for sent in pairs[1::2]]
         parts = collect_slots(sums)
         outs = attend_part(0, parts, outs[0])
-        whole, held, gots[0], gots[1], second_experts = tie(
-            outs[1], held, gots[0], gots[1], second_experts
-        )
-        second_total = reduce_line(halve_pair(held, 1))
+        whole, gots[0], second_experts = tie(outs[1], gots[0], second_experts)
+        second_total = reduce_line(held)
 
         def block(expert, step):
             return add(kepts[expert][step], gots[expert][step]).astype(bf16)

time: 535 us -> 522 us (0.976)
  waiting for transfers between devices: 254 us -> 234 us
    ppermute x31, waiting for transfers between devices: 106 us -> 95.2 us  [swap(): return lax.ppermute(values, 'expert', [(i, i ^ flip) for i in range(count)])]
    ppermute x2, waiting for transfers between devices: 14 us -> 3.35 us  [halve_pair(): lax.ppermute(pick(blocks, 1 - mine, axis), 'dp', pair_perm(lax.axis_size(...]
    ppermute x6, starting transfers between devices: 10.6 us -> 16.3 us  [reduce_line(): lax.ppermute(sent, 'dp', shift_perm(count, step)).astype(f32)]
    unnamed x82 -> x76, local copies, waits for them, and re-layouts: 13.8 us -> 14 us
  transfers between devices with their start and end apart: 65 -> 65, of which waited for: 34 -> 36; matrix products, arithmetic and copies ran while one was open for 8% -> 9% of each run, Pallas kernels for 22% -> 23%
where the time goes in v4:
time: 522 us; the launch traced here: 516 us
  waiting for transfers between devices  234 us (45%)
  Pallas kernels  139 us (27%)
  starting transfers between devices  66.7 us (13%)
  local copies, waits for them, and re-layouts  33.5 us (6%)
  other arithmetic  24.3 us (5%)
  between operations  14.9 us (3%)
    ppermute x31, waiting for transfers between devices, swap(): return lax.ppermute(values, 'expert', [(i, i ^ flip) for i in range(count)])  95.2 us
    pallas_call x2, Pallas kernels, attend_part(): whole_call(partial(attend_backward_body, last), [shape_of(row_count, widt...  47 us
    ppermute x9, waiting for transfers between devices, ring_step(): return lax.ppermute(values, 'dp', ring_perm(lax.axis_size('dp')))  45.3 us
    pallas_call x2, Pallas kernels, expert_backward(): pl.pallas_call(partial(expert_backward_body, split), grid_spec=pltpu.Pref...  36.8 us
    pallas_call x2, Pallas kernels, on_device(): whole_call(partial(attend_forward_body, first), [shape_of(row_count, 3 *...  29.2 us
    ppermute x3, waiting for transfers between devices, gather_rows(): moving = lax.ppermute(moving, 'dp', ring_perm(count))  28.4 us
    pallas_call x2, Pallas kernels, expert_forward(): pl.pallas_call(expert_forward_body, grid=(EXPERTS,), in_specs=[block] * 4...  20.6 us
    ppermute x4, waiting for transfers between devices, gather_rows(): mate = lax.ppermute(mate, 'dp', pair_perm(count))  18.7 us
  transfers between devices with their start and end apart: 65, of which 36 were waited for; matrix products, arithmetic and copies ran while one was open for 9% of the time, Pallas kernels for 23%

profile of v4, /device:TPU:0, one launch (start us, length us, event | category | flops | bytes accessed | tf_op | source)
XLA Modules:
  0.0 516.1 jit_solution(7453334770565169307)
XLA Ops:
  9.2 3.1 collective-permute-start
  12.3 2.6 collective-permute-start.1
  26.8 5.0 collective-permute-start.12
  32.0 9.1 %collective-permute-done.3 = bf16[4,24,3200]{2,1,0:T(8,128)(2,1)S(1)} collective-permute-done((bf16[4,24,3200]{2,1,0:T(8,128)(2,1)S(1)}, bf16[4,24,3200]{2,1,0:T(8,128)(2,1)S(1)}, u32[]{:S(2)}, u32[]{:S(2)}) %collective-permute-start.3) | collective-permute-done | bytes 614432 | tf_op jit(solution)/shard_map/ppermute | solution.py:458
  44.3 2.2 collective-permute-start.11
  47.1 11.9 %collective-permute-done.12 = bf16[96,4608]{1,0:T(8,128)(2,1)S(1)} collective-permute-done((bf16[96,4608]{1,0:T(8,128)(2,1)}, bf16[96,4608]{1,0:T(8,128)(2,1)S(1)}, u32[]{:S(2)}, u32[]{:S(2)}) %collective-permute-start.12) | collective-permute-done | bytes 884768 | tf_op jit(solution)/shard_map/ppermute | solution.py:420
  60.9 20.2 %collective-permute-done.5 = bf16[4,2,24,3200]{3,2,1,0:T(8,128)(2,1)S(1)} collective-permute-done((bf16[4,2,24,3200]{3,2,1,0:T(8,128)(2,1)S(1)}, bf16[4,2,24,3200]{3,2,1,0:T(8,128)(2,1)S(1)}, u32[]{:S(2)}, u32[]{:S(2)}) %collective-permute-start.5) | collective-permute-done | bytes 1228832 | tf_op jit(solution)/shard_map/ppermute | solution.py:369
  81.5 13.0 %collective-permute-done.14 = bf16[96,4608]{1,0:T(8,128)(2,1)} collective-permute-done((bf16[96,4608]{1,0:T(8,128)(2,1)S(1)}, bf16[96,4608]{1,0:T(8,128)(2,1)}, u32[]{:S(2)}, u32[]{:S(2)}) %collective-permute-start.14) | collective-permute-done | bytes 884768 | tf_op jit(solution)/shard_map/ppermute | solution.py:420
  98.0 2.1 copy-done.1
  100.1 14.1 %attend_forward.2 = (bf16[384,2304]{1,0:T(8,128)(2,1)}, f32[384,128]{1,0:T(8,128)}, bf16[384,768]{1,0:T(8,128)(2,1)}, f32[384,768]{1,0:T(8,128)}, bf16[432,768]{1,0:T(8,128)(2,1)}) custom-call(bf16[384,768]{1,0:T(8,128)(2,1)} %refs_4_.3, bf16[384,432]{1,0:T(8,128)(2,1)} %fusion.9.refs_1_.refs_3_.refs_8_, f32[384,384]{1,0:T(8,128)} %fusion.20.refs_2_.refs_4_.refs_9_, ...), custom_call_target="tpu_custom_call" | custom-call | flops 1500000 | bytes 1500 | tf_op jit(solution)/shard_map/attend_forward/pallas_call | solution.py:601
  116.8 7.7 %collective-permute-done.15 = bf16[96,4608]{1,0:T(8,128)(2,1)} collective-permute-done((bf16[96,4608]{1,0:T(8,128)(2,1)}, bf16[96,4608]{1,0:T(8,128)(2,1)}, u32[]{:S(2)}, u32[]{:S(2)}) %collective-permute-start.15) | collective-permute-done | bytes 884768 | tf_op jit(solution)/shard_map/ppermute | solution.py:415
  124.5 3.5 collective-permute-done.16
  131.2 11.0 %collective-permute-done.17 = bf16[96,4608]{1,0:T(8,128)(2,1)S(1)} collective-permute-done((bf16[96,4608]{1,0:T(8,128)(2,1)}, bf16[96,4608]{1,0:T(8,128)(2,1)S(1)}, u32[]{:S(2)}, u32[]{:S(2)}) %collective-permute-start.17) | collective-permute-done | bytes 884768 | tf_op jit(solution)/shard_map/ppermute | solution.py:415
  143.1 2.2 copy-done
  145.3 10.4 %expert_forward.2 = (bf16[432,768]{1,0:T(8,128)(2,1)}, bf16[432,768]{1,0:T(8,128)(2,1)}, bf16[432,768]{1,0:T(8,128)(2,1)}, bf16[432,768]{1,0:T(8,128)(2,1)}, bf1...) custom-call(bf16[432,768]{1,0:T(8,128)(2,1)} %get-tuple-element.96.refs_0_.refs_5_, bf16[432,768]{1,0:T(8,128)(2,1)} %copy-done.10, ...), custom_call_target="tpu_custom_call" | custom-call | flops 1000000 | bytes 1000 | tf_op jit(solution)/shard_map/expert_forward/pallas_call | solution.py:314
  162.1 14.3 %collective-permute-done.20.refs_2_ = bf16[432,768]{1,0:T(8,128)(2,1)S(1)} collective-permute-done((bf16[432,768]{1,0:T(8,128)(2,1)S(1)}, bf16[432,768]{1,0:T(8,128)(2,1)S(1)}, u32[]{:S(2)}, u32[]{:S(2)}) %collective-permute-start.20) | collective-permute-done | bytes 663584 | tf_op jit(solution)/shard_map/ppermute | solution.py:369
  177.3 15.0 %attend_forward.3 = (bf16[384,2304]{1,0:T(8,128)(2,1)}, f32[384,128]{1,0:T(8,128)}, bf16[384,768]{1,0:T(8,128)(2,1)}, f32[384,768]{1,0:T(8,128)}, bf16[432,768]{1,0:T(8,128)(2,1)}, /*index=5*/f32[384,768]{1,0:T(8,128)}) custom-call(f32[384,768]{1,0:T(8,128)} %get-tuple-element.93.refs_0_.refs_3_, bf16[432,768]{1,0:T(8,128)(2,1)} %add_convert_fusion.7.refs_1_, ...), custom_call_target="tpu_custom_call" | custom-call | flops 1500000 | bytes 1500 | tf_op jit(solution)/shard_map/attend_forward/pallas_call | solution.py:601
  194.0 14.8 %collective-permute-done.24.refs_2_.refs_7_ = bf16[432,768]{1,0:T(8,128)(2,1)S(1)} collective-permute-done((bf16[432,768]{1,0:T(8,128)(2,1)}, bf16[432,768]{1,0:T(8,128)(2,1)S(1)}, u32[]{:S(2)}, u32[]{:S(2)}) %collective-permute-start.24) | collective-permute-done | bytes 663584 | tf_op jit(solution)/shard_map/ppermute | solution.py:369
  212.6 10.1 %expert_forward.3 = (bf16[432,768]{1,0:T(8,128)(2,1)}, bf16[432,768]{1,0:T(8,128)(2,1)}, bf16[432,768]{1,0:T(8,128)(2,1)}, bf16[432,768]{1,0:T(8,128)(2,1)}, bf1...) custom-call(bf16[432,768]{1,0:T(8,128)(2,1)} %get-tuple-element.111.refs_0_.refs_5_, bf16[432,768]{1,0:T(8,128)(2,1)} %copy-done.12, ...), custom_call_target="tpu_custom_call" | custom-call | flops 1000000 | bytes 1000 | tf_op jit(solution)/shard_map/expert_forward/pallas_call | solution.py:314
  223.9 16.0 %expert_backward.2 = (bf16[432,768]{1,0:T(8,128)(2,1)}, bf16[432,768]{1,0:T(8,128)(2,1)}, bf16[432,768]{1,0:T(8,128)(2,1)}, bf16[432,768]{1,0:T(8,128)(2,1)}, bf16[768,4608]{1,0:T(8,128)(2,1)}) custom-call(s32[2]{0:T(128)} %pad_add_fusion.refs_0_, bf16[432,768]{1,0:T(8,128)(2,1)} %convolution_convert_fusion.refs_1_, bf16[432,768]{1,0:T(8,128)(2,1)} %copy-done.19, ...), custom_call_target="tpu_custom_call" | custom-call | flops 1600000 | bytes 1600 | tf_op jit(solution)/shard_map/expert_backward/pallas_call | solution.py:344
  247.3 12.2 %collective-permute-done.28.refs_1_ = bf16[432,768]{1,0:T(8,128)(2,1)S(1)} collective-permute-done((bf16[432,768]{1,0:T(8,128)(2,1)S(1)}, bf16[432,768]{1,0:T(8,128)(2,1)S(1)}, u32[]{:S(2)}, u32[]{:S(2)}) %collective-permute-start.28) | collective-permute-done | bytes 663584 | tf_op jit(solution)/shard_map/ppermute | solution.py:369
  260.3 24.3 %attend_backward.2 = (f32[384,768]{1,0:T(8,128)}, bf16[768,3200]{1,0:T(8,128)(2,1)}, bf16[432,768]{1,0:T(8,128)(2,1)}) custom-call(bf16[432,768]{1,0:T(8,128)(2,1)} %add_convert_fusion.5.refs_0_, bf16[432,768]{1,0:T(8,128)(2,1)} %copy-done.22, f32[384,768]{1,0:T(8,128)} %refs_2_.3, f32[384,768]{1,0:T(8,128)} %get-tuple-element.110.refs_3_, ...), custom_call_target="tpu_custom_call" | custom-call | flops 1500000 | bytes 1500 | tf_op jit(solution)/shard_map/attend_backward/pallas_call | solution.py:633
  284.6 3.0 constant_dynamic-slice_fusion.3
  291.1 15.8 %collective-permute-done.32.refs_3_ = bf16[432,768]{1,0:T(8,128)(2,1)} collective-permute-done((bf16[432,768]{1,0:T(8,128)(2,1)}, bf16[432,768]{1,0:T(8,128)(2,1)}, u32[]{:S(2)}, u32[]{:S(2)}) %collective-permute-start.32) | collective-permute-done | bytes 663584 | tf_op jit(solution)/shard_map/ppermute | solution.py:369
  306.9 2.3 fusion.1
  313.6 20.9 %expert_backward.3 = (bf16[432,768]{1,0:T(8,128)(2,1)}, bf16[432,768]{1,0:T(8,128)(2,1)}, bf16[432,768]{1,0:T(8,128)(2,1)}, bf16[432,768]{1,0:T(8,128)(2,1)}, bf...) custom-call(s32[2]{0:T(128)} %pad_add_fusion.refs_0_, ...), custom_call_target="tpu_custom_call" | custom-call | flops 1600000 | bytes 1600 | tf_op jit(solution)/shard_map/expert_backward/pallas_call | solution.py:344
  338.9 3.2 collective-permute-done.57
  346.8 9.2 %collective-permute-done.37.refs_1_ = bf16[432,768]{1,0:T(8,128)(2,1)S(1)} collective-permute-done((bf16[432,768]{1,0:T(8,128)(2,1)S(1)}, bf16[432,768]{1,0:T(8,128)(2,1)S(1)}, u32[]{:S(2)}, u32[]{:S(2)}) %collective-permute-start.37) | collective-permute-done | bytes 663584 | tf_op jit(solution)/shard_map/ppermute | solution.py:369
  356.8 22.8 %attend_backward.3 = (f32[384,768]{1,0:T(8,128)}, bf16[768,3200]{1,0:T(8,128)(2,1)}) custom-call(bf16[432,768]{1,0:T(8,128)(2,1)} %add_convert_fusion.1.refs_0_, bf16[432,768]{1,0:T(8,128)(2,1)} %copy-done.30, f32[384,768]{1,0:T(8,128)} %get-tuple-element.141.refs_2_, f32[384,768]{1,0:T(8,128)} %get-tuple-element.93.refs_0_.refs_3_, ...), custom_call_target="tpu_custom_call" | custom-call | flops 1500000 | bytes 1500 | tf_op jit(solution)/shard_map/attend_backward/pallas_call | solution.py:633
  379.6 2.5 reduce-scatter.2.cloned.1.call-done.refs_4_
  382.1 2.8 constant_dynamic-slice_fusion.1
  386.3 9.7 %collective-permute-start.59 = (bf16[24,3200]{1,0:T(8,128)(2,1)S(1)}, bf16[24,3200]{1,0:T(8,128)(2,1)S(1)}, u32[]{:S(2)}, u32[]{:S(2)}) collective-permute-start(bf16[24,3200]{1,0:T(8,128)(2,1)S(1)} %get-tuple-element.182), channel_id=1, source_target_pairs={{0,8},{4,12},{8,16},{12,20},{16,24},{20,28},{24,0},{28,4},{1,9},{5... | collective-permute-start | bytes 460808 | tf_op jit(solution)/shard_map/ppermute | solution.py:520
  396.1 2.4 collective-permute-start.61
  401.1 4.7 collective-permute-done.60
  409.3 3.6 collective-permute-start.40
  414.1 8.2 %collective-permute-done.40 = bf16[96,1536]{1,0:T(8,128)(2,1)S(1)} collective-permute-done((bf16[96,1536]{1,0:T(8,128)(2,1)S(1)}, bf16[96,1536]{1,0:T(8,128)(2,1)S(1)}, u32[]{:S(2)}, u32[]{:S(2)}) %collective-permute-start.40) | collective-permute-done | bytes 294944 | tf_op jit(solution)/shard_map/ppermute | solution.py:483
  422.4 5.1 collective-permute-done.41
  429.7 8.7 %collective-permute-done.42 = bf16[96,1536]{1,0:T(8,128)(2,1)S(1)} collective-permute-done((bf16[96,1536]{1,0:T(8,128)(2,1)S(1)}, bf16[96,1536]{1,0:T(8,128)(2,1)S(1)}, u32[]{:S(2)}, u32[]{:S(2)}) %collective-permute-start.42) | collective-permute-done | bytes 294944 | tf_op jit(solution)/shard_map/ppermute | solution.py:483
  438.4 12.7 %collective-permute-done.48 = bf16[4,96,1536]{2,1,0:T(8,128)(2,1)S(1)} collective-permute-done((bf16[4,96,1536]{2,1,0:T(8,128)(2,1)S(1)}, bf16[4,96,1536]{2,1,0:T(8,128)(2,1)S(1)}, u32[]{:S(2)}, u32[]{:S(2)}) %collective-permute-start.48) | collective-permute-done | bytes 1179680 | tf_op jit(solution)/shard_map/ppermute | solution.py:479
  456.5 6.5 %collective-permute-done.49 = bf16[96,1536]{1,0:T(8,128)(2,1)S(1)} collective-permute-done((bf16[96,1536]{1,0:T(8,128)(2,1)S(1)}, bf16[96,1536]{1,0:T(8,128)(2,1)S(1)}, u32[]{:S(2)}, u32[]{:S(2)}) %collective-permute-start.49) | collective-permute-done | bytes 294944 | tf_op jit(solution)/shard_map/ppermute | solution.py:483
  463.2 6.1 %collective-permute-done.46 = bf16[96,1536]{1,0:T(8,128)(2,1)S(1)} collective-permute-done((bf16[96,1536]{1,0:T(8,128)(2,1)S(1)}, bf16[96,1536]{1,0:T(8,128)(2,1)S(1)}, u32[]{:S(2)}, u32[]{:S(2)}) %collective-permute-start.46) | collective-permute-done | bytes 294944 | tf_op jit(solution)/shard_map/ppermute | solution.py:483
  469.7 5.9 %collective-permute-done.45 = bf16[96,1536]{1,0:T(8,128)(2,1)S(1)} collective-permute-done((bf16[96,1536]{1,0:T(8,128)(2,1)S(1)}, bf16[96,1536]{1,0:T(8,128)(2,1)S(1)}, u32[]{:S(2)}, u32[]{:S(2)}) %collective-permute-start.45) | collective-permute-done | bytes 294944 | tf_op jit(solution)/shard_map/ppermute | solution.py:483
  477.6 4.4 collective-permute-done.50
  483.0 5.3 %collective-permute-done.47 = bf16[96,1536]{1,0:T(8,128)(2,1)S(1)} collective-permute-done((bf16[96,1536]{1,0:T(8,128)(2,1)S(1)}, bf16[96,1536]{1,0:T(8,128)(2,1)S(1)}, u32[]{:S(2)}, u32[]{:S(2)}) %collective-permute-start.47) | collective-permute-done | bytes 294944 | tf_op jit(solution)/shard_map/ppermute | solution.py:483
  491.1 2.4 collective-permute-done.53
  493.8 4.1 collective-permute-start.55
  500.9 3.3 collective-permute-done.55
  505.5 3.9 finish.1
  (247 shorter events, 96.9 us)
Async XLA Ops:
  7.2 169.3 %all-gather.3.cloned.1.call-start = ((), (), s32[]{:S(2)}) async-start(), calls=%async_computation.1 | async-start | bytes 5068800 | tf_op jit(solution)/shard_map/all_gather | solution.py:570
  9.1 202.7 %all-gather.5.cloned.1.call-start = ((), (), s32[]{:S(2)}) async-start(), calls=%async_computation.2 | async-start | bytes 7962624 | tf_op jit(solution)/shard_map/all_gather | solution.py:574
  9.2 14.5 %collective-permute-start = (bf16[24,3200]{1,0:T(8,128)(2,1)}, bf16[24,3200]{1,0:T(8,128)(2,1)S(1)}, u32[]{:S(2)}, u32[]{:S(2)}) collective-permute-start(bf16[24,3200]{1,0:T(8,128)(2,1)} %get-tuple-element.92), channel_id=1, source_target_pairs={{0,8},{4,12},{8,16},{12,20},{16,24},{20,28},{24,0},{28,4},{1,9},{5... | collective-permute-start | bytes 460808 | tf_op jit(solution)/shard_map/ppermute | solution.py:456
  12.3 12.9 %collective-permute-start.1 = (bf16[24,3200]{1,0:T(8,128)(2,1)}, bf16[24,3200]{1,0:T(8,128)(2,1)S(1)}, u32[]{:S(2)}, u32[]{:S(2)}) collective-permute-start(bf16[24,3200]{1,0:T(8,128)(2,1)} %get-tuple-element.92), channel_id=1, source_target_pairs={{0,16},{4,20},{8,24},{12,28},{16,0},{20,4},{24,8},{28,12},{1,17},{... | collective-permute-start | bytes 460808 | tf_op jit(solution)/shard_map/ppermute | solution.py:456
  18.7 363.4 %reduce-scatter.2.cloned.1.call-start = ((), (), s32[]{:S(2)}) async-start(), calls=%async_computation.3 | async-start | bytes 7962624 | tf_op jit(solution)/shard_map/reduce_scatter | solution.py:645
  25.2 15.8 %collective-permute-start.3 = (bf16[4,24,3200]{2,1,0:T(8,128)(2,1)S(1)}, bf16[4,24,3200]{2,1,0:T(8,128)(2,1)S(1)}, u32[]{:S(2)}, u32[]{:S(2)}) collective-permute-start(bf16[4,24,3200]{2,1,0:T(8,128)(2,1)S(1)} %bitcast_dynamic-update-slice_fusion.6), channel_id=1, source_target_pairs={{0,4},{4,0},{8,12},{12,8},{16,20},{20,16},{24,28},{28,24},{1,5},{5... | collective-permute-start | bytes 1843208 | tf_op jit(solution)/shard_map/ppermute | solution.py:458
  26.8 32.2 %collective-permute-start.12 = (bf16[96,4608]{1,0:T(8,128)(2,1)}, bf16[96,4608]{1,0:T(8,128)(2,1)S(1)}, u32[]{:S(2)}, u32[]{:S(2)}) collective-permute-start(bf16[96,4608]{1,0:T(8,128)(2,1)} %bitcast.84), channel_id=1, source_target_pairs={{0,8},{4,12},{8,16},{12,20},{16,24},{20,28},{24,0},{28,4},{1,9},{5... | collective-permute-start | bytes 2654216 | tf_op jit(solution)/shard_map/ppermute | solution.py:420
  41.1 40.0 %collective-permute-start.5 = (bf16[4,2,24,3200]{3,2,1,0:T(8,128)(2,1)S(1)}, bf16[4,2,24,3200]{3,2,1,0:T(8,128)(2,1)S(1)}, u32[]{:S(2)}, u32[]{:S(2)}) collective-permute-start(bf16[4,2,24,3200]{3,2,1,0:T(8,128)(2,1)S(1)} %bitcast_dynamic-update-slice_fusion.5), channel_id=1, source_target_pairs={{0,2},{1,3},{2,0},{3,1},{4,6},{5,7},{6,4},{7,5},{8,10},{9,11},{10,... | collective-permute-start | bytes 3686408 | tf_op jit(solution)/shard_map/ppermute | solution.py:369
  42.6 38.5 %collective-permute-start.4 = (bf16[4,2,24,3200]{3,2,1,0:T(8,128)(2,1)S(1)}, bf16[4,2,24,3200]{3,2,1,0:T(8,128)(2,1)S(1)}, u32[]{:S(2)}, u32[]{:S(2)}) collective-permute-start(bf16[4,2,24,3200]{3,2,1,0:T(8,128)(2,1)S(1)} %bitcast_dynamic-update-slice_fusion.5), channel_id=1, source_target_pairs={{0,1},{1,0},{2,3},{3,2},{4,5},{5,4},{6,7},{7,6},{8,9},{9,8},{10,11... | collective-permute-start | bytes 3686408 | tf_op jit(solution)/shard_map/ppermute | solution.py:369
  44.3 51.8 %collective-permute-start.11 = (bf16[96,4608]{1,0:T(8,128)(2,1)}, bf16[96,4608]{1,0:T(8,128)(2,1)S(1)}, u32[]{:S(2)}, u32[]{:S(2)}) collective-permute-start(bf16[96,4608]{1,0:T(8,128)(2,1)} %bitcast.84), channel_id=1, source_target_pairs={{0,4},{4,0},{8,12},{12,8},{16,20},{20,16},{24,28},{28,24},{1,5},{5... | collective-permute-start | bytes 2654216 | tf_op jit(solution)/shard_map/ppermute | solution.py:415
  59.0 41.1 %collective-permute-start.13 = (bf16[96,4608]{1,0:T(8,128)(2,1)S(1)}, bf16[96,4608]{1,0:T(8,128)(2,1)S(1)}, u32[]{:S(2)}, u32[]{:S(2)}) collective-permute-start(bf16[96,4608]{1,0:T(8,128)(2,1)S(1)} %collective-permute-done.12), channel_id=1, source_target_pairs={{0,4},{4,0},{8,12},{12,8},{16,20},{20,16},{24,28},{28,24},{1,5},{5... | collective-permute-start | bytes 2654216 | tf_op jit(solution)/shard_map/ppermute | solution.py:415
  59.6 34.8 %collective-permute-start.14 = (bf16[96,4608]{1,0:T(8,128)(2,1)S(1)}, bf16[96,4608]{1,0:T(8,128)(2,1)}, u32[]{:S(2)}, u32[]{:S(2)}) collective-permute-start(bf16[96,4608]{1,0:T(8,128)(2,1)S(1)} %collective-permute-done.12), channel_id=1, source_target_pairs={{0,8},{4,12},{8,16},{12,20},{16,24},{20,28},{24,0},{28,4},{1,9},{5... | collective-permute-start | bytes 2654216 | tf_op jit(solution)/shard_map/ppermute | solution.py:420
  81.1 13.3 %collective-permute-start.6 = (bf16[4,2,24,3200]{3,2,1,0:T(8,128)(2,1)S(1)}, bf16[4,2,24,3200]{3,2,1,0:T(8,128)(2,1)S(1)}, u32[]{:S(2)}, u32[]{:S(2)}) collective-permute-start(bf16[4,2,24,3200]{3,2,1,0:T(8,128)(2,1)S(1)} %collective-permute-done.5), channel_id=1, source_target_pairs={{0,1},{1,0},{2,3},{3,2},{4,5},{5,4},{6,7},{7,6},{8,9},{9,8},{10,11... | collective-permute-start | bytes 3686408 | tf_op jit(solution)/shard_map/ppermute | solution.py:369
  94.5 30.0 %collective-permute-start.15 = (bf16[96,4608]{1,0:T(8,128)(2,1)}, bf16[96,4608]{1,0:T(8,128)(2,1)}, u32[]{:S(2)}, u32[]{:S(2)}) collective-permute-start(bf16[96,4608]{1,0:T(8,128)(2,1)} %collective-permute-done.14), channel_id=1, source_target_pairs={{0,4},{4,0},{8,12},{12,8},{16,20},{20,16},{24,28},{28,24},{1,5},{5... | collective-permute-start | bytes 2654216 | tf_op jit(solution)/shard_map/ppermute | solution.py:415
  96.1 31.9 %collective-permute-start.16 = (bf16[96,4608]{1,0:T(8,128)(2,1)}, bf16[96,4608]{1,0:T(8,128)(2,1)}, u32[]{:S(2)}, u32[]{:S(2)}) collective-permute-start(bf16[96,4608]{1,0:T(8,128)(2,1)} %collective-permute-done.14), channel_id=1, source_target_pairs={{0,8},{4,12},{8,16},{12,20},{16,24},{20,28},{24,0},{28,4},{1,9},{5... | collective-permute-start | bytes 2654216 | tf_op jit(solution)/shard_map/ppermute | solution.py:420
  96.1 18.1 %collective-permute-start.7 = (bf16[432,768]{1,0:T(8,128)(2,1)}, bf16[432,768]{1,0:T(8,128)(2,1)}, u32[]{:S(2)}, u32[]{:S(2)}) collective-permute-start(bf16[432,768]{1,0:T(8,128)(2,1)} %convolution_convert_fusion.refs_1_), channel_id=1, source_target_pairs={{0,2},{1,3},{2,0},{3,1},{4,6},{5,7},{6,4},{7,5},{8,10},{9,11},{10,... | collective-permute-start | bytes 1990664 | tf_op jit(solution)/shard_map/ppermute | solution.py:369
  115.3 14.3 %collective-permute-start.9 = (bf16[432,768]{1,0:T(8,128)(2,1)S(1)}, bf16[432,768]{1,0:T(8,128)(2,1)S(1)}, u32[]{:S(2)}, u32[]{:S(2)}) collective-permute-start(bf16[432,768]{1,0:T(8,128)(2,1)S(1)} %copy-done.8), channel_id=1, source_target_pairs={{0,2},{1,3},{2,0},{3,1},{4,6},{5,7},{6,4},{7,5},{8,10},{9,11},{10,... | collective-permute-start | bytes 1990664 | tf_op jit(solution)/shard_map/ppermute | solution.py:369
  116.7 25.5 %collective-permute-start.8 = (bf16[432,768]{1,0:T(8,128)(2,1)S(1)}, bf16[432,768]{1,0:T(8,128)(2,1)S(1)}, u32[]{:S(2)}, u32[]{:S(2)}) collective-permute-start(bf16[432,768]{1,0:T(8,128)(2,1)S(1)} %copy-done.8), channel_id=1, source_target_pairs={{0,1},{1,0},{2,3},{3,2},{4,5},{5,4},{6,7},{7,6},{8,9},{9,8},{10,11... | collective-permute-start | bytes 1990664 | tf_op jit(solution)/shard_map/ppermute | solution.py:369
  128.0 14.2 %collective-permute-start.17 = (bf16[96,4608]{1,0:T(8,128)(2,1)}, bf16[96,4608]{1,0:T(8,128)(2,1)S(1)}, u32[]{:S(2)}, u32[]{:S(2)}) collective-permute-start(bf16[96,4608]{1,0:T(8,128)(2,1)} %collective-permute-done.16), channel_id=1, source_target_pairs={{0,4},{4,0},{8,12},{12,8},{16,20},{20,16},{24,28},{28,24},{1,5},{5... | collective-permute-start | bytes 2654216 | tf_op jit(solution)/shard_map/ppermute | solution.py:415
  129.7 13.5 %collective-permute-start.10 = (bf16[432,768]{1,0:T(8,128)(2,1)S(1)}, bf16[432,768]{1,0:T(8,128)(2,1)}, u32[]{:S(2)}, u32[]{:S(2)}) collective-permute-start(bf16[432,768]{1,0:T(8,128)(2,1)S(1)} %collective-permute-done.9.refs_2_.refs_7_), channel_id=1, source_target_pairs={{0,1},{1,0},{2,3},{3,2},{4,5},{5,4},{6,7},{7,6},{8,9},{9,8},{10,11... | collective-permute-start | bytes 1990664 | tf_op jit(solution)/shard_map/ppermute | solution.py:369
  159.4 17.0 %collective-permute-start.20 = (bf16[432,768]{1,0:T(8,128)(2,1)S(1)}, bf16[432,768]{1,0:T(8,128)(2,1)S(1)}, u32[]{:S(2)}, u32[]{:S(2)}) collective-permute-start(bf16[432,768]{1,0:T(8,128)(2,1)S(1)} %add_convert_fusion.6), channel_id=1, source_target_pairs={{0,2},{1,3},{2,0},{3,1},{4,6},{5,7},{6,4},{7,5},{8,10},{9,11},{10,... | collective-permute-start | bytes 1990664 | tf_op jit(solution)/shard_map/ppermute | solution.py:369
  192.4 16.4 %collective-permute-start.24 = (bf16[432,768]{1,0:T(8,128)(2,1)}, bf16[432,768]{1,0:T(8,128)(2,1)S(1)}, u32[]{:S(2)}, u32[]{:S(2)}) collective-permute-start(bf16[432,768]{1,0:T(8,128)(2,1)} %get-tuple-element.111.refs_0_.refs_5_), channel_id=1, source_target_pairs={{0,2},{1,3},{2,0},{3,1},{4,6},{5,7},{6,4},{7,5},{8,10},{9,11},{10,... | collective-permute-start | bytes 1990664 | tf_op jit(solution)/shard_map/ppermute | solution.py:369
  194.0 15.9 %collective-permute-start.23 = (bf16[432,768]{1,0:T(8,128)(2,1)}, bf16[432,768]{1,0:T(8,128)(2,1)S(1)}, u32[]{:S(2)}, u32[]{:S(2)}) collective-permute-start(bf16[432,768]{1,0:T(8,128)(2,1)} %get-tuple-element.111.refs_0_.refs_5_), channel_id=1, source_target_pairs={{0,1},{1,0},{2,3},{3,2},{4,5},{5,4},{6,7},{7,6},{8,9},{9,8},{10,11... | collective-permute-start | bytes 1990664 | tf_op jit(solution)/shard_map/ppermute | solution.py:369
  208.8 14.0 %collective-permute-start.21 = (bf16[432,768]{1,0:T(8,128)(2,1)}, bf16[432,768]{1,0:T(8,128)(2,1)S(1)}, u32[]{:S(2)}, u32[]{:S(2)}) collective-permute-start(bf16[432,768]{1,0:T(8,128)(2,1)} %convolution_convert_fusion.refs_1_), channel_id=1, source_target_pairs={{0,1},{1,0},{2,3},{3,2},{4,5},{5,4},{6,7},{7,6},{8,9},{9,8},{10,11... | collective-permute-start | bytes 1990664 | tf_op jit(solution)/shard_map/ppermute | solution.py:369
  209.3 13.5 %collective-permute-start.22 = (bf16[432,768]{1,0:T(8,128)(2,1)}, bf16[432,768]{1,0:T(8,128)(2,1)S(1)}, u32[]{:S(2)}, u32[]{:S(2)}) collective-permute-start(bf16[432,768]{1,0:T(8,128)(2,1)} %collective-permute-done.7.refs_3_), channel_id=1, source_target_pairs={{0,1},{1,0},{2,3},{3,2},{4,5},{5,4},{6,7},{7,6},{8,9},{9,8},{10,11... | collective-permute-start | bytes 1990664 | tf_op jit(solution)/shard_map/ppermute | solution.py:369
  242.5 17.0 %collective-permute-start.28 = (bf16[432,768]{1,0:T(8,128)(2,1)S(1)}, bf16[432,768]{1,0:T(8,128)(2,1)S(1)}, u32[]{:S(2)}, u32[]{:S(2)}) collective-permute-start(bf16[432,768]{1,0:T(8,128)(2,1)S(1)} %add_convert_fusion.4), channel_id=1, source_target_pairs={{0,2},{1,3},{2,0},{3,1},{4,6},{5,7},{6,4},{7,5},{8,10},{9,11},{10,... | collective-permute-start | bytes 1990664 | tf_op jit(solution)/shard_map/ppermute | solution.py:369
  289.3 17.6 %collective-permute-start.34 = (bf16[4,2,2,24,3200]{4,3,0,1,2:T(8,128)(2,1)}, bf16[4,2,2,24,3200]{4,3,0,1,2:T(8,128)(2,1)}, u32[]{:S(2)}, u32[]{:S(2)}) collective-permute-start(bf16[4,2,2,24,3200]{4,3,0,1,2:T(8,128)(2,1)} %bitcast.160), channel_id=1, source_target_pairs={{0,1},{1,0},{2,3},{3,2},{4,5},{5,4},{6,7},{7,6},{8,9},{9,8},{10,11... | collective-permute-start | bytes 7372808 | tf_op jit(solution)/shard_map/ppermute | solution.py:369
  289.3 17.6 %collective-permute-start.32 = (bf16[432,768]{1,0:T(8,128)(2,1)}, bf16[432,768]{1,0:T(8,128)(2,1)}, u32[]{:S(2)}, u32[]{:S(2)}) collective-permute-start(bf16[432,768]{1,0:T(8,128)(2,1)} %get-tuple-element.131.refs_1_), channel_id=1, source_target_pairs={{0,2},{1,3},{2,0},{3,1},{4,6},{5,7},{6,4},{7,5},{8,10},{9,11},{10,... | collective-permute-start | bytes 1990664 | tf_op jit(solution)/shard_map/ppermute | solution.py:369
  290.9 18.3 %collective-permute-start.31 = (bf16[432,768]{1,0:T(8,128)(2,1)}, bf16[432,768]{1,0:T(8,128)(2,1)S(1)}, u32[]{:S(2)}, u32[]{:S(2)}) collective-permute-start(bf16[432,768]{1,0:T(8,128)(2,1)} %get-tuple-element.131.refs_1_), channel_id=1, source_target_pairs={{0,1},{1,0},{2,3},{3,2},{4,5},{5,4},{6,7},{7,6},{8,9},{9,8},{10,11... | collective-permute-start | bytes 1990664 | tf_op jit(solution)/shard_map/ppermute | solution.py:369
  312.0 30.1 %collective-permute-start.57 = (bf16[4,2,24,3200]{3,2,0,1:T(8,128)(2,1)}, bf16[4,2,24,3200]{3,2,0,1:T(8,128)(2,1)}, u32[]{:S(2)}, u32[]{:S(2)}) collective-permute-start(bf16[4,2,24,3200]{3,2,0,1:T(8,128)(2,1)} %dynamic-slice_bitcast_fusion), channel_id=1, source_target_pairs={{0,2},{1,3},{2,0},{3,1},{4,6},{5,7},{6,4},{7,5},{8,10},{9,11},{10,... | collective-permute-start | bytes 3686408 | tf_op jit(solution)/shard_map/ppermute | solution.py:369
  335.0 44.5 %collective-permute-start.38 = (bf16[4,96,1536]{2,1,0:T(8,128)(2,1)}, bf16[4,96,1536]{2,1,0:T(8,128)(2,1)}, u32[]{:S(2)}, u32[]{:S(2)}) collective-permute-start(bf16[4,96,1536]{2,1,0:T(8,128)(2,1)} %get-tuple-element.146), channel_id=1, source_target_pairs={{0,4},{4,0},{8,12},{12,8},{16,20},{20,16},{24,28},{28,24},{1,5},{5... | collective-permute-start | bytes 3538952 | tf_op jit(solution)/shard_map/ppermute | solution.py:479
  338.4 17.5 %collective-permute-start.37 = (bf16[432,768]{1,0:T(8,128)(2,1)S(1)}, bf16[432,768]{1,0:T(8,128)(2,1)S(1)}, u32[]{:S(2)}, u32[]{:S(2)}) collective-permute-start(bf16[432,768]{1,0:T(8,128)(2,1)S(1)} %add_convert_fusion), channel_id=1, source_target_pairs={{0,2},{1,3},{2,0},{3,1},{4,6},{5,7},{6,4},{7,5},{8,10},{9,11},{10,... | collective-permute-start | bytes 1990664 | tf_op jit(solution)/shard_map/ppermute | solution.py:369
  343.8 42.3 %collective-permute-start.58 = (bf16[4,24,3200]{2,1,0:T(8,128)(2,1)S(1)}, bf16[4,24,3200]{2,1,0:T(8,128)(2,1)S(1)}, u32[]{:S(2)}, u32[]{:S(2)}) collective-permute-start(bf16[4,24,3200]{2,1,0:T(8,128)(2,1)S(1)} %dynamic-slice_bitcast_fusion.2), channel_id=1, source_target_pairs={{0,4},{4,0},{8,12},{12,8},{16,20},{20,16},{24,28},{28,24},{1,5},{5... | collective-permute-start | bytes 1843208 | tf_op jit(solution)/shard_map/ppermute | solution.py:509
  385.0 21.9 %collective-permute-start.39 = (bf16[4,2,2,24,3200]{4,3,0,1,2:T(8,128)(2,1)S(1)}, bf16[4,2,2,24,3200]{4,3,0,1,2:T(8,128)(2,1)S(1)}, u32[]{:S(2)}, u32[]{:S(2)}) collective-permute-start(bf16[4,2,2,24,3200]{4,3,0,1,2:T(8,128)(2,1)S(1)} %bitcast.166), channel_id=1, source_target_pairs={{0,1},{1,0},{2,3},{3,2},{4,5},{5,4},{6,7},{7,6},{8,9},{9,8},{10,11... | collective-permute-start | bytes 7372808 | tf_op jit(solution)/shard_map/ppermute | solution.py:369
  386.3 14.1 %collective-permute-start.59 = (bf16[24,3200]{1,0:T(8,128)(2,1)S(1)}, bf16[24,3200]{1,0:T(8,128)(2,1)S(1)}, u32[]{:S(2)}, u32[]{:S(2)}) collective-permute-start(bf16[24,3200]{1,0:T(8,128)(2,1)S(1)} %get-tuple-element.182), channel_id=1, source_target_pairs={{0,8},{4,12},{8,16},{12,20},{16,24},{20,28},{24,0},{28,4},{1,9},{5... | collective-permute-start | bytes 460808 | tf_op jit(solution)/shard_map/ppermute | solution.py:520
  398.5 28.9 %collective-permute-start.41 = (bf16[4,96,1536]{2,1,0:T(8,128)(2,1)S(1)}, bf16[4,96,1536]{2,1,0:T(8,128)(2,1)S(1)}, u32[]{:S(2)}, u32[]{:S(2)}) collective-permute-start(bf16[4,96,1536]{2,1,0:T(8,128)(2,1)S(1)} %copy-done.37), channel_id=1, source_target_pairs={{0,4},{4,0},{8,12},{12,8},{16,20},{20,16},{24,28},{28,24},{1,5},{5... | collective-permute-start | bytes 3538952 | tf_op jit(solution)/shard_map/ppermute | solution.py:479
  400.4 50.7 %collective-permute-start.48 = (bf16[4,96,1536]{2,1,0:T(8,128)(2,1)S(1)}, bf16[4,96,1536]{2,1,0:T(8,128)(2,1)S(1)}, u32[]{:S(2)}, u32[]{:S(2)}) collective-permute-start(bf16[4,96,1536]{2,1,0:T(8,128)(2,1)S(1)} %copy-done.36), channel_id=1, source_target_pairs={{0,4},{4,0},{8,12},{12,8},{16,20},{20,16},{24,28},{28,24},{1,5},{5... | collective-permute-start | bytes 3538952 | tf_op jit(solution)/shard_map/ppermute | solution.py:479
  409.3 13.1 %collective-permute-start.40 = (bf16[96,1536]{1,0:T(8,128)(2,1)S(1)}, bf16[96,1536]{1,0:T(8,128)(2,1)S(1)}, u32[]{:S(2)}, u32[]{:S(2)}) collective-permute-start(bf16[96,1536]{1,0:T(8,128)(2,1)S(1)} %fusion.28), channel_id=1, source_target_pairs={{0,8},{4,12},{8,16},{12,20},{16,24},{20,28},{24,0},{28,4},{1,9},{5... | collective-permute-start | bytes 884744 | tf_op jit(solution)/shard_map/ppermute | solution.py:483
  412.9 69.2 %collective-permute-start.52 = (bf16[4,2,24,3200]{3,2,0,1:T(8,128)(2,1)S(1)}, bf16[4,2,24,3200]{3,2,0,1:T(8,128)(2,1)S(1)}, u32[]{:S(2)}, u32[]{:S(2)}) collective-permute-start(bf16[4,2,24,3200]{3,2,0,1:T(8,128)(2,1)S(1)} %dynamic-slice_bitcast_fusion.1), channel_id=1, source_target_pairs={{0,2},{1,3},{2,0},{3,1},{4,6},{5,7},{6,4},{7,5},{8,10},{9,11},{10,... | collective-permute-start | bytes 3686408 | tf_op jit(solution)/shard_map/ppermute | solution.py:369
  428.6 23.9 %collective-permute-start.44 = (bf16[96,1536]{1,0:T(8,128)(2,1)S(1)}, bf16[96,1536]{1,0:T(8,128)(2,1)S(1)}, u32[]{:S(2)}, u32[]{:S(2)}) collective-permute-start(bf16[96,1536]{1,0:T(8,128)(2,1)S(1)} %fusion.15), channel_id=1, source_target_pairs={{0,8},{4,12},{8,16},{12,20},{16,24},{20,28},{24,0},{28,4},{1,9},{5... | collective-permute-start | bytes 884744 | tf_op jit(solution)/shard_map/ppermute | solution.py:483
  451.2 11.8 %collective-permute-start.49 = (bf16[96,1536]{1,0:T(8,128)(2,1)S(1)}, bf16[96,1536]{1,0:T(8,128)(2,1)S(1)}, u32[]{:S(2)}, u32[]{:S(2)}) collective-permute-start(bf16[96,1536]{1,0:T(8,128)(2,1)S(1)} %fusion.36), channel_id=1, source_target_pairs={{0,8},{4,12},{8,16},{12,20},{16,24},{20,28},{24,0},{28,4},{1,9},{5... | collective-permute-start | bytes 884744 | tf_op jit(solution)/shard_map/ppermute | solution.py:483
  451.4 17.9 %collective-permute-start.46 = (bf16[96,1536]{1,0:T(8,128)(2,1)S(1)}, bf16[96,1536]{1,0:T(8,128)(2,1)S(1)}, u32[]{:S(2)}, u32[]{:S(2)}) collective-permute-start(bf16[96,1536]{1,0:T(8,128)(2,1)S(1)} %fusion.13), channel_id=1, source_target_pairs={{0,8},{4,12},{8,16},{12,20},{16,24},{20,28},{24,0},{28,4},{1,9},{5... | collective-permute-start | bytes 884744 | tf_op jit(solution)/shard_map/ppermute | solution.py:483
  453.6 22.1 %collective-permute-start.45 = (bf16[96,1536]{1,0:T(8,128)(2,1)S(1)}, bf16[96,1536]{1,0:T(8,128)(2,1)S(1)}, u32[]{:S(2)}, u32[]{:S(2)}) collective-permute-start(bf16[96,1536]{1,0:T(8,128)(2,1)S(1)} %fusion.14), channel_id=1, source_target_pairs={{0,8},{4,12},{8,16},{12,20},{16,24},{20,28},{24,0},{28,4},{1,9},{5... | collective-permute-start | bytes 884744 | tf_op jit(solution)/shard_map/ppermute | solution.py:483
  455.4 33.8 %collective-permute-start.43 = (bf16[432,768]{1,0:T(8,128)(2,1)S(1)}, bf16[432,768]{1,0:T(8,128)(2,1)S(1)}, u32[]{:S(2)}, u32[]{:S(2)}) collective-permute-start(bf16[432,768]{1,0:T(8,128)(2,1)S(1)} %copy-done.23), channel_id=1, source_target_pairs={{0,2},{1,3},{2,0},{3,1},{4,6},{5,7},{6,4},{7,5},{8,10},{9,11},{10,... | collective-permute-start | bytes 1990664 | tf_op jit(solution)/shard_map/ppermute | solution.py:369
  463.1 18.8 %collective-permute-start.50 = (bf16[96,1536]{1,0:T(8,128)(2,1)S(1)}, bf16[96,1536]{1,0:T(8,128)(2,1)S(1)}, u32[]{:S(2)}, u32[]{:S(2)}) collective-permute-start(bf16[96,1536]{1,0:T(8,128)(2,1)S(1)} %fusion.11), channel_id=1, source_target_pairs={{0,8},{4,12},{8,16},{12,20},{16,24},{20,28},{24,0},{28,4},{1,9},{5... | collective-permute-start | bytes 884744 | tf_op jit(solution)/shard_map/ppermute | solution.py:483
  469.5 18.8 %collective-permute-start.47 = (bf16[96,1536]{1,0:T(8,128)(2,1)S(1)}, bf16[96,1536]{1,0:T(8,128)(2,1)S(1)}, u32[]{:S(2)}, u32[]{:S(2)}) collective-permute-start(bf16[96,1536]{1,0:T(8,128)(2,1)S(1)} %fusion.12), channel_id=1, source_target_pairs={{0,8},{4,12},{8,16},{12,20},{16,24},{20,28},{24,0},{28,4},{1,9},{5... | collective-permute-start | bytes 884744 | tf_op jit(solution)/shard_map/ppermute | solution.py:483
  482.1 15.8 %collective-permute-start.51 = (bf16[96,1536]{1,0:T(8,128)(2,1)S(1)}, bf16[96,1536]{1,0:T(8,128)(2,1)S(1)}, u32[]{:S(2)}, u32[]{:S(2)}) collective-permute-start(bf16[96,1536]{1,0:T(8,128)(2,1)S(1)} %fusion.10), channel_id=1, source_target_pairs={{0,8},{4,12},{8,16},{12,20},{16,24},{20,28},{24,0},{28,4},{1,9},{5... | collective-permute-start | bytes 884744 | tf_op jit(solution)/shard_map/ppermute | solution.py:483
  482.6 11.0 %collective-permute-start.53 = (bf16[4,24,3200]{2,1,0:T(8,128)(2,1)S(1)}, bf16[4,24,3200]{2,1,0:T(8,128)(2,1)S(1)}, u32[]{:S(2)}, u32[]{:S(2)}) collective-permute-start(bf16[4,24,3200]{2,1,0:T(8,128)(2,1)S(1)} %dynamic-slice_bitcast_fusion.3), channel_id=1, source_target_pairs={{0,4},{4,0},{8,12},{12,8},{16,20},{20,16},{24,28},{28,24},{1,5},{5... | collective-permute-start | bytes 1843208 | tf_op jit(solution)/shard_map/ppermute | solution.py:509
  (55 other events, 313.6 us)
Sparse Core Ops, SparseCore 0:
  10.9 83.8 all-gather.2
  97.0 114.6 all-gather.4
  240.0 141.9 reduce-scatter.1

commit v5 on v4

--- a/solution.py
+++ b/solution.py
@@ -52,7 +52,7 @@
 
 def cost(micros):
     return pl.CostEstimate(
-        flops=micros * 10**5, transcendentals=0, bytes_accessed=micros * 10**2
+        flops=micros * 10**7, transcendentals=0, bytes_accessed=micros * 10**4
     )
 
 

time: 522 us -> 521 us (level)
    unnamed x76 -> x72, local copies, waits for them, and re-layouts: 14 us -> 12.8 us
  transfers between devices with their start and end apart: 65 -> 65, of which waited for: 36 -> 34; matrix products, arithmetic and copies ran while one was open for 9% -> 9% of each run, Pallas kernels for 23% -> 23%
where the time goes in v5:
time: 521 us; the launch traced here: 515 us
  waiting for transfers between devices  231 us (44%)
  Pallas kernels  139 us (27%)
  starting transfers between devices  70.9 us (14%)
  local copies, waits for them, and re-layouts  31.3 us (6%)
  other arithmetic  24.1 us (5%)
  between operations  14.9 us (3%)
    ppermute x31, waiting for transfers between devices, swap(): return lax.ppermute(values, 'expert', [(i, i ^ flip) for i in range(count)])  94.3 us
    pallas_call x2, Pallas kernels, attend_part(): whole_call(partial(attend_backward_body, last), [shape_of(row_count, widt...  47 us
    ppermute x9, waiting for transfers between devices, ring_step(): return lax.ppermute(values, 'dp', ring_perm(lax.axis_size('dp')))  43.3 us
    pallas_call x2, Pallas kernels, expert_backward(): pl.pallas_call(partial(expert_backward_body, split), grid_spec=pltpu.Pref...  36.7 us
    pallas_call x2, Pallas kernels, on_device(): whole_call(partial(attend_forward_body, first), [shape_of(row_count, 3 *...  29.2 us
    ppermute x3, waiting for transfers between devices, gather_rows(): moving = lax.ppermute(moving, 'dp', ring_perm(count))  28.6 us
    pallas_call x2, Pallas kernels, expert_forward(): pl.pallas_call(expert_forward_body, grid=(EXPERTS,), in_specs=[block] * 4...  20.6 us
    ppermute x4, waiting for transfers between devices, gather_rows(): mate = lax.ppermute(mate, 'dp', pair_perm(count))  19.6 us
  transfers between devices with their start and end apart: 65, of which 34 were waited for; matrix products, arithmetic and copies ran while one was open for 9% of the time, Pallas kernels for 23%

profile of v5, /device:TPU:0, one launch (start us, length us, event | category | flops | bytes accessed | tf_op | source)
XLA Modules:
  0.0 514.9 jit_solution(16266222338947588261)
XLA Ops:
  9.2 3.1 collective-permute-start
  12.3 2.6 collective-permute-start.1
  26.8 5.0 collective-permute-start.12
  32.0 9.1 %collective-permute-done.3 = bf16[4,24,3200]{2,1,0:T(8,128)(2,1)S(1)} collective-permute-done((bf16[4,24,3200]{2,1,0:T(8,128)(2,1)S(1)}, bf16[4,24,3200]{2,1,0:T(8,128)(2,1)S(1)}, u32[]{:S(2)}, u32[]{:S(2)}) %collective-permute-start.3) | collective-permute-done | bytes 614432 | tf_op jit(solution)/shard_map/ppermute | solution.py:458
  44.3 2.2 collective-permute-start.11
  47.1 11.9 %collective-permute-done.12 = bf16[96,4608]{1,0:T(8,128)(2,1)S(1)} collective-permute-done((bf16[96,4608]{1,0:T(8,128)(2,1)}, bf16[96,4608]{1,0:T(8,128)(2,1)S(1)}, u32[]{:S(2)}, u32[]{:S(2)}) %collective-permute-start.12) | collective-permute-done | bytes 884768 | tf_op jit(solution)/shard_map/ppermute | solution.py:420
  61.0 20.2 %collective-permute-done.5 = bf16[4,2,24,3200]{3,2,1,0:T(8,128)(2,1)S(1)} collective-permute-done((bf16[4,2,24,3200]{3,2,1,0:T(8,128)(2,1)S(1)}, bf16[4,2,24,3200]{3,2,1,0:T(8,128)(2,1)S(1)}, u32[]{:S(2)}, u32[]{:S(2)}) %collective-permute-start.5) | collective-permute-done | bytes 1228832 | tf_op jit(solution)/shard_map/ppermute | solution.py:369
  81.5 13.0 %collective-permute-done.14 = bf16[96,4608]{1,0:T(8,128)(2,1)} collective-permute-done((bf16[96,4608]{1,0:T(8,128)(2,1)S(1)}, bf16[96,4608]{1,0:T(8,128)(2,1)}, u32[]{:S(2)}, u32[]{:S(2)}) %collective-permute-start.14) | collective-permute-done | bytes 884768 | tf_op jit(solution)/shard_map/ppermute | solution.py:420
  100.1 14.1 %attend_forward.2 = (bf16[384,2304]{1,0:T(8,128)(2,1)}, f32[384,128]{1,0:T(8,128)}, bf16[384,768]{1,0:T(8,128)(2,1)}, f32[384,768]{1,0:T(8,128)}, bf16[432,768]{1,0:T(8,128)(2,1)}) custom-call(bf16[384,768]{1,0:T(8,128)(2,1)} %refs_4_.3, bf16[384,432]{1,0:T(8,128)(2,1)} %fusion.9.refs_1_.refs_3_.refs_8_, f32[384,384]{1,0:T(8,128)} %fusion.20.refs_2_.refs_4_.refs_9_, ...), custom_call_target="tpu_custom_call" | custom-call | flops 150000000 | bytes 150000 | tf_op jit(solution)/shard_map/attend_forward/pallas_call | solution.py:601
  115.8 8.6 %collective-permute-done.15 = bf16[96,4608]{1,0:T(8,128)(2,1)} collective-permute-done((bf16[96,4608]{1,0:T(8,128)(2,1)}, bf16[96,4608]{1,0:T(8,128)(2,1)}, u32[]{:S(2)}, u32[]{:S(2)}) %collective-permute-start.15) | collective-permute-done | bytes 884768 | tf_op jit(solution)/shard_map/ppermute | solution.py:415
  124.5 3.6 collective-permute-done.16
  131.3 10.9 %collective-permute-done.17 = bf16[96,4608]{1,0:T(8,128)(2,1)S(1)} collective-permute-done((bf16[96,4608]{1,0:T(8,128)(2,1)}, bf16[96,4608]{1,0:T(8,128)(2,1)S(1)}, u32[]{:S(2)}, u32[]{:S(2)}) %collective-permute-start.17) | collective-permute-done | bytes 884768 | tf_op jit(solution)/shard_map/ppermute | solution.py:415
  143.2 2.2 copy-done
  145.4 10.4 %expert_forward.2 = (bf16[432,768]{1,0:T(8,128)(2,1)}, bf16[432,768]{1,0:T(8,128)(2,1)}, bf16[432,768]{1,0:T(8,128)(2,1)}, bf16[432,768]{1,0:T(8,128)(2,1)}, bf1...) custom-call(bf16[432,768]{1,0:T(8,128)(2,1)} %get-tuple-element.96.refs_0_.refs_5_, bf16[432,768]{1,0:T(8,128)(2,1)} %copy-done.8, ...), custom_call_target="tpu_custom_call" | custom-call | flops 100000000 | bytes 100000 | tf_op jit(solution)/shard_map/expert_forward/pallas_call | solution.py:314
  162.2 14.3 %collective-permute-done.20.refs_2_ = bf16[432,768]{1,0:T(8,128)(2,1)S(1)} collective-permute-done((bf16[432,768]{1,0:T(8,128)(2,1)S(1)}, bf16[432,768]{1,0:T(8,128)(2,1)S(1)}, u32[]{:S(2)}, u32[]{:S(2)}) %collective-permute-start.20) | collective-permute-done | bytes 663584 | tf_op jit(solution)/shard_map/ppermute | solution.py:369
  177.3 15.0 %attend_forward.3 = (bf16[384,2304]{1,0:T(8,128)(2,1)}, f32[384,128]{1,0:T(8,128)}, bf16[384,768]{1,0:T(8,128)(2,1)}, f32[384,768]{1,0:T(8,128)}, bf16[432,768]{1,0:T(8,128)(2,1)}, /*index=5*/f32[384,768]{1,0:T(8,128)}) custom-call(f32[384,768]{1,0:T(8,128)} %get-tuple-element.93.refs_0_.refs_3_, bf16[432,768]{1,0:T(8,128)(2,1)} %add_convert_fusion.7.refs_1_, ...), custom_call_target="tpu_custom_call" | custom-call | flops 150000000 | bytes 150000 | tf_op jit(solution)/shard_map/attend_forward/pallas_call | solution.py:601
  194.1 14.7 %collective-permute-done.24.refs_2_.refs_7_ = bf16[432,768]{1,0:T(8,128)(2,1)S(1)} collective-permute-done((bf16[432,768]{1,0:T(8,128)(2,1)}, bf16[432,768]{1,0:T(8,128)(2,1)S(1)}, u32[]{:S(2)}, u32[]{:S(2)}) %collective-permute-start.24) | collective-permute-done | bytes 663584 | tf_op jit(solution)/shard_map/ppermute | solution.py:369
  212.7 10.1 %expert_forward.3 = (bf16[432,768]{1,0:T(8,128)(2,1)}, bf16[432,768]{1,0:T(8,128)(2,1)}, bf16[432,768]{1,0:T(8,128)(2,1)}, bf16[432,768]{1,0:T(8,128)(2,1)}, bf1...) custom-call(bf16[432,768]{1,0:T(8,128)(2,1)} %get-tuple-element.111.refs_0_.refs_5_, bf16[432,768]{1,0:T(8,128)(2,1)} %copy-done.10, ...), custom_call_target="tpu_custom_call" | custom-call | flops 100000000 | bytes 100000 | tf_op jit(solution)/shard_map/expert_forward/pallas_call | solution.py:314
  224.0 16.0 %expert_backward.2 = (bf16[432,768]{1,0:T(8,128)(2,1)}, bf16[432,768]{1,0:T(8,128)(2,1)}, bf16[432,768]{1,0:T(8,128)(2,1)}, bf16[432,768]{1,0:T(8,128)(2,1)}, bf16[768,4608]{1,0:T(8,128)(2,1)}) custom-call(s32[2]{0:T(128)} %pad_add_fusion.refs_0_, bf16[432,768]{1,0:T(8,128)(2,1)} %convolution_convert_fusion.refs_1_, bf16[432,768]{1,0:T(8,128)(2,1)} %copy-done.17, ...), custom_call_target="tpu_custom_call" | custom-call | flops 160000000 | bytes 160000 | tf_op jit(solution)/shard_map/expert_backward/pallas_call | solution.py:344
  247.5 12.1 %collective-permute-done.28.refs_1_ = bf16[432,768]{1,0:T(8,128)(2,1)S(1)} collective-permute-done((bf16[432,768]{1,0:T(8,128)(2,1)S(1)}, bf16[432,768]{1,0:T(8,128)(2,1)S(1)}, u32[]{:S(2)}, u32[]{:S(2)}) %collective-permute-start.28) | collective-permute-done | bytes 663584 | tf_op jit(solution)/shard_map/ppermute | solution.py:369
  260.5 24.2 %attend_backward.2 = (f32[384,768]{1,0:T(8,128)}, bf16[768,3200]{1,0:T(8,128)(2,1)}, bf16[432,768]{1,0:T(8,128)(2,1)}) custom-call(bf16[432,768]{1,0:T(8,128)(2,1)} %add_convert_fusion.5.refs_0_, bf16[432,768]{1,0:T(8,128)(2,1)} %copy-done.20, f32[384,768]{1,0:T(8,128)} %refs_2_.3, f32[384,768]{1,0:T(8,128)} %get-tuple-element.110.refs_3_, ...), custom_call_target="tpu_custom_call" | custom-call | flops 150000000 | bytes 150000 | tf_op jit(solution)/shard_map/attend_backward/pallas_call | solution.py:633
  284.7 3.0 constant_dynamic-slice_fusion.3
  291.3 15.7 %collective-permute-done.32.refs_3_ = bf16[432,768]{1,0:T(8,128)(2,1)} collective-permute-done((bf16[432,768]{1,0:T(8,128)(2,1)}, bf16[432,768]{1,0:T(8,128)(2,1)}, u32[]{:S(2)}, u32[]{:S(2)}) %collective-permute-start.32) | collective-permute-done | bytes 663584 | tf_op jit(solution)/shard_map/ppermute | solution.py:369
  307.0 2.3 fusion.1
  312.7 20.7 %expert_backward.3 = (bf16[432,768]{1,0:T(8,128)(2,1)}, bf16[432,768]{1,0:T(8,128)(2,1)}, bf16[432,768]{1,0:T(8,128)(2,1)}, bf16[432,768]{1,0:T(8,128)(2,1)}, bf...) custom-call(s32[2]{0:T(128)} %pad_add_fusion.refs_0_, ...), custom_call_target="tpu_custom_call" | custom-call | flops 160000000 | bytes 160000 | tf_op jit(solution)/shard_map/expert_backward/pallas_call | solution.py:344
  338.6 2.1 add_convert_fusion.1.refs_0_
  341.0 2.1 collective-permute-start.58
  343.1 11.7 %collective-permute-done.37.refs_1_ = bf16[432,768]{1,0:T(8,128)(2,1)S(1)} collective-permute-done((bf16[432,768]{1,0:T(8,128)(2,1)S(1)}, bf16[432,768]{1,0:T(8,128)(2,1)S(1)}, u32[]{:S(2)}, u32[]{:S(2)}) %collective-permute-start.37) | collective-permute-done | bytes 663584 | tf_op jit(solution)/shard_map/ppermute | solution.py:369
  355.6 22.8 %attend_backward.3 = (f32[384,768]{1,0:T(8,128)}, bf16[768,3200]{1,0:T(8,128)(2,1)}) custom-call(bf16[432,768]{1,0:T(8,128)(2,1)} %add_convert_fusion.1.refs_0_, bf16[432,768]{1,0:T(8,128)(2,1)} %copy-done.28, f32[384,768]{1,0:T(8,128)} %get-tuple-element.141.refs_2_, f32[384,768]{1,0:T(8,128)} %get-tuple-element.93.refs_0_.refs_3_, ...), custom_call_target="tpu_custom_call" | custom-call | flops 150000000 | bytes 150000 | tf_op jit(solution)/shard_map/attend_backward/pallas_call | solution.py:633
  378.4 3.6 reduce-scatter.2.cloned.1.call-done.refs_4_
  382.1 2.8 constant_dynamic-slice_fusion.1
  385.4 9.8 %collective-permute-start.59 = (bf16[24,3200]{1,0:T(8,128)(2,1)S(1)}, bf16[24,3200]{1,0:T(8,128)(2,1)S(1)}, u32[]{:S(2)}, u32[]{:S(2)}) collective-permute-start(bf16[24,3200]{1,0:T(8,128)(2,1)S(1)} %get-tuple-element.182), channel_id=1, source_target_pairs={{0,8},{4,12},{8,16},{12,20},{16,24},{20,28},{24,0},{28,4},{1,9},{5... | collective-permute-start | bytes 460808 | tf_op jit(solution)/shard_map/ppermute | solution.py:520
  395.2 2.4 collective-permute-start.61
  401.0 3.7 collective-permute-done.60
  408.2 3.6 collective-permute-start.40
  412.9 8.2 %collective-permute-done.40 = bf16[96,1536]{1,0:T(8,128)(2,1)S(1)} collective-permute-done((bf16[96,1536]{1,0:T(8,128)(2,1)S(1)}, bf16[96,1536]{1,0:T(8,128)(2,1)S(1)}, u32[]{:S(2)}, u32[]{:S(2)}) %collective-permute-start.40) | collective-permute-done | bytes 294944 | tf_op jit(solution)/shard_map/ppermute | solution.py:483
  421.0 5.5 %collective-permute-done.41 = bf16[4,96,1536]{2,1,0:T(8,128)(2,1)S(1)} collective-permute-done((bf16[4,96,1536]{2,1,0:T(8,128)(2,1)S(1)}, bf16[4,96,1536]{2,1,0:T(8,128)(2,1)S(1)}, u32[]{:S(2)}, u32[]{:S(2)}) %collective-permute-start.41) | collective-permute-done | bytes 1179680 | tf_op jit(solution)/shard_map/ppermute | solution.py:479
  428.9 8.3 %collective-permute-done.42 = bf16[96,1536]{1,0:T(8,128)(2,1)S(1)} collective-permute-done((bf16[96,1536]{1,0:T(8,128)(2,1)S(1)}, bf16[96,1536]{1,0:T(8,128)(2,1)S(1)}, u32[]{:S(2)}, u32[]{:S(2)}) %collective-permute-start.42) | collective-permute-done | bytes 294944 | tf_op jit(solution)/shard_map/ppermute | solution.py:483
  437.1 12.9 %collective-permute-done.48 = bf16[4,96,1536]{2,1,0:T(8,128)(2,1)S(1)} collective-permute-done((bf16[4,96,1536]{2,1,0:T(8,128)(2,1)S(1)}, bf16[4,96,1536]{2,1,0:T(8,128)(2,1)S(1)}, u32[]{:S(2)}, u32[]{:S(2)}) %collective-permute-start.48) | collective-permute-done | bytes 1179680 | tf_op jit(solution)/shard_map/ppermute | solution.py:479
  455.5 6.4 %collective-permute-done.49 = bf16[96,1536]{1,0:T(8,128)(2,1)S(1)} collective-permute-done((bf16[96,1536]{1,0:T(8,128)(2,1)S(1)}, bf16[96,1536]{1,0:T(8,128)(2,1)S(1)}, u32[]{:S(2)}, u32[]{:S(2)}) %collective-permute-start.49) | collective-permute-done | bytes 294944 | tf_op jit(solution)/shard_map/ppermute | solution.py:483
  462.1 6.1 %collective-permute-done.46 = bf16[96,1536]{1,0:T(8,128)(2,1)S(1)} collective-permute-done((bf16[96,1536]{1,0:T(8,128)(2,1)S(1)}, bf16[96,1536]{1,0:T(8,128)(2,1)S(1)}, u32[]{:S(2)}, u32[]{:S(2)}) %collective-permute-start.46) | collective-permute-done | bytes 294944 | tf_op jit(solution)/shard_map/ppermute | solution.py:483
  468.7 5.9 %collective-permute-done.45 = bf16[96,1536]{1,0:T(8,128)(2,1)S(1)} collective-permute-done((bf16[96,1536]{1,0:T(8,128)(2,1)S(1)}, bf16[96,1536]{1,0:T(8,128)(2,1)S(1)}, u32[]{:S(2)}, u32[]{:S(2)}) %collective-permute-start.45) | collective-permute-done | bytes 294944 | tf_op jit(solution)/shard_map/ppermute | solution.py:483
  476.5 4.4 collective-permute-done.50
  483.2 4.0 collective-permute-done.47
  490.0 2.4 collective-permute-done.53
  492.7 4.1 collective-permute-start.55
  499.8 3.3 collective-permute-done.55
  504.3 3.9 finish.1
  (243 shorter events, 94.6 us)
Async XLA Ops:
  7.2 169.3 %all-gather.3.cloned.1.call-start = ((), (), s32[]{:S(2)}) async-start(), calls=%async_computation.1 | async-start | bytes 5068800 | tf_op jit(solution)/shard_map/all_gather | solution.py:570
  9.2 202.7 %all-gather.5.cloned.1.call-start = ((), (), s32[]{:S(2)}) async-start(), calls=%async_computation.2 | async-start | bytes 7962624 | tf_op jit(solution)/shard_map/all_gather | solution.py:574
  9.2 14.5 %collective-permute-start = (bf16[24,3200]{1,0:T(8,128)(2,1)}, bf16[24,3200]{1,0:T(8,128)(2,1)S(1)}, u32[]{:S(2)}, u32[]{:S(2)}) collective-permute-start(bf16[24,3200]{1,0:T(8,128)(2,1)} %get-tuple-element.92), channel_id=1, source_target_pairs={{0,8},{4,12},{8,16},{12,20},{16,24},{20,28},{24,0},{28,4},{1,9},{5... | collective-permute-start | bytes 460808 | tf_op jit(solution)/shard_map/ppermute | solution.py:456
  12.3 12.9 %collective-permute-start.1 = (bf16[24,3200]{1,0:T(8,128)(2,1)}, bf16[24,3200]{1,0:T(8,128)(2,1)S(1)}, u32[]{:S(2)}, u32[]{:S(2)}) collective-permute-start(bf16[24,3200]{1,0:T(8,128)(2,1)} %get-tuple-element.92), channel_id=1, source_target_pairs={{0,16},{4,20},{8,24},{12,28},{16,0},{20,4},{24,8},{28,12},{1,17},{... | collective-permute-start | bytes 460808 | tf_op jit(solution)/shard_map/ppermute | solution.py:456
  18.7 363.4 %reduce-scatter.2.cloned.1.call-start = ((), (), s32[]{:S(2)}) async-start(), calls=%async_computation.3 | async-start | bytes 7962624 | tf_op jit(solution)/shard_map/reduce_scatter | solution.py:645
  25.2 15.9 %collective-permute-start.3 = (bf16[4,24,3200]{2,1,0:T(8,128)(2,1)S(1)}, bf16[4,24,3200]{2,1,0:T(8,128)(2,1)S(1)}, u32[]{:S(2)}, u32[]{:S(2)}) collective-permute-start(bf16[4,24,3200]{2,1,0:T(8,128)(2,1)S(1)} %bitcast_dynamic-update-slice_fusion.6), channel_id=1, source_target_pairs={{0,4},{4,0},{8,12},{12,8},{16,20},{20,16},{24,28},{28,24},{1,5},{5... | collective-permute-start | bytes 1843208 | tf_op jit(solution)/shard_map/ppermute | solution.py:458
  26.8 32.2 %collective-permute-start.12 = (bf16[96,4608]{1,0:T(8,128)(2,1)}, bf16[96,4608]{1,0:T(8,128)(2,1)S(1)}, u32[]{:S(2)}, u32[]{:S(2)}) collective-permute-start(bf16[96,4608]{1,0:T(8,128)(2,1)} %bitcast.84), channel_id=1, source_target_pairs={{0,8},{4,12},{8,16},{12,20},{16,24},{20,28},{24,0},{28,4},{1,9},{5... | collective-permute-start | bytes 2654216 | tf_op jit(solution)/shard_map/ppermute | solution.py:420
  41.2 40.0 %collective-permute-start.5 = (bf16[4,2,24,3200]{3,2,1,0:T(8,128)(2,1)S(1)}, bf16[4,2,24,3200]{3,2,1,0:T(8,128)(2,1)S(1)}, u32[]{:S(2)}, u32[]{:S(2)}) collective-permute-start(bf16[4,2,24,3200]{3,2,1,0:T(8,128)(2,1)S(1)} %bitcast_dynamic-update-slice_fusion.5), channel_id=1, source_target_pairs={{0,2},{1,3},{2,0},{3,1},{4,6},{5,7},{6,4},{7,5},{8,10},{9,11},{10,... | collective-permute-start | bytes 3686408 | tf_op jit(solution)/shard_map/ppermute | solution.py:369
  42.6 38.5 %collective-permute-start.4 = (bf16[4,2,24,3200]{3,2,1,0:T(8,128)(2,1)S(1)}, bf16[4,2,24,3200]{3,2,1,0:T(8,128)(2,1)S(1)}, u32[]{:S(2)}, u32[]{:S(2)}) collective-permute-start(bf16[4,2,24,3200]{3,2,1,0:T(8,128)(2,1)S(1)} %bitcast_dynamic-update-slice_fusion.5), channel_id=1, source_target_pairs={{0,1},{1,0},{2,3},{3,2},{4,5},{5,4},{6,7},{7,6},{8,9},{9,8},{10,11... | collective-permute-start | bytes 3686408 | tf_op jit(solution)/shard_map/ppermute | solution.py:369
  44.3 51.8 %collective-permute-start.11 = (bf16[96,4608]{1,0:T(8,128)(2,1)}, bf16[96,4608]{1,0:T(8,128)(2,1)S(1)}, u32[]{:S(2)}, u32[]{:S(2)}) collective-permute-start(bf16[96,4608]{1,0:T(8,128)(2,1)} %bitcast.84), channel_id=1, source_target_pairs={{0,4},{4,0},{8,12},{12,8},{16,20},{20,16},{24,28},{28,24},{1,5},{5... | collective-permute-start | bytes 2654216 | tf_op jit(solution)/shard_map/ppermute | solution.py:415
  59.0 39.0 %collective-permute-start.13 = (bf16[96,4608]{1,0:T(8,128)(2,1)S(1)}, bf16[96,4608]{1,0:T(8,128)(2,1)S(1)}, u32[]{:S(2)}, u32[]{:S(2)}) collective-permute-start(bf16[96,4608]{1,0:T(8,128)(2,1)S(1)} %collective-permute-done.12), channel_id=1, source_target_pairs={{0,4},{4,0},{8,12},{12,8},{16,20},{20,16},{24,28},{28,24},{1,5},{5... | collective-permute-start | bytes 2654216 | tf_op jit(solution)/shard_map/ppermute | solution.py:415
  59.6 34.9 %collective-permute-start.14 = (bf16[96,4608]{1,0:T(8,128)(2,1)S(1)}, bf16[96,4608]{1,0:T(8,128)(2,1)}, u32[]{:S(2)}, u32[]{:S(2)}) collective-permute-start(bf16[96,4608]{1,0:T(8,128)(2,1)S(1)} %collective-permute-done.12), channel_id=1, source_target_pairs={{0,8},{4,12},{8,16},{12,20},{16,24},{20,28},{24,0},{28,4},{1,9},{5... | collective-permute-start | bytes 2654216 | tf_op jit(solution)/shard_map/ppermute | solution.py:420
  81.1 13.4 %collective-permute-start.6 = (bf16[4,2,24,3200]{3,2,1,0:T(8,128)(2,1)S(1)}, bf16[4,2,24,3200]{3,2,1,0:T(8,128)(2,1)S(1)}, u32[]{:S(2)}, u32[]{:S(2)}) collective-permute-start(bf16[4,2,24,3200]{3,2,1,0:T(8,128)(2,1)S(1)} %collective-permute-done.5), channel_id=1, source_target_pairs={{0,1},{1,0},{2,3},{3,2},{4,5},{5,4},{6,7},{7,6},{8,9},{9,8},{10,11... | collective-permute-start | bytes 3686408 | tf_op jit(solution)/shard_map/ppermute | solution.py:369
  94.5 30.0 %collective-permute-start.15 = (bf16[96,4608]{1,0:T(8,128)(2,1)}, bf16[96,4608]{1,0:T(8,128)(2,1)}, u32[]{:S(2)}, u32[]{:S(2)}) collective-permute-start(bf16[96,4608]{1,0:T(8,128)(2,1)} %collective-permute-done.14), channel_id=1, source_target_pairs={{0,4},{4,0},{8,12},{12,8},{16,20},{20,16},{24,28},{28,24},{1,5},{5... | collective-permute-start | bytes 2654216 | tf_op jit(solution)/shard_map/ppermute | solution.py:415
  96.1 32.0 %collective-permute-start.16 = (bf16[96,4608]{1,0:T(8,128)(2,1)}, bf16[96,4608]{1,0:T(8,128)(2,1)}, u32[]{:S(2)}, u32[]{:S(2)}) collective-permute-start(bf16[96,4608]{1,0:T(8,128)(2,1)} %collective-permute-done.14), channel_id=1, source_target_pairs={{0,8},{4,12},{8,16},{12,20},{16,24},{20,28},{24,0},{28,4},{1,9},{5... | collective-permute-start | bytes 2654216 | tf_op jit(solution)/shard_map/ppermute | solution.py:420
  96.2 18.1 %collective-permute-start.7 = (bf16[432,768]{1,0:T(8,128)(2,1)}, bf16[432,768]{1,0:T(8,128)(2,1)}, u32[]{:S(2)}, u32[]{:S(2)}) collective-permute-start(bf16[432,768]{1,0:T(8,128)(2,1)} %convolution_convert_fusion.refs_1_), channel_id=1, source_target_pairs={{0,2},{1,3},{2,0},{3,1},{4,6},{5,7},{6,4},{7,5},{8,10},{9,11},{10,... | collective-permute-start | bytes 1990664 | tf_op jit(solution)/shard_map/ppermute | solution.py:369
  114.2 15.5 %collective-permute-start.9 = (bf16[432,768]{1,0:T(8,128)(2,1)}, bf16[432,768]{1,0:T(8,128)(2,1)S(1)}, u32[]{:S(2)}, u32[]{:S(2)}) collective-permute-start(bf16[432,768]{1,0:T(8,128)(2,1)} %get-tuple-element.96.refs_0_.refs_5_), channel_id=1, source_target_pairs={{0,2},{1,3},{2,0},{3,1},{4,6},{5,7},{6,4},{7,5},{8,10},{9,11},{10,... | collective-permute-start | bytes 1990664 | tf_op jit(solution)/shard_map/ppermute | solution.py:369
  115.7 26.6 %collective-permute-start.8 = (bf16[432,768]{1,0:T(8,128)(2,1)S(1)}, bf16[432,768]{1,0:T(8,128)(2,1)S(1)}, u32[]{:S(2)}, u32[]{:S(2)}) collective-permute-start(bf16[432,768]{1,0:T(8,128)(2,1)S(1)} %copy-done.6), channel_id=1, source_target_pairs={{0,1},{1,0},{2,3},{3,2},{4,5},{5,4},{6,7},{7,6},{8,9},{9,8},{10,11... | collective-permute-start | bytes 1990664 | tf_op jit(solution)/shard_map/ppermute | solution.py:369
  128.1 14.1 %collective-permute-start.17 = (bf16[96,4608]{1,0:T(8,128)(2,1)}, bf16[96,4608]{1,0:T(8,128)(2,1)S(1)}, u32[]{:S(2)}, u32[]{:S(2)}) collective-permute-start(bf16[96,4608]{1,0:T(8,128)(2,1)} %collective-permute-done.16), channel_id=1, source_target_pairs={{0,4},{4,0},{8,12},{12,8},{16,20},{20,16},{24,28},{28,24},{1,5},{5... | collective-permute-start | bytes 2654216 | tf_op jit(solution)/shard_map/ppermute | solution.py:415
  129.8 13.4 %collective-permute-start.10 = (bf16[432,768]{1,0:T(8,128)(2,1)S(1)}, bf16[432,768]{1,0:T(8,128)(2,1)}, u32[]{:S(2)}, u32[]{:S(2)}) collective-permute-start(bf16[432,768]{1,0:T(8,128)(2,1)S(1)} %collective-permute-done.9.refs_2_.refs_7_), channel_id=1, source_target_pairs={{0,1},{1,0},{2,3},{3,2},{4,5},{5,4},{6,7},{7,6},{8,9},{9,8},{10,11... | collective-permute-start | bytes 1990664 | tf_op jit(solution)/shard_map/ppermute | solution.py:369
  159.5 17.0 %collective-permute-start.20 = (bf16[432,768]{1,0:T(8,128)(2,1)S(1)}, bf16[432,768]{1,0:T(8,128)(2,1)S(1)}, u32[]{:S(2)}, u32[]{:S(2)}) collective-permute-start(bf16[432,768]{1,0:T(8,128)(2,1)S(1)} %add_convert_fusion.6), channel_id=1, source_target_pairs={{0,2},{1,3},{2,0},{3,1},{4,6},{5,7},{6,4},{7,5},{8,10},{9,11},{10,... | collective-permute-start | bytes 1990664 | tf_op jit(solution)/shard_map/ppermute | solution.py:369
  192.4 16.4 %collective-permute-start.24 = (bf16[432,768]{1,0:T(8,128)(2,1)}, bf16[432,768]{1,0:T(8,128)(2,1)S(1)}, u32[]{:S(2)}, u32[]{:S(2)}) collective-permute-start(bf16[432,768]{1,0:T(8,128)(2,1)} %get-tuple-element.111.refs_0_.refs_5_), channel_id=1, source_target_pairs={{0,2},{1,3},{2,0},{3,1},{4,6},{5,7},{6,4},{7,5},{8,10},{9,11},{10,... | collective-permute-start | bytes 1990664 | tf_op jit(solution)/shard_map/ppermute | solution.py:369
  194.1 15.8 %collective-permute-start.23 = (bf16[432,768]{1,0:T(8,128)(2,1)}, bf16[432,768]{1,0:T(8,128)(2,1)S(1)}, u32[]{:S(2)}, u32[]{:S(2)}) collective-permute-start(bf16[432,768]{1,0:T(8,128)(2,1)} %get-tuple-element.111.refs_0_.refs_5_), channel_id=1, source_target_pairs={{0,1},{1,0},{2,3},{3,2},{4,5},{5,4},{6,7},{7,6},{8,9},{9,8},{10,11... | collective-permute-start | bytes 1990664 | tf_op jit(solution)/shard_map/ppermute | solution.py:369
  208.8 14.0 %collective-permute-start.21 = (bf16[432,768]{1,0:T(8,128)(2,1)}, bf16[432,768]{1,0:T(8,128)(2,1)S(1)}, u32[]{:S(2)}, u32[]{:S(2)}) collective-permute-start(bf16[432,768]{1,0:T(8,128)(2,1)} %convolution_convert_fusion.refs_1_), channel_id=1, source_target_pairs={{0,1},{1,0},{2,3},{3,2},{4,5},{5,4},{6,7},{7,6},{8,9},{9,8},{10,11... | collective-permute-start | bytes 1990664 | tf_op jit(solution)/shard_map/ppermute | solution.py:369
  209.3 13.5 %collective-permute-start.22 = (bf16[432,768]{1,0:T(8,128)(2,1)}, bf16[432,768]{1,0:T(8,128)(2,1)S(1)}, u32[]{:S(2)}, u32[]{:S(2)}) collective-permute-start(bf16[432,768]{1,0:T(8,128)(2,1)} %collective-permute-done.7.refs_3_), channel_id=1, source_target_pairs={{0,1},{1,0},{2,3},{3,2},{4,5},{5,4},{6,7},{7,6},{8,9},{9,8},{10,11... | collective-permute-start | bytes 1990664 | tf_op jit(solution)/shard_map/ppermute | solution.py:369
  242.6 17.0 %collective-permute-start.28 = (bf16[432,768]{1,0:T(8,128)(2,1)S(1)}, bf16[432,768]{1,0:T(8,128)(2,1)S(1)}, u32[]{:S(2)}, u32[]{:S(2)}) collective-permute-start(bf16[432,768]{1,0:T(8,128)(2,1)S(1)} %add_convert_fusion.4), channel_id=1, source_target_pairs={{0,2},{1,3},{2,0},{3,1},{4,6},{5,7},{6,4},{7,5},{8,10},{9,11},{10,... | collective-permute-start | bytes 1990664 | tf_op jit(solution)/shard_map/ppermute | solution.py:369
  289.4 17.6 %collective-permute-start.34 = (bf16[4,2,2,24,3200]{4,3,0,1,2:T(8,128)(2,1)}, bf16[4,2,2,24,3200]{4,3,0,1,2:T(8,128)(2,1)}, u32[]{:S(2)}, u32[]{:S(2)}) collective-permute-start(bf16[4,2,2,24,3200]{4,3,0,1,2:T(8,128)(2,1)} %bitcast.160), channel_id=1, source_target_pairs={{0,1},{1,0},{2,3},{3,2},{4,5},{5,4},{6,7},{7,6},{8,9},{9,8},{10,11... | collective-permute-start | bytes 7372808 | tf_op jit(solution)/shard_map/ppermute | solution.py:369
  289.4 17.6 %collective-permute-start.32 = (bf16[432,768]{1,0:T(8,128)(2,1)}, bf16[432,768]{1,0:T(8,128)(2,1)}, u32[]{:S(2)}, u32[]{:S(2)}) collective-permute-start(bf16[432,768]{1,0:T(8,128)(2,1)} %get-tuple-element.131.refs_1_), channel_id=1, source_target_pairs={{0,2},{1,3},{2,0},{3,1},{4,6},{5,7},{6,4},{7,5},{8,10},{9,11},{10,... | collective-permute-start | bytes 1990664 | tf_op jit(solution)/shard_map/ppermute | solution.py:369
  291.1 18.3 %collective-permute-start.31 = (bf16[432,768]{1,0:T(8,128)(2,1)}, bf16[432,768]{1,0:T(8,128)(2,1)S(1)}, u32[]{:S(2)}, u32[]{:S(2)}) collective-permute-start(bf16[432,768]{1,0:T(8,128)(2,1)} %get-tuple-element.131.refs_1_), channel_id=1, source_target_pairs={{0,1},{1,0},{2,3},{3,2},{4,5},{5,4},{6,7},{7,6},{8,9},{9,8},{10,11... | collective-permute-start | bytes 1990664 | tf_op jit(solution)/shard_map/ppermute | solution.py:369
  311.0 29.7 %collective-permute-start.57 = (bf16[4,2,24,3200]{3,2,0,1:T(8,128)(2,1)S(1)}, bf16[4,2,24,3200]{3,2,0,1:T(8,128)(2,1)S(1)}, u32[]{:S(2)}, u32[]{:S(2)}) collective-permute-start(bf16[4,2,24,3200]{3,2,0,1:T(8,128)(2,1)S(1)} %dynamic-slice_bitcast_fusion), channel_id=1, source_target_pairs={{0,2},{1,3},{2,0},{3,1},{4,6},{5,7},{6,4},{7,5},{8,10},{9,11},{10,... | collective-permute-start | bytes 3686408 | tf_op jit(solution)/shard_map/ppermute | solution.py:369
  334.0 44.4 %collective-permute-start.38 = (bf16[4,96,1536]{2,1,0:T(8,128)(2,1)}, bf16[4,96,1536]{2,1,0:T(8,128)(2,1)}, u32[]{:S(2)}, u32[]{:S(2)}) collective-permute-start(bf16[4,96,1536]{2,1,0:T(8,128)(2,1)} %get-tuple-element.146), channel_id=1, source_target_pairs={{0,4},{4,0},{8,12},{12,8},{16,20},{20,16},{24,28},{28,24},{1,5},{5... | collective-permute-start | bytes 3538952 | tf_op jit(solution)/shard_map/ppermute | solution.py:479
  337.6 17.2 %collective-permute-start.37 = (bf16[432,768]{1,0:T(8,128)(2,1)S(1)}, bf16[432,768]{1,0:T(8,128)(2,1)S(1)}, u32[]{:S(2)}, u32[]{:S(2)}) collective-permute-start(bf16[432,768]{1,0:T(8,128)(2,1)S(1)} %add_convert_fusion), channel_id=1, source_target_pairs={{0,2},{1,3},{2,0},{3,1},{4,6},{5,7},{6,4},{7,5},{8,10},{9,11},{10,... | collective-permute-start | bytes 1990664 | tf_op jit(solution)/shard_map/ppermute | solution.py:369
  341.0 44.1 %collective-permute-start.58 = (bf16[4,24,3200]{2,1,0:T(8,128)(2,1)S(1)}, bf16[4,24,3200]{2,1,0:T(8,128)(2,1)S(1)}, u32[]{:S(2)}, u32[]{:S(2)}) collective-permute-start(bf16[4,24,3200]{2,1,0:T(8,128)(2,1)S(1)} %dynamic-slice_bitcast_fusion.2), channel_id=1, source_target_pairs={{0,4},{4,0},{8,12},{12,8},{16,20},{20,16},{24,28},{28,24},{1,5},{5... | collective-permute-start | bytes 1843208 | tf_op jit(solution)/shard_map/ppermute | solution.py:509
  385.1 20.8 %collective-permute-start.39 = (bf16[4,2,2,24,3200]{4,3,0,1,2:T(8,128)(2,1)S(1)}, bf16[4,2,2,24,3200]{4,3,0,1,2:T(8,128)(2,1)S(1)}, u32[]{:S(2)}, u32[]{:S(2)}) collective-permute-start(bf16[4,2,2,24,3200]{4,3,0,1,2:T(8,128)(2,1)S(1)} %bitcast.166), channel_id=1, source_target_pairs={{0,1},{1,0},{2,3},{3,2},{4,5},{5,4},{6,7},{7,6},{8,9},{9,8},{10,11... | collective-permute-start | bytes 7372808 | tf_op jit(solution)/shard_map/ppermute | solution.py:369
  385.4 14.2 %collective-permute-start.59 = (bf16[24,3200]{1,0:T(8,128)(2,1)S(1)}, bf16[24,3200]{1,0:T(8,128)(2,1)S(1)}, u32[]{:S(2)}, u32[]{:S(2)}) collective-permute-start(bf16[24,3200]{1,0:T(8,128)(2,1)S(1)} %get-tuple-element.182), channel_id=1, source_target_pairs={{0,8},{4,12},{8,16},{12,20},{16,24},{20,28},{24,0},{28,4},{1,9},{5... | collective-permute-start | bytes 460808 | tf_op jit(solution)/shard_map/ppermute | solution.py:520
  397.6 28.9 %collective-permute-start.41 = (bf16[4,96,1536]{2,1,0:T(8,128)(2,1)S(1)}, bf16[4,96,1536]{2,1,0:T(8,128)(2,1)S(1)}, u32[]{:S(2)}, u32[]{:S(2)}) collective-permute-start(bf16[4,96,1536]{2,1,0:T(8,128)(2,1)S(1)} %copy-done.35), channel_id=1, source_target_pairs={{0,4},{4,0},{8,12},{12,8},{16,20},{20,16},{24,28},{28,24},{1,5},{5... | collective-permute-start | bytes 3538952 | tf_op jit(solution)/shard_map/ppermute | solution.py:479
  399.6 50.5 %collective-permute-start.48 = (bf16[4,96,1536]{2,1,0:T(8,128)(2,1)S(1)}, bf16[4,96,1536]{2,1,0:T(8,128)(2,1)S(1)}, u32[]{:S(2)}, u32[]{:S(2)}) collective-permute-start(bf16[4,96,1536]{2,1,0:T(8,128)(2,1)S(1)} %copy-done.34), channel_id=1, source_target_pairs={{0,4},{4,0},{8,12},{12,8},{16,20},{20,16},{24,28},{28,24},{1,5},{5... | collective-permute-start | bytes 3538952 | tf_op jit(solution)/shard_map/ppermute | solution.py:479
  408.2 12.9 %collective-permute-start.40 = (bf16[96,1536]{1,0:T(8,128)(2,1)S(1)}, bf16[96,1536]{1,0:T(8,128)(2,1)S(1)}, u32[]{:S(2)}, u32[]{:S(2)}) collective-permute-start(bf16[96,1536]{1,0:T(8,128)(2,1)S(1)} %fusion.28), channel_id=1, source_target_pairs={{0,8},{4,12},{8,16},{12,20},{16,24},{20,28},{24,0},{28,4},{1,9},{5... | collective-permute-start | bytes 884744 | tf_op jit(solution)/shard_map/ppermute | solution.py:483
  411.9 69.2 %collective-permute-start.52 = (bf16[4,2,24,3200]{3,2,0,1:T(8,128)(2,1)S(1)}, bf16[4,2,24,3200]{3,2,0,1:T(8,128)(2,1)S(1)}, u32[]{:S(2)}, u32[]{:S(2)}) collective-permute-start(bf16[4,2,24,3200]{3,2,0,1:T(8,128)(2,1)S(1)} %dynamic-slice_bitcast_fusion.1), channel_id=1, source_target_pairs={{0,2},{1,3},{2,0},{3,1},{4,6},{5,7},{6,4},{7,5},{8,10},{9,11},{10,... | collective-permute-start | bytes 3686408 | tf_op jit(solution)/shard_map/ppermute | solution.py:369
  427.8 23.7 %collective-permute-start.44 = (bf16[96,1536]{1,0:T(8,128)(2,1)S(1)}, bf16[96,1536]{1,0:T(8,128)(2,1)S(1)}, u32[]{:S(2)}, u32[]{:S(2)}) collective-permute-start(bf16[96,1536]{1,0:T(8,128)(2,1)S(1)} %fusion.15), channel_id=1, source_target_pairs={{0,8},{4,12},{8,16},{12,20},{16,24},{20,28},{24,0},{28,4},{1,9},{5... | collective-permute-start | bytes 884744 | tf_op jit(solution)/shard_map/ppermute | solution.py:483
  450.1 11.8 %collective-permute-start.49 = (bf16[96,1536]{1,0:T(8,128)(2,1)S(1)}, bf16[96,1536]{1,0:T(8,128)(2,1)S(1)}, u32[]{:S(2)}, u32[]{:S(2)}) collective-permute-start(bf16[96,1536]{1,0:T(8,128)(2,1)S(1)} %fusion.36), channel_id=1, source_target_pairs={{0,8},{4,12},{8,16},{12,20},{16,24},{20,28},{24,0},{28,4},{1,9},{5... | collective-permute-start | bytes 884744 | tf_op jit(solution)/shard_map/ppermute | solution.py:483
  450.3 17.9 %collective-permute-start.46 = (bf16[96,1536]{1,0:T(8,128)(2,1)S(1)}, bf16[96,1536]{1,0:T(8,128)(2,1)S(1)}, u32[]{:S(2)}, u32[]{:S(2)}) collective-permute-start(bf16[96,1536]{1,0:T(8,128)(2,1)S(1)} %fusion.13), channel_id=1, source_target_pairs={{0,8},{4,12},{8,16},{12,20},{16,24},{20,28},{24,0},{28,4},{1,9},{5... | collective-permute-start | bytes 884744 | tf_op jit(solution)/shard_map/ppermute | solution.py:483
  452.5 22.1 %collective-permute-start.45 = (bf16[96,1536]{1,0:T(8,128)(2,1)S(1)}, bf16[96,1536]{1,0:T(8,128)(2,1)S(1)}, u32[]{:S(2)}, u32[]{:S(2)}) collective-permute-start(bf16[96,1536]{1,0:T(8,128)(2,1)S(1)} %fusion.14), channel_id=1, source_target_pairs={{0,8},{4,12},{8,16},{12,20},{16,24},{20,28},{24,0},{28,4},{1,9},{5... | collective-permute-start | bytes 884744 | tf_op jit(solution)/shard_map/ppermute | solution.py:483
  454.3 33.8 %collective-permute-start.43 = (bf16[432,768]{1,0:T(8,128)(2,1)S(1)}, bf16[432,768]{1,0:T(8,128)(2,1)S(1)}, u32[]{:S(2)}, u32[]{:S(2)}) collective-permute-start(bf16[432,768]{1,0:T(8,128)(2,1)S(1)} %copy-done.21), channel_id=1, source_target_pairs={{0,2},{1,3},{2,0},{3,1},{4,6},{5,7},{6,4},{7,5},{8,10},{9,11},{10,... | collective-permute-start | bytes 1990664 | tf_op jit(solution)/shard_map/ppermute | solution.py:369
  462.1 18.8 %collective-permute-start.50 = (bf16[96,1536]{1,0:T(8,128)(2,1)S(1)}, bf16[96,1536]{1,0:T(8,128)(2,1)S(1)}, u32[]{:S(2)}, u32[]{:S(2)}) collective-permute-start(bf16[96,1536]{1,0:T(8,128)(2,1)S(1)} %fusion.11), channel_id=1, source_target_pairs={{0,8},{4,12},{8,16},{12,20},{16,24},{20,28},{24,0},{28,4},{1,9},{5... | collective-permute-start | bytes 884744 | tf_op jit(solution)/shard_map/ppermute | solution.py:483
  468.4 18.8 %collective-permute-start.47 = (bf16[96,1536]{1,0:T(8,128)(2,1)S(1)}, bf16[96,1536]{1,0:T(8,128)(2,1)S(1)}, u32[]{:S(2)}, u32[]{:S(2)}) collective-permute-start(bf16[96,1536]{1,0:T(8,128)(2,1)S(1)} %fusion.12), channel_id=1, source_target_pairs={{0,8},{4,12},{8,16},{12,20},{16,24},{20,28},{24,0},{28,4},{1,9},{5... | collective-permute-start | bytes 884744 | tf_op jit(solution)/shard_map/ppermute | solution.py:483
  481.0 15.8 %collective-permute-start.51 = (bf16[96,1536]{1,0:T(8,128)(2,1)S(1)}, bf16[96,1536]{1,0:T(8,128)(2,1)S(1)}, u32[]{:S(2)}, u32[]{:S(2)}) collective-permute-start(bf16[96,1536]{1,0:T(8,128)(2,1)S(1)} %fusion.10), channel_id=1, source_target_pairs={{0,8},{4,12},{8,16},{12,20},{16,24},{20,28},{24,0},{28,4},{1,9},{5... | collective-permute-start | bytes 884744 | tf_op jit(solution)/shard_map/ppermute | solution.py:483
  481.5 10.9 %collective-permute-start.53 = (bf16[4,24,3200]{2,1,0:T(8,128)(2,1)S(1)}, bf16[4,24,3200]{2,1,0:T(8,128)(2,1)S(1)}, u32[]{:S(2)}, u32[]{:S(2)}) collective-permute-start(bf16[4,24,3200]{2,1,0:T(8,128)(2,1)S(1)} %dynamic-slice_bitcast_fusion.3), channel_id=1, source_target_pairs={{0,4},{4,0},{8,12},{12,8},{16,20},{20,16},{24,28},{28,24},{1,5},{5... | collective-permute-start | bytes 1843208 | tf_op jit(solution)/shard_map/ppermute | solution.py:509
  (53 other events, 278.3 us)
Sparse Core Ops, SparseCore 0:
  10.9 83.8 all-gather.2
  97.0 114.7 all-gather.4
  240.1 141.8 reduce-scatter.1
